TPU v7x, 32 devices: a whole 2x2x4 slice. The times are simulated.
32 devices in a mesh: gx: 8 (over y, x, core), gy: 4 (over z).
Axes of the slice: x: 2, y: 2, z: 4, core: 2. Of those that a mesh axis runs over, the one named last changes fastest.
Arguments:
- flow_state: float32 [5, 64, 4096], P(None, 'gx', 'gy'), as said below
- x_codes: int32 [2, 128], P(None, 'gy'), may hold values from 0 to 1
- y_codes: int32 [2, 64], P(None, 'gx'), may hold values from 0 to 1
Outputs:
- increment: float32 [5, 64, 4096], P(None, 'gx', 'gy')
Inputs may be any that keep to these rules, and one draw needn't show every extreme that they name: `flow_state`: density lies in [0.75, 1.33], each velocity in [-0.5, 0.5], pressure in [0.6, 1.4]. `x_codes`: 0: the increment beyond the face is zero; 1: it equals that of the boundary cell. `y_codes`: 0: the increment beyond the face is zero; 1: it equals that of the boundary cell.
All inputs are finite; a program needn't handle non-finite values.
Results may differ from a plain program's by a relative error of at most 0.0003.
Values sent between devices are 32-bit elements; how exact they have to be, the bound alone decides.
No kernel may reach another device: no remote copies, remote signals or barrier semaphores. Data moves between devices by JAX's collectives and lax.ppermute only.
A program may use at most 64 MiB of HBM per device.

v0:
```python
import jax
import jax.numpy as jnp
from jax import lax
from jax.sharding import PartitionSpec as P

NZ = 32


GAMMA = 1.4
SIGMA = 0.5
DIFFUSE = 400.0


def padded_2(block, sides, width):
    for axis, dim in sides:
        count = lax.axis_size(axis)
        forward = [(i, i + 1) for i in range(count - 1)]
        backward = [(target, source) for source, target in forward]
        low = lax.ppermute(
            lax.slice_in_dim(block, block.shape[dim] - width, None, axis=dim), axis, forward
        )
        high = lax.ppermute(lax.slice_in_dim(block, 0, width, axis=dim), axis, backward)
        block = jnp.concatenate([low, block, high], axis=dim)
    return block


def primitives(conserved):
    density = conserved[0]
    vel_u = conserved[1] / density
    vel_v = conserved[2] / density
    vel_w = conserved[3] / density
    kinetic = 0.5 * (vel_u * vel_u + vel_v * vel_v + vel_w * vel_w)
    pressure = (GAMMA - 1.0) * (conserved[4] - density * kinetic)
    sound_speed = jnp.sqrt(GAMMA * pressure / density)
    return (density, vel_u, vel_v, vel_w, pressure, sound_speed)


def explicit_terms(padded):
    primitive = primitives(padded)
    density, vel_u, vel_v, vel_w, pressure, sound_speed = primitive
    enthalpy = padded[4] + pressure
    flux_x = jnp.stack(
        [
            padded[1],
            padded[1] * vel_u + pressure,
            padded[2] * vel_u,
            padded[3] * vel_u,
            vel_u * enthalpy,
        ]
    )
    flux_y = jnp.stack(
        [
            padded[2],
            padded[1] * vel_v,
            padded[2] * vel_v + pressure,
            padded[3] * vel_v,
            vel_v * enthalpy,
        ]
    )
    interior = padded[:, 1:-1, 1:-1]
    inner_speed = vel_w[1:-1, 1:-1]
    inner_pressure = pressure[1:-1, 1:-1]
    flux_z = jnp.stack(
        [
            interior[3],
            interior[1] * inner_speed,
            interior[2] * inner_speed,
            interior[3] * inner_speed + inner_pressure,
            inner_speed * (interior[4] + inner_pressure),
        ]
    )
    change = (
        flux_x[:, 2:, 1:-1]
        - flux_x[:, :-2, 1:-1]
        + (flux_y[:, 1:-1, 2:] - flux_y[:, 1:-1, :-2])
        + (jnp.roll(flux_z, -1, axis=3) - jnp.roll(flux_z, 1, axis=3))
    )
    smooth = (
        padded[:, 2:, 1:-1]
        + padded[:, :-2, 1:-1]
        + padded[:, 1:-1, 2:]
        + padded[:, 1:-1, :-2]
        - 4.0 * interior
    )
    residual = -0.5 * SIGMA * change + DIFFUSE * smooth
    return (residual, primitive)


def primitive_change(residual, primitive):
    density, vel_u, vel_v, vel_w, pressure, sound_speed = primitive
    change_u = (residual[1] - vel_u * residual[0]) / density
    change_v = (residual[2] - vel_v * residual[0]) / density
    change_w = (residual[3] - vel_w * residual[0]) / density
    kinetic = 0.5 * (vel_u * vel_u + vel_v * vel_v + vel_w * vel_w)
    change_pressure = (GAMMA - 1.0) * (
        residual[4]
        - vel_u * residual[1]
        - vel_v * residual[2]
        - vel_w * residual[3]
        + kinetic * residual[0]
    )
    return (residual[0], change_u, change_v, change_w, change_pressure)


def to_characteristic(changes, primitive, normal_index):
    impedance = primitive[0] * primitive[5]
    normal_change = changes[normal_index]
    if normal_index == 1:
        tangent_one, tangent_two = (changes[2], changes[3])
    else:
        tangent_one, tangent_two = (changes[1], changes[3])
    pressure_change = changes[4]
    squared = primitive[5] * primitive[5]
    return jnp.stack(
        [
            pressure_change - impedance * normal_change,
            squared * changes[0] - pressure_change,
            tangent_one,
            tangent_two,
            pressure_change + impedance * normal_change,
        ]
    )


def from_characteristic(waves, primitive, normal_index):
    impedance = primitive[0] * primitive[5]
    squared = primitive[5] * primitive[5]
    pressure_change = 0.5 * (waves[0] + waves[4])
    normal_change = (waves[4] - waves[0]) / (2.0 * impedance)
    density_change = (waves[1] + pressure_change) / squared
    if normal_index == 1:
        return (density_change, normal_change, waves[2], waves[3], pressure_change)
    return (density_change, waves[2], normal_change, waves[3], pressure_change)


def to_conserved(changes, primitive):
    density, vel_u, vel_v, vel_w, pressure, sound_speed = primitive
    kinetic = 0.5 * (vel_u * vel_u + vel_v * vel_v + vel_w * vel_w)
    energy_change = (
        kinetic * changes[0]
        + density * (vel_u * changes[1] + vel_v * changes[2] + vel_w * changes[3])
        + changes[4] / (GAMMA - 1.0)
    )
    return jnp.stack(
        [
            changes[0],
            vel_u * changes[0] + density * changes[1],
            vel_v * changes[0] + density * changes[2],
            vel_w * changes[0] + density * changes[3],
            energy_change,
        ]
    )


def eigenvalues(primitive, normal_index):
    normal_speed = primitive[normal_index]
    sound_speed = primitive[5]
    return jnp.stack(
        [
            normal_speed - sound_speed,
            normal_speed,
            normal_speed,
            normal_speed,
            normal_speed + sound_speed,
        ]
    )


def coefficients(speeds, face_codes, at_start, at_end):
    lower_band = -0.5 * SIGMA * speeds[:, :-2] - DIFFUSE
    upper_band = 0.5 * SIGMA * speeds[:, 2:] - DIFFUSE
    main_band = jnp.full(lower_band.shape, 1.0 + 2.0 * DIFFUSE, jnp.float32)
    first_neumann = jnp.logical_and(at_start, face_codes[0] == 1)
    last_neumann = jnp.logical_and(at_end, face_codes[1] == 1)
    main_band = main_band.at[:, 0].add(jnp.where(first_neumann, lower_band[:, 0], 0.0))
    main_band = main_band.at[:, -1].add(jnp.where(last_neumann, upper_band[:, -1], 0.0))
    lower_band = lower_band.at[:, 0].set(jnp.where(at_start, 0.0, lower_band[:, 0]))
    upper_band = upper_band.at[:, -1].set(jnp.where(at_end, 0.0, upper_band[:, -1]))
    return (lower_band, main_band, upper_band)


def thomas_rows(lower_band, main_band, upper_band, right_side):
    nothing = jnp.zeros_like(right_side[0])

    def forward_step(carry, row_set):
        prev_upper, prev_value = carry
        lower_row, main_row, upper_row, right_row = row_set
        pivot_value = main_row - lower_row * prev_upper
        next_upper = upper_row / pivot_value
        next_value = (right_row - lower_row * prev_value) / pivot_value
        return ((next_upper, next_value), (next_upper, next_value))

    final_carry, (uppers, values) = lax.scan(
        forward_step, (nothing, nothing), (lower_band, main_band, upper_band, right_side)
    )

    def backward_step(later_value, row_set):
        upper_row, value_row = row_set
        current = value_row - upper_row * later_value
        return (current, current)

    last_carry, result = lax.scan(backward_step, nothing, (uppers, values), reverse=True)
    return result


def reduce_segment(lower_band, main_band, upper_band, right_side):
    cells = lower_band.shape[1]
    nothing = jnp.zeros_like(right_side[:, 0])
    carry_upper = nothing
    carry_values = (nothing, nothing, nothing)
    uppers = []
    values = []
    for cell_at in range(1, cells - 1):
        lower_here = lower_band[:, cell_at] if cell_at > 1 else nothing
        upper_here = upper_band[:, cell_at] if cell_at < cells - 2 else nothing
        source_left = -lower_band[:, 1] if cell_at == 1 else nothing
        source_right = -upper_band[:, cells - 2] if cell_at == cells - 2 else nothing
        pivot_value = main_band[:, cell_at] - lower_here * carry_upper
        carry_upper = upper_here / pivot_value
        sources = (right_side[:, cell_at], source_left, source_right)
        carry_values = tuple(
            (
                (source - lower_here * previous) / pivot_value
                for source, previous in zip(sources, carry_values)
            )
        )
        uppers.append(carry_upper)
        values.append(carry_values)
    later_values = (nothing, nothing, nothing)
    solutions = []
    for back_at in range(len(values) - 1, -1, -1):
        later_values = tuple(
            (
                forward_value - uppers[back_at] * later_value
                for forward_value, later_value in zip(values[back_at], later_values)
            )
        )
        solutions.append(later_values)
    solutions = solutions[::-1]
    first_u, first_p, first_q = solutions[0]
    last_u, last_p, last_q = solutions[-1]
    row_first = (
        lower_band[:, 0],
        main_band[:, 0] + upper_band[:, 0] * first_p,
        upper_band[:, 0] * first_q,
        right_side[:, 0] - upper_band[:, 0] * first_u,
    )
    row_last = (
        lower_band[:, -1] * last_p,
        main_band[:, -1] + lower_band[:, -1] * last_q,
        upper_band[:, -1],
        right_side[:, -1] - lower_band[:, -1] * last_u,
    )
    return ((row_first, row_last), solutions)


def assemble(first_value, last_value, solutions):
    columns = (
        [first_value]
        + [
            piece_u + piece_p * first_value + piece_q * last_value
            for piece_u, piece_p, piece_q in solutions
        ]
        + [last_value]
    )
    return jnp.stack(columns, axis=1)


def gathered_join(reduced_rows, direction):
    row_first, row_last = reduced_rows
    stacked = jnp.stack(list(row_first) + list(row_last))[None]
    if direction == "x":
        everything = lax.all_gather(stacked, "gx", axis=0, tiled=True)
        own_index = lax.axis_index("gx")
    else:
        everything = lax.all_gather(stacked, "gy", axis=0, tiled=True)
        own_index = lax.axis_index("gy")
    segment_count = everything.shape[0]
    flat_rows = everything.reshape((segment_count * 2, 4) + everything.shape[2:])
    solved = thomas_rows(flat_rows[:, 0], flat_rows[:, 1], flat_rows[:, 2], flat_rows[:, 3])
    first_value = lax.dynamic_index_in_dim(solved, 2 * own_index, 0, keepdims=False)
    last_value = lax.dynamic_index_in_dim(solved, 2 * own_index + 1, 0, keepdims=False)
    return (first_value, last_value)


def solve_lines(band_set, right_side, direction):
    lower_band, main_band, upper_band = band_set
    reduced_rows, solutions = reduce_segment(lower_band, main_band, upper_band, right_side)
    first_value, last_value = gathered_join(reduced_rows, direction)
    return assemble(first_value, last_value, solutions)


def local(flow_state, x_codes, y_codes):
    cells_x = flow_state.shape[1]
    cells_y = flow_state.shape[2] // NZ
    local_block = flow_state.reshape(5, cells_x, cells_y, NZ)
    padded = padded_2(local_block, (("gx", 1), ("gy", 2)), 1)
    start_x = lax.axis_index("gx") == 0
    end_x = lax.axis_index("gx") == lax.axis_size("gx") - 1
    start_y = lax.axis_index("gy") == 0
    end_y = lax.axis_index("gy") == lax.axis_size("gy") - 1
    padded = padded.at[:, 0].set(jnp.where(start_x, padded[:, 1], padded[:, 0]))
    padded = padded.at[:, -1].set(jnp.where(end_x, padded[:, -2], padded[:, -1]))
    padded = padded.at[:, :, 0].set(jnp.where(start_y, padded[:, :, 1], padded[:, :, 0]))
    padded = padded.at[:, :, -1].set(jnp.where(end_y, padded[:, :, -2], padded[:, :, -1]))
    residual, primitive = explicit_terms(padded)
    interior = tuple((member[1:-1, 1:-1] for member in primitive))
    changes = primitive_change(residual, interior)
    speeds_x = eigenvalues(tuple((member[:, 1:-1] for member in primitive)), 1).reshape(
        5, cells_x + 2, cells_y * NZ
    )
    codes_x = jnp.broadcast_to(x_codes[:, :, None], (2, cells_y, NZ)).reshape(2, cells_y * NZ)
    band_set = coefficients(speeds_x, codes_x, start_x, end_x)
    right_x = to_characteristic(changes, interior, 1).reshape(5, cells_x, cells_y * NZ)
    solved_x = solve_lines(band_set, right_x, "x").reshape(5, cells_x, cells_y, NZ)
    changes = from_characteristic(solved_x, interior, 1)
    right_y = jnp.transpose(to_characteristic(changes, interior, 2), (0, 2, 1, 3)).reshape(
        5, cells_y, cells_x * NZ
    )
    speeds_y = jnp.transpose(
        eigenvalues(tuple((member[1:-1] for member in primitive)), 2), (0, 2, 1, 3)
    ).reshape(5, cells_y + 2, cells_x * NZ)
    codes_y = jnp.broadcast_to(y_codes[:, :, None], (2, cells_x, NZ)).reshape(2, cells_x * NZ)
    band_set = coefficients(speeds_y, codes_y, start_y, end_y)
    solved_y = jnp.transpose(
        solve_lines(band_set, right_y, "y").reshape(5, cells_y, cells_x, NZ), (0, 2, 1, 3)
    )
    changes = from_characteristic(solved_y, interior, 2)
    return to_conserved(changes, interior).reshape(5, cells_x, cells_y * NZ)


def solution(mesh):
    in_specs = (P(None, "gx", "gy"), P(None, "gy"), P(None, "gx"))
    out_specs = P(None, "gx", "gy")
    return jax.shard_map(local, mesh=mesh, in_specs=in_specs, out_specs=out_specs, check_vma=False)
```

profile of v0, /device:TPU:0, one launch (start us, length us, event | category | flops | bytes accessed | tf_op | source)
XLA Modules:
  0.0 151.8 jit_solution(18336795575651251900)
XLA Ops:
  7.7 2.4 %collective-permute-start = (f32[5,1,32,32]{3,2,1,0:T(8,128)S(1)}, f32[5,1,32,32]{3,2,1,0:T(8,128)S(1)}, u32[]{:S(2)}, u32[]{:S(2)}) collective-permute-start(f32[5,1,32,32]{3,2,1,0:T(8,128)S(1)} %get-tuple-element.998), channel_id=1, source_target_pairs={{0,4},{4,8},{8,12},{12,16},{16,20},{20,24},{24,28},{1,5},{5,9},{9,... | collective-permute-start | bytes 61448 | tf_op jit(solution)/shard_map/ppermute | solution.py:19
  12.3 3.1 %collective-permute-done.1 = f32[5,1,32,32]{3,2,1,0:T(8,128)S(1)} collective-permute-done((f32[5,1,32,32]{3,2,1,0:T(8,128)S(1)}, f32[5,1,32,32]{3,2,1,0:T(8,128)S(1)}, u32[]{:S(2)}, u32[]{:S(2)}) %collective-permute-start.1) | collective-permute-done | bytes 20512 | tf_op jit(solution)/shard_map/ppermute | solution.py:22
  15.4 3.5 %collective-permute-start.2 = (f32[5,10,1,32]{3,2,1,0:T(1,128)S(1)}, f32[5,10,1,32]{3,2,1,0:T(1,128)S(1)}, u32[]{:S(2)}, u32[]{:S(2)}) collective-permute-start(f32[5,10,1,32]{3,2,1,0:T(1,128)S(1)} %get-tuple-element.991), channel_id=1, source_target_pairs={{0,1},{1,2},{2,3},{4,5},{5,6},{6,7},{8,9},{9,10},{10,11},{12,13},{... | collective-permute-start | bytes 19208 | tf_op jit(solution)/shard_map/ppermute | solution.py:19
  22.1 2.5 %collective-permute-done.3 = f32[5,10,1,32]{3,2,1,0:T(1,128)S(1)} collective-permute-done((f32[5,10,1,32]{3,2,1,0:T(1,128)S(1)}, f32[5,10,1,32]{3,2,1,0:T(1,128)S(1)}, u32[]{:S(2)}, u32[]{:S(2)}) %collective-permute-start.3) | collective-permute-done | bytes 6432 | tf_op jit(solution)/shard_map/ppermute | solution.py:22
  36.0 22.7 %all-gather.4.cloned.1.call-done = f32[64,5,1024]{2,0,1:T(8,128)} async-done(((f32[8,5,1024]{2,0,1:T(8,128)}), f32[64,5,1024]{2,0,1:T(8,128)}) %all-gather.4.cloned.1.call-update) | async-done | bytes 1310736 | tf_op jit(solution)/shard_map/all_gather | solution.py:273
  58.7 1.7 %reshape.6437 = f32[16,4,5,1024]{3,1,0,2:T(4,128)S(1)} reshape(f32[64,5,1024]{2,0,1:T(8,128)} %all-gather.4.cloned.1.call-done) | data formatting | bytes 2621440 | tf_op jit(solution)/shard_map/reshape | solution.py:279
  64.9 23.7 %while.80 = (s32[]{:T(128)}, f32[5,1024]{1,0:T(8,128)}, f32[5,1024]{1,0:T(8,128)}, f32[16,5,1024]{2,1,0:T(8,128)}, f32[16,5,1024]{2,1,0:T(8,128)}, /*index=5*/f3...) while((s32[]{:T(128)}, f32[5,1024]{1,0:T(8,128)}, ...), condition=%wide.region_1.2_spmd.clone, body=%wide.region_0.1_spmd.clone.sunk | while | flops 40963 | bytes 291447 | solution.py:193
  66.3 1.5 bitcast_dynamic-update-slice_fusion.19
  67.8 1.5 bitcast_dynamic-update-slice_fusion.19
  69.3 1.5 bitcast_dynamic-update-slice_fusion.19
  70.8 1.5 bitcast_dynamic-update-slice_fusion.19
  72.3 1.5 bitcast_dynamic-update-slice_fusion.19
  73.8 1.5 bitcast_dynamic-update-slice_fusion.19
  75.2 1.5 bitcast_dynamic-update-slice_fusion.19
  76.7 1.5 bitcast_dynamic-update-slice_fusion.19
  78.2 1.5 bitcast_dynamic-update-slice_fusion.19
  79.7 1.5 bitcast_dynamic-update-slice_fusion.19
  81.2 1.5 bitcast_dynamic-update-slice_fusion.19
  82.7 1.5 bitcast_dynamic-update-slice_fusion.19
  84.1 1.5 bitcast_dynamic-update-slice_fusion.19
  85.6 1.5 bitcast_dynamic-update-slice_fusion.19
  87.1 1.5 bitcast_dynamic-update-slice_fusion.19
  88.7 22.7 %while.81 = (s32[]{:T(128)}, f32[5,1024]{1,0:T(8,128)}, f32[16,5,1024]{2,1,0:T(8,128)S(1)}, f32[16,5,1024]{2,1,0:T(8,128)}, f32[16,5,1024]{2,1,0:T(8,128)}, /*index=5*/s32[]{:T(128)}, s32[]{:T(128)}, s32[]{:T(128)}) while((s32[]{:T(128)}, f32[5,1024]{1,0:T(8,128)}, f32[16,5,1024]{2,1,0:T(8,128)S(1)}, f32[16,5,1024]{2,1,0:T(8,128)}, ...), condition=%wide.region_3.4_spmd.clone, body=%wide.region_2.3_spmd.clone.sunk | while | flops 15364 | bytes 114799 | solution.py:202
  117.7 13.6 %all-gather.1 = f32[32,5,256]{2,0,1:T(8,128)S(1)} all-gather(f32[8,5,256]{2,0,1:T(8,128)S(1)} %stack.267), channel_id=3, replica_groups=mesh['gx'=8,'gy'=4] {'gy'}, dimensions={0}, use_global_device_ids=true | all-gather | bytes 204800 | tf_op jit(solution)/shard_map/all_gather | solution.py:276
  (456 shorter events, 64.3 us)
Async XLA Ops:
  6.5 13.7 %copy-start.108 = (s32[2,8]{1,0:T(2,128)S(1)}, s32[2,8]{1,0:T(2,128)}, u32[]{:S(2)}) copy-start(s32[2,8]{1,0:T(2,128)} %param.37) | copy-start | bytes 196
  6.5 52.2 %all-gather.4.cloned.1.call-start = ((), (), s32[]{:S(2)}) async-start(), calls=%async_computation | async-start | bytes 1474560 | tf_op jit(solution)/shard_map/all_gather | solution.py:273
  7.7 4.5 %collective-permute-start = (f32[5,1,32,32]{3,2,1,0:T(8,128)S(1)}, f32[5,1,32,32]{3,2,1,0:T(8,128)S(1)}, u32[]{:S(2)}, u32[]{:S(2)}) collective-permute-start(f32[5,1,32,32]{3,2,1,0:T(8,128)S(1)} %get-tuple-element.998), channel_id=1, source_target_pairs={{0,4},{4,8},{8,12},{12,16},{16,20},{20,24},{24,28},{1,5},{5,9},{9,... | collective-permute-start | bytes 61448 | tf_op jit(solution)/shard_map/ppermute | solution.py:19
  10.1 5.3 %collective-permute-start.1 = (f32[5,1,32,32]{3,2,1,0:T(8,128)S(1)}, f32[5,1,32,32]{3,2,1,0:T(8,128)S(1)}, u32[]{:S(2)}, u32[]{:S(2)}) collective-permute-start(f32[5,1,32,32]{3,2,1,0:T(8,128)S(1)} %get-tuple-element.997), channel_id=1, source_target_pairs={{4,0},{8,4},{12,8},{16,12},{20,16},{24,20},{28,24},{5,1},{9,5},{13... | collective-permute-start | bytes 61448 | tf_op jit(solution)/shard_map/ppermute | solution.py:22
  15.4 6.7 %collective-permute-start.2 = (f32[5,10,1,32]{3,2,1,0:T(1,128)S(1)}, f32[5,10,1,32]{3,2,1,0:T(1,128)S(1)}, u32[]{:S(2)}, u32[]{:S(2)}) collective-permute-start(f32[5,10,1,32]{3,2,1,0:T(1,128)S(1)} %get-tuple-element.991), channel_id=1, source_target_pairs={{0,1},{1,2},{2,3},{4,5},{5,6},{6,7},{8,9},{9,10},{10,11},{12,13},{... | collective-permute-start | bytes 19208 | tf_op jit(solution)/shard_map/ppermute | solution.py:19
  18.9 5.7 %collective-permute-start.3 = (f32[5,10,1,32]{3,2,1,0:T(1,128)S(1)}, f32[5,10,1,32]{3,2,1,0:T(1,128)S(1)}, u32[]{:S(2)}, u32[]{:S(2)}) collective-permute-start(f32[5,10,1,32]{3,2,1,0:T(1,128)S(1)} %get-tuple-element.992), channel_id=1, source_target_pairs={{1,0},{2,1},{3,2},{5,4},{6,5},{7,6},{9,8},{10,9},{11,10},{13,12},{... | collective-permute-start | bytes 19208 | tf_op jit(solution)/shard_map/ppermute | solution.py:22
  88.6 22.8 %copy-start.2 = (f32[5,1,1024]{2,1,0:T(1,128)S(1)}, f32[5,1,1024]{2,1,0:T(1,128)}, u32[]{:S(2)}) copy-start(f32[5,1,1024]{2,1,0:T(1,128)} %get-tuple-element.938) | copy-start | bytes 61444
  88.6 22.8 %copy-start.3 = (f32[5,1,1024]{2,1,0:T(1,128)S(1)}, f32[5,1,1024]{2,1,0:T(1,128)}, u32[]{:S(2)}) copy-start(f32[5,1,1024]{2,1,0:T(1,128)} %get-tuple-element.939) | copy-start | bytes 61444
  88.6 22.8 %copy-start.4 = (f32[5,1,1024]{2,1,0:T(1,128)S(1)}, f32[5,1,1024]{2,1,0:T(1,128)}, u32[]{:S(2)}) copy-start(f32[5,1,1024]{2,1,0:T(1,128)} %get-tuple-element.936) | copy-start | bytes 61444
  88.6 22.8 %copy-start.5 = (f32[5,1,1024]{2,1,0:T(1,128)S(1)}, f32[5,1,1024]{2,1,0:T(1,128)}, u32[]{:S(2)}) copy-start(f32[5,1,1024]{2,1,0:T(1,128)} %get-tuple-element.937) | copy-start | bytes 61444
  88.6 22.8 %copy-start.62 = (f32[5,1,1024]{2,1,0:T(1,128)S(1)}, f32[5,1,1024]{2,1,0:T(1,128)}, u32[]{:S(2)}) copy-start(f32[5,1,1024]{2,1,0:T(1,128)} %get-tuple-element.935) | copy-start | bytes 61444
  116.5 15.3 %copy-start = (f32[5,256]{1,0:T(8,128)S(1)}, f32[5,256]{1,0:T(8,128)}, u32[]{:S(2)}) copy-start(f32[5,256]{1,0:T(8,128)} %custom-call.3) | copy-start | bytes 15364
  116.5 15.3 %copy-start.1 = (f32[5,256]{1,0:T(8,128)S(1)}, f32[5,256]{1,0:T(8,128)}, u32[]{:S(2)}) copy-start(f32[5,256]{1,0:T(8,128)} %custom-call.4) | copy-start | bytes 15364
  117.7 15.3 %copy-start.76 = (f32[5,1,256]{2,1,0:T(1,128)S(1)}, f32[5,1,256]{2,1,0:T(1,128)}, u32[]{:S(2)}) copy-start(f32[5,1,256]{2,1,0:T(1,128)} %get-tuple-element.727) | copy-start | bytes 15364
  117.7 15.3 %copy-start.78 = (f32[5,1,256]{2,1,0:T(1,128)S(1)}, f32[5,1,256]{2,1,0:T(1,128)}, u32[]{:S(2)}) copy-start(f32[5,1,256]{2,1,0:T(1,128)} %get-tuple-element.814) | copy-start | bytes 15364
  131.9 7.3 %copy-start.83 = (f32[5,1,256]{2,1,0:T(1,128)S(1)}, f32[5,1,256]{2,1,0:T(1,128)}, u32[]{:S(2)}) copy-start(f32[5,1,256]{2,1,0:T(1,128)} %get-tuple-element.748) | copy-start | bytes 15364
  131.9 7.3 %copy-start.65 = (f32[5,1,256]{2,1,0:T(1,128)S(1)}, f32[5,1,256]{2,1,0:T(1,128)}, u32[]{:S(2)}) copy-start(f32[5,1,256]{2,1,0:T(1,128)} %get-tuple-element.751) | copy-start | bytes 15364
  131.9 7.3 %copy-start.66 = (f32[5,1,256]{2,1,0:T(1,128)S(1)}, f32[5,1,256]{2,1,0:T(1,128)}, u32[]{:S(2)}) copy-start(f32[5,1,256]{2,1,0:T(1,128)} %get-tuple-element.838) | copy-start | bytes 15364
  131.9 7.3 %copy-start.80 = (f32[5,1,256]{2,1,0:T(1,128)S(1)}, f32[5,1,256]{2,1,0:T(1,128)}, u32[]{:S(2)}) copy-start(f32[5,1,256]{2,1,0:T(1,128)} %get-tuple-element.749) | copy-start | bytes 15364
  131.9 7.3 %copy-start.81 = (f32[5,1,256]{2,1,0:T(1,128)S(1)}, f32[5,1,256]{2,1,0:T(1,128)}, u32[]{:S(2)}) copy-start(f32[5,1,256]{2,1,0:T(1,128)} %get-tuple-element.750) | copy-start | bytes 15364
  131.9 7.3 %copy-start.86 = (f32[5,1,256]{2,1,0:T(1,128)S(1)}, f32[5,1,256]{2,1,0:T(1,128)}, u32[]{:S(2)}) copy-start(f32[5,1,256]{2,1,0:T(1,128)} %get-tuple-element.836) | copy-start | bytes 15364
  131.9 7.3 %copy-start.87 = (f32[5,1,256]{2,1,0:T(1,128)S(1)}, f32[5,1,256]{2,1,0:T(1,128)}, u32[]{:S(2)}) copy-start(f32[5,1,256]{2,1,0:T(1,128)} %get-tuple-element.837) | copy-start | bytes 15364
  131.9 7.4 %copy-start.79 = (f32[5,1,256]{2,1,0:T(1,128)S(1)}, f32[5,1,256]{2,1,0:T(1,128)}, u32[]{:S(2)}) copy-start(f32[5,1,256]{2,1,0:T(1,128)} %get-tuple-element.752) | copy-start | bytes 15364
  132.0 7.4 %copy-start.82 = (f32[5,1,256]{2,1,0:T(1,128)S(1)}, f32[5,1,256]{2,1,0:T(1,128)}, u32[]{:S(2)}) copy-start(f32[5,1,256]{2,1,0:T(1,128)} %get-tuple-element.839) | copy-start | bytes 15364
  (92 other events, 260.1 us)
Sparse Core Ops, SparseCore 0:
  32.3 26.3 all-gather.3
where the time goes:
time: 155 us; the launch traced here: 152 us
  other arithmetic  65.2 us (42%)
  waiting for transfers between devices  28.4 us (18%)
  local copies, waits for them, and re-layouts  19.6 us (13%)
  between operations  15.8 us (10%)
  blocking collectives  13.6 us (9%)
  starting transfers between devices  8.47 us (5%)
    dynamic_update_slice x48, other arithmetic, thomas_rows(): lax.scan(forward_step, (nothing, nothing), (lower_band, main_band, upper_...  46.6 us
    all_gather x1, waiting for transfers between devices, gathered_join(): everything = lax.all_gather(stacked, 'gx', axis=0, tiled=True)  22.7 us
    all_gather x1, blocking collectives, gathered_join(): everything = lax.all_gather(stacked, 'gy', axis=0, tiled=True)  13.6 us
    ppermute x2, starting transfers between devices, padded_2(): lax.ppermute(lax.slice_in_dim(block, block.shape[dim] - width, None, axis...  5.88 us
    ppermute x2, waiting for transfers between devices, padded_2(): lax.ppermute(lax.slice_in_dim(block, 0, width, axis=dim), axis, backward)  5.63 us
    sub x10, other arithmetic, reduce_segment(): forward_value - uppers[back_at] * later_value  4.89 us
    add x12, other arithmetic, assemble(): piece_u + piece_p * first_value + piece_q * last_value  4.67 us
    another operation x35, local copies, waits for them, and re-layouts, assemble(): return jnp.stack(columns, axis=1)  3.61 us
  transfers between devices with their start and end apart: 5, of which 3 were waited for; matrix products, arithmetic and copies ran while one was open for 4% of the time, Pallas kernels for 0%

commit v1 on v0

v1 whole, which is shorter than its diff:
```python
import functools

import jax
import jax.numpy as jnp
from jax import lax
from jax.experimental import pallas as pl
from jax.experimental.pallas import tpu as pltpu
from jax.sharding import PartitionSpec as P

NZ = 32
GAMMA = 1.4
SIGMA = 0.5
DIFFUSE = 400.0
LANES = 128
GROUPS = LANES // NZ
SPEED_OF = (0, 1, 1, 1, 2)
ROWS = 22


def primitives(q):
    inverse = 1.0 / q[0]
    vel_u, vel_v, vel_w = q[1] * inverse, q[2] * inverse, q[3] * inverse
    kinetic = 0.5 * (vel_u * vel_u + vel_v * vel_v + vel_w * vel_w)
    pressure = (GAMMA - 1.0) * (q[4] - q[0] * kinetic)
    sound = jnp.sqrt(GAMMA * pressure * inverse)
    return inverse, vel_u, vel_v, vel_w, kinetic, pressure, sound


def flux(q, normal, speed, pressure):
    parts = [q[normal], q[1] * speed, q[2] * speed, q[3] * speed, speed * (q[4] + pressure)]
    parts[normal] = parts[normal] + pressure
    return parts


def flux_of(q, normal, speed, pressure):
    return [q[normal]] + [
        q[f] * speed + pressure if f == normal else q[f] * speed for f in (1, 2, 3)
    ] + [speed * (q[4] + pressure)]


def three_speeds(velocity, sound):
    return (velocity - sound, velocity, velocity + sound)


def sweep(speeds, rights, first, last):
    cells = len(rights)
    ups, owns, lefts = [], [], []
    for i in range(cells):
        up_i, own_i, left_i = [], [None] * 5, []
        for k in range(3):
            lower = -0.5 * SIGMA * speeds[i][k] - DIFFUSE
            upper = 0.5 * SIGMA * speeds[i + 2][k] - DIFFUSE
            main = 1.0 + 2.0 * DIFFUSE
            if i == 0:
                main = main + lower * first[1]
                lower = lower * first[0]
            if i == cells - 1:
                main = main + upper * last[1]
                upper = upper * last[0]
            pivot = main if i == 0 else main - lower * ups[-1][k]
            inverse = 1.0 / pivot
            up_i.append(upper * inverse)
            scaled = lower * inverse
            left_i.append(-scaled if i == 0 else -scaled * lefts[-1][k])
            for f in range(5):
                if SPEED_OF[f] == k:
                    own = rights[i][f] * inverse
                    own_i[f] = own if i == 0 else own - scaled * owns[-1][f]
        ups.append(up_i)
        owns.append(own_i)
        lefts.append(left_i)
    right_terms = [None] * cells
    right_terms[-1] = [-u for u in ups[-1]]
    for i in range(cells - 2, -1, -1):
        owns[i] = [owns[i][f] - ups[i][SPEED_OF[f]] * owns[i + 1][f] for f in range(5)]
        lefts[i] = [lefts[i][k] - ups[i][k] * lefts[i + 1][k] for k in range(3)]
        right_terms[i] = [-ups[i][k] * right_terms[i + 1][k] for k in range(3)]
    return owns, lefts, right_terms


def ends_of(owns, lefts, rights):
    return owns[0] + owns[-1] + lefts[0] + rights[0] + lefts[-1] + rights[-1]


def unpack(rows, fields=5, speeds=3):
    out, at = [], 0
    for n in (fields, fields, speeds, speeds, speeds, speeds):
        out.append(rows[at : at + n])
        at += n
    return out


def merge(low, own, other, speed_of):
    fields = len(speed_of)
    speeds = max(speed_of) + 1
    before = [jnp.where(low, a, b) for a, b in zip(own, other)]
    after = [jnp.where(low, b, a) for a, b in zip(own, other)]
    a_f, a_e, b_f, c_f, b_e, c_e = unpack(before, fields, speeds)
    a_g, a_h, b_g, c_g, b_h, c_h = unpack(after, fields, speeds)
    inv = [1.0 / (1.0 - c_e[k] * b_g[k]) for k in range(speeds)]
    e_1 = [b_e[k] * inv[k] for k in range(speeds)]
    f_2 = [c_g[k] * inv[k] for k in range(speeds)]
    e_2 = [c_e[k] * f_2[k] for k in range(speeds)]
    f_1 = [b_g[k] * e_1[k] for k in range(speeds)]
    e_0 = [(a_e[f] + c_e[speed_of[f]] * a_g[f]) * inv[speed_of[f]] for f in range(fields)]
    f_0 = [(a_g[f] + b_g[speed_of[f]] * a_e[f]) * inv[speed_of[f]] for f in range(fields)]
    joined = (
        [a_f[f] + c_f[speed_of[f]] * f_0[f] for f in range(fields)]
        + [a_h[f] + b_h[speed_of[f]] * e_0[f] for f in range(fields)]
        + [b_f[k] + c_f[k] * f_1[k] for k in range(speeds)]
        + [c_f[k] * f_2[k] for k in range(speeds)]
        + [b_h[k] * e_1[k] for k in range(speeds)]
        + [c_h[k] + b_h[k] * e_2[k] for k in range(speeds)]
    )
    side = [jnp.where(low, f, e) for f, e in zip(f_0 + f_1 + f_2, e_0 + e_1 + e_2)]
    return joined, side


def facing(low, rows, fields=5, speeds=3):
    a_f, a_e, b_f, c_f, b_e, c_e = unpack(rows, fields, speeds)
    return [jnp.where(low, e, f) for e, f in zip(a_e + c_e, a_f + b_f)]


def last_join(low, own, other, speed_of):
    fields = len(speed_of)
    result = []
    for f in range(fields):
        k = fields + speed_of[f]
        result.append((other[f] + other[k] * own[f]) / (1.0 - own[k] * other[k]))
    return result


def step_down(low, side, outer, speed_of):
    fields = len(speed_of)
    speeds = max(speed_of) + 1
    left, right = outer
    new = [
        side[f] + side[fields + speed_of[f]] * left[f] + side[fields + speeds + speed_of[f]] * right[f]
        for f in range(fields)
    ]
    return (
        [jnp.where(low, a, b) for a, b in zip(left, new)],
        [jnp.where(low, b, a) for a, b in zip(right, new)],
    )


def from_last(low, new):
    zero = jnp.zeros_like(new[0])
    return [jnp.where(low, zero, x) for x in new], [jnp.where(low, x, zero) for x in new]


def bit_low(axis, level):
    return (lax.axis_index(axis) >> level) % 2 == 0


def pack_kernel(flow_ref, qx_ref, near_ref, far_ref, one_ref, two_ref):
    cells = flow_ref.shape[1]
    chunks = flow_ref.shape[2] // LANES
    even_x = bit_low("gx", 0)
    even_y = bit_low("gy", 0)
    for f in range(5):
        for c in range(chunks):
            qx_ref[f, pl.ds(c, cells, stride=chunks), :] = flow_ref[f, :, c * LANES : (c + 1) * LANES]
        low = flow_ref[f, :, 0:LANES]
        high = flow_ref[f, :, (chunks - 1) * LANES : chunks * LANES]
        one_ref[f] = jnp.where(even_y, high, low)
        two_ref[f] = jnp.where(even_y, low, high)
    for f in range(5):
        low = qx_ref[f, 0:chunks, :]
        high = qx_ref[f, (cells - 1) * chunks : cells * chunks, :]
        near_ref[f] = jnp.where(even_x, high, low)
        far_ref[f] = jnp.where(even_x, low, high)


def y_halos(flow_ref, one_ref, two_ref, f):
    chunks = flow_ref.shape[2] // LANES
    at, count = lax.axis_index("gy"), lax.axis_size("gy")
    even = bit_low("gy", 0)
    one, two = one_ref[f], two_ref[f]
    low = jnp.where(even, two, one)
    high = jnp.where(even, one, two)
    own_low = pltpu.roll(flow_ref[f, :, 0:LANES], LANES - NZ, 1)
    own_high = pltpu.roll(flow_ref[f, :, (chunks - 1) * LANES : chunks * LANES], NZ, 1)
    return jnp.where(at == 0, own_low, low), jnp.where(at == count - 1, own_high, high)


def x_kernel(
    flow_ref, qx_ref, near_ref, far_ref, one_ref, two_ref, edge_ref,
    rows_ref, own_ref, left_ref, right_ref, halo_low, halo_high,
):
    cells = flow_ref.shape[1]
    chunks = flow_ref.shape[2] // LANES
    at, count = lax.axis_index("gx"), lax.axis_size("gx")
    even = bit_low("gx", 0)
    lane = lax.broadcasted_iota(jnp.int32, (chunks, LANES), 1)
    sub = lax.broadcasted_iota(jnp.int32, (chunks, LANES), 0)
    lows, highs = zip(*[y_halos(flow_ref, one_ref, two_ref, f) for f in range(5)])
    for ghosts, ref, turn in ((lows, halo_low, NZ), (highs, halo_high, LANES - NZ)):
        prim = primitives(ghosts)
        for n, value in enumerate(list(ghosts) + [prim[2], prim[5]]):
            ref[n] = pltpu.roll(value, turn, 1)
    rows = [[qx_ref[f, i * chunks : (i + 1) * chunks, :] for f in range(5)] for i in range(cells)]
    near, far = [near_ref[f] for f in range(5)], [far_ref[f] for f in range(5)]
    ghost_low = [
        jnp.where(at == 0, rows[0][f], jnp.where(even, far[f], near[f])) for f in range(5)
    ]
    ghost_high = [
        jnp.where(at == count - 1, rows[-1][f], jnp.where(even, near[f], far[f])) for f in range(5)
    ]
    padded = [ghost_low] + rows + [ghost_high]
    prims = [primitives(q) for q in padded]
    speeds = [three_speeds(p[1], p[6]) for p in prims]
    fluxes = [flux_of(q, 1, p[1], p[5]) for q, p in zip(padded, prims)]

    up_edge = jnp.logical_and(sub == chunks - 1, lane >= LANES - NZ)
    down_edge = jnp.logical_and(sub == 0, lane < NZ)
    z_of = lane % NZ

    def y_next(value, n, i):
        turned = pltpu.roll(value, LANES - NZ, 1)
        turned = jnp.where(lane >= LANES - NZ, pltpu.roll(turned, chunks - 1, 0), turned)
        ghost = jnp.broadcast_to(halo_high[n, i : i + 1, :], turned.shape)
        return jnp.where(up_edge, ghost, turned)

    def y_before(value, n, i):
        turned = pltpu.roll(value, NZ, 1)
        turned = jnp.where(lane < NZ, pltpu.roll(turned, 1, 0), turned)
        ghost = jnp.broadcast_to(halo_low[n, i : i + 1, :], turned.shape)
        return jnp.where(down_edge, ghost, turned)

    def z_change(value):
        after = jnp.where(z_of == NZ - 1, pltpu.roll(value, NZ - 1, 1), pltpu.roll(value, LANES - 1, 1))
        before = jnp.where(z_of == 0, pltpu.roll(value, LANES - NZ + 1, 1), pltpu.roll(value, 1, 1))
        return after - before

    rights = []
    for i in range(cells):
        q = padded[i + 1]
        inverse, vel_u, vel_v, vel_w, kinetic, pressure, sound = prims[i + 1]
        after = [y_next(v, n, i) for n, v in enumerate(list(q) + [vel_v, pressure])]
        before = [y_before(v, n, i) for n, v in enumerate(list(q) + [vel_v, pressure])]
        flux_after = flux_of(after, 2, after[5], after[6])
        flux_before = flux_of(before, 2, before[5], before[6])
        flux_z = flux_of(q, 3, vel_w, pressure)
        res = []
        for f in range(5):
            change = (
                (fluxes[i + 2][f] - fluxes[i][f])
                + (flux_after[f] - flux_before[f])
                + z_change(flux_z[f])
            )
            smooth = padded[i + 2][f] + padded[i][f] + after[f] + before[f] - 4.0 * q[f]
            res.append(-0.5 * SIGMA * change + DIFFUSE * smooth)
        du = (res[1] - vel_u * res[0]) * inverse
        dv = (res[2] - vel_v * res[0]) * inverse
        dw = (res[3] - vel_w * res[0]) * inverse
        dp = (GAMMA - 1.0) * (
            res[4] - vel_u * res[1] - vel_v * res[2] - vel_w * res[3] + kinetic * res[0]
        )
        normal = q[0] * sound * du
        rights.append([dp - normal, sound * sound * res[0] - dp, dv, dw, dp + normal])
    owns, lefts, right_terms = sweep(
        speeds, rights, (edge_ref[0], edge_ref[1]), (edge_ref[2], edge_ref[3])
    )
    for n, value in enumerate(ends_of(owns, lefts, right_terms)):
        rows_ref[n] = value
    for i in range(cells):
        for f in range(5):
            own_ref[f, i] = owns[i][f]
        for k in range(3):
            left_ref[k, i] = lefts[i][k]
            right_ref[k, i] = right_terms[i][k]


def merge_kernel(axis, level, final, speed_of, own_ref, other_ref, out_ref, side_ref):
    own = [own_ref[n] for n in range(own_ref.shape[0])]
    other = [other_ref[n] for n in range(other_ref.shape[0])]
    joined, side = merge(bit_low(axis, level), own, other, speed_of)
    if final:
        joined = facing(bit_low(axis, level + 1), joined, len(speed_of), max(speed_of) + 1)
    for n, value in enumerate(joined):
        out_ref[n] = value
    for n, value in enumerate(side):
        side_ref[n] = value


def outer_values(axis, levels, speed_of, own_ref, other_ref, side_refs):
    own = [own_ref[n] for n in range(own_ref.shape[0])]
    other = [other_ref[n] for n in range(other_ref.shape[0])]
    low = bit_low(axis, levels - 1)
    outer = from_last(low, last_join(low, own, other, speed_of))
    for level in range(levels - 2, -1, -1):
        ref = side_refs[level]
        side = [ref[n] for n in range(ref.shape[0])]
        outer = step_down(bit_low(axis, level), side, outer, speed_of)
    return outer


PACKED_SPEED = (0, 0)


def y_kernel(levels, *refs):
    (flow_ref, qx_ref, one_ref, two_ref, edge_ref, own_ref, left_ref, right_ref,
     mine_ref, other_ref) = refs[:10]
    sides = refs[10 : 10 + levels - 1]
    (out_ref, yown_ref, yleft_ref, yright_ref, s0_ref, s1_ref, turn_ref) = refs[10 + levels - 1 :]
    cells = flow_ref.shape[1]
    chunks = flow_ref.shape[2] // LANES
    steps = chunks
    outer_l, outer_r = outer_values("gx", levels, SPEED_OF, mine_ref, other_ref, sides)
    for i in range(cells):
        q = [qx_ref[f, i * chunks : (i + 1) * chunks, :] for f in range(5)]
        inverse, vel_u, vel_v, vel_w, kinetic, pressure, sound = primitives(q)
        wave = [
            own_ref[f, i] + left_ref[SPEED_OF[f], i] * outer_l[f] + right_ref[SPEED_OF[f], i] * outer_r[f]
            for f in range(5)
        ]
        impedance = q[0] * sound
        squared = sound * sound
        dp = 0.5 * (wave[0] + wave[4])
        du = (wave[4] - wave[0]) / (2.0 * impedance)
        dr = (wave[1] + dp) / squared
        normal = impedance * wave[2]
        values = [dp - normal, squared * dr - dp, du, wave[3], dp + normal, vel_v, sound]
        for n, value in enumerate(values):
            turn_ref[n, i * chunks : (i + 1) * chunks, :] = value
    lane = lax.broadcasted_iota(jnp.int32, (cells, LANES), 1)
    group = lane // NZ

    def regroup(n):
        parts = [turn_ref[n, pl.ds(c, cells, stride=chunks), :] for c in range(chunks)]
        result = []
        for jj in range(steps):
            pieces = []
            for s in range(GROUPS):
                y = s * steps + jj
                piece = parts[y // GROUPS]
                shift = (s - y % GROUPS) * NZ % LANES
                pieces.append(pltpu.roll(piece, shift, 1) if shift else piece)
            value = pieces[0]
            for s in range(1, GROUPS):
                value = jnp.where(group == s, pieces[s], value)
            result.append(value)
        return result

    fields = [regroup(n) for n in range(7)]
    rights = [[fields[f][jj] for f in range(5)] for jj in range(steps)]
    speeds = [three_speeds(fields[5][jj], fields[6][jj]) for jj in range(steps)]
    lows, highs = zip(*[y_halos(flow_ref, one_ref, two_ref, f) for f in range(5)])
    low_prim, high_prim = primitives(lows), primitives(highs)
    low_speed = three_speeds(low_prim[2], low_prim[6])
    high_speed = three_speeds(high_prim[2], high_prim[6])
    before = tuple(
        pltpu.roll(jnp.where(group == GROUPS - 1, low_speed[k], speeds[-1][k]), NZ, 1) for k in range(3)
    )
    after = tuple(
        pltpu.roll(jnp.where(group == 0, high_speed[k], speeds[0][k]), LANES - NZ, 1) for k in range(3)
    )
    owns, lefts, right_terms = sweep(
        [before] + speeds + [after], rights, (edge_ref[0], edge_ref[1]), (edge_ref[2], edge_ref[3])
    )
    for i in range(steps):
        for f in range(5):
            yown_ref[f, i] = owns[i][f]
        for k in range(3):
            yleft_ref[k, i] = lefts[i][k]
            yright_ref[k, i] = right_terms[i][k]
    ends = ends_of(owns, lefts, right_terms)
    low = group % 2 == 0
    other = [jnp.where(low, pltpu.roll(v, LANES - NZ, 1), pltpu.roll(v, NZ, 1)) for v in ends]
    ends, side = merge(low, ends, other, SPEED_OF)
    for n, value in enumerate(side):
        s0_ref[n] = value
    low = group // 2 == 0
    other = [pltpu.roll(v, LANES // 2, 1) for v in ends]
    ends, side = merge(low, ends, other, SPEED_OF)
    for n, value in enumerate(side):
        s1_ref[n] = value
    for n, value in enumerate(pack_groups(group, ends)):
        out_ref[n] = value


def pack_groups(group, ends):
    a_f, a_e, b_f, c_f, b_e, c_e = unpack(ends)

    def four(a, b, c, d):
        return jnp.where(group == 0, a, jnp.where(group == 1, b, jnp.where(group == 2, c, d)))

    firsts = [four(a_f[0], a_f[1], a_f[4], a_f[2]), a_f[3]]
    lasts = [four(a_e[0], a_e[1], a_e[4], a_e[2]), a_e[3]]
    factors = [four(t[0], t[1], t[2], t[1]) for t in (b_f, c_f, b_e, c_e)]
    return firsts + lasts + factors


def spread(group, value, source):
    half = jnp.where(group // 2 == source // 2, value, pltpu.roll(value, LANES // 2, 1))
    down, up = pltpu.roll(half, NZ, 1), pltpu.roll(half, LANES - NZ, 1)
    if source % 2 == 0:
        return jnp.where(group % 2 == 0, half, down)
    return jnp.where(group % 2 == 1, half, up)


def final_kernel(levels, *refs):
    (flow_ref, yown_ref, yleft_ref, yright_ref, s0_ref, s1_ref, mine_ref, other_ref) = refs[:8]
    sides = refs[8 : 8 + levels - 1]
    out_ref = refs[8 + levels - 1]
    cells = flow_ref.shape[1]
    chunks = flow_ref.shape[2] // LANES
    steps = chunks
    lane = lax.broadcasted_iota(jnp.int32, (cells, LANES), 1)
    group = lane // NZ
    outer = outer_values("gy", levels, PACKED_SPEED, mine_ref, other_ref, sides)
    outer = tuple(
        [spread(group, v[0], 0), spread(group, v[0], 1), spread(group, v[0], 3),
         spread(group, v[1], 1), spread(group, v[0], 2)]
        for v in outer
    )
    outer = step_down(group // 2 == 0, [s1_ref[n] for n in range(11)], outer, SPEED_OF)
    outer_l, outer_r = step_down(group % 2 == 0, [s0_ref[n] for n in range(11)], outer, SPEED_OF)
    solved = [
        [
            yown_ref[f, j] + yleft_ref[SPEED_OF[f], j] * outer_l[f] + yright_ref[SPEED_OF[f], j] * outer_r[f]
            for f in range(5)
        ]
        for j in range(steps)
    ]
    for c in range(chunks):
        wave = []
        for f in range(5):
            value = None
            for g in range(GROUPS):
                y = c * GROUPS + g
                piece = solved[y % steps][f]
                shift = (g - y // steps) * NZ % LANES
                piece = pltpu.roll(piece, shift, 1) if shift else piece
                value = piece if g == 0 else jnp.where(group == g, piece, value)
            wave.append(value)
        q = [flow_ref[f, :, c * LANES : (c + 1) * LANES] for f in range(5)]
        inverse, vel_u, vel_v, vel_w, kinetic, pressure, sound = primitives(q)
        dp = 0.5 * (wave[0] + wave[4])
        dv = (wave[4] - wave[0]) / (2.0 * q[0] * sound)
        dr = (wave[1] + dp) / (sound * sound)
        du, dw = wave[2], wave[3]
        energy = (
            kinetic * dr + q[0] * (vel_u * du + vel_v * dv + vel_w * dw) + dp * (1.0 / (GAMMA - 1.0))
        )
        result = [dr, vel_u * dr + q[0] * du, vel_v * dr + q[0] * dv, vel_w * dr + q[0] * dw, energy]
        for f in range(5):
            out_ref[f, :, c * LANES : (c + 1) * LANES] = result[f]


def call(kernel, name, args, outs, scratch=()):
    vmem = pl.BlockSpec(memory_space=pltpu.VMEM)
    return pl.pallas_call(
        kernel,
        out_shape=[jax.ShapeDtypeStruct(shape, jnp.float32) for shape in outs],
        in_specs=[vmem] * len(args),
        out_specs=[vmem] * len(outs),
        scratch_shapes=[pltpu.VMEM(shape, jnp.float32) for shape in scratch],
        compiler_params=pltpu.CompilerParams(vmem_limit_bytes=16 * 1024 * 1024),
        name=name,
    )(*args)


def pairs_at(count, level):
    return [(i, i ^ (1 << level)) for i in range(count)]


def pairs_far(count):
    steps = [(i, i + 1) for i in range(1, count - 1, 2)]
    return steps + [(b, a) for a, b in steps]


def levels_of(count):
    levels = count.bit_length() - 1
    assert count == 1 << levels and levels >= 1
    return levels


def edges(codes, axis):
    at, count = lax.axis_index(axis), lax.axis_size(axis)
    start = (at == 0).astype(jnp.float32)
    end = (at == count - 1).astype(jnp.float32)
    ones = jnp.ones_like(codes[0], jnp.float32)
    is_one = (codes == 1).astype(jnp.float32)
    return jnp.stack([(1.0 - start) * ones, start * is_one[0], (1.0 - end) * ones, end * is_one[1]])


def local(flow, x_codes, y_codes):
    cells = flow.shape[1]
    columns = flow.shape[2]
    chunks = columns // LANES
    count_x, count_y = lax.axis_size("gx"), lax.axis_size("gy")
    levels_x, levels_y = levels_of(count_x), levels_of(count_y)
    tile_x, tile_y = (chunks, LANES), (cells, LANES)

    qx, near, far, one, two = call(
        pack_kernel, "pack", [flow],
        [(5, cells * chunks, LANES), (5,) + tile_x, (5,) + tile_x, (5,) + tile_y, (5,) + tile_y],
    )
    one = lax.ppermute(one, "gy", pairs_at(count_y, 0))
    two = lax.ppermute(two, "gy", pairs_far(count_y))
    far = lax.ppermute(far, "gx", pairs_far(count_x))
    near = lax.ppermute(near, "gx", pairs_at(count_x, 0))

    codes_x = jnp.broadcast_to(x_codes[:, :, None], x_codes.shape + (NZ,)).reshape((2,) + tile_x)
    edge_x = edges(codes_x, "gx")
    lane_group = lax.broadcasted_iota(jnp.int32, (4,) + tile_y, 2) // NZ
    edge_y = edges(jnp.broadcast_to(y_codes[:, :, None], (2,) + tile_y), "gy")
    side = lax.broadcasted_iota(jnp.int32, (4,) + tile_y, 0)
    inner = jnp.where(side < 2, lane_group != 0, lane_group != GROUPS - 1)
    edge_y = jnp.where(inner, jnp.where(side % 2 == 0, 1.0, 0.0), edge_y)

    rows, own, left, right = call(
        x_kernel, "xsweep", [flow, qx, near, far, one, two, edge_x],
        [(ROWS,) + tile_x, (5, cells) + tile_x, (3, cells) + tile_x, (3, cells) + tile_x],
        [(7,) + tile_y, (7,) + tile_y],
    )
    sides = []
    for level in range(levels_x - 1):
        other = lax.ppermute(rows, "gx", pairs_at(count_x, level))
        final = level == levels_x - 2
        rows, side_rows = call(
            functools.partial(merge_kernel, "gx", level, final, SPEED_OF), f"xmerge{level}",
            [rows, other], [(8 if final else ROWS,) + tile_x, (11,) + tile_x],
        )
        sides.append(side_rows)
    other = lax.ppermute(rows, "gx", pairs_at(count_x, levels_x - 1))
    packed, yown, yleft, yright, side_0, side_1 = call(
        functools.partial(y_kernel, levels_x), "ysweep",
        [flow, qx, one, two, edge_y, own, left, right, rows, other] + sides,
        [(8,) + tile_y, (5, chunks) + tile_y, (3, chunks) + tile_y, (3, chunks) + tile_y,
         (11,) + tile_y, (11,) + tile_y],
        [(7, cells * chunks, LANES)],
    )
    sides = []
    for level in range(levels_y - 1):
        other = lax.ppermute(packed, "gy", pairs_at(count_y, level))
        final = level == levels_y - 2
        packed, side_rows = call(
            functools.partial(merge_kernel, "gy", level, final, PACKED_SPEED), f"ymerge{level}",
            [packed, other], [(3 if final else 8,) + tile_y, (4,) + tile_y],
        )
        sides.append(side_rows)
    other = lax.ppermute(packed, "gy", pairs_at(count_y, levels_y - 1))
    (result,) = call(
        functools.partial(final_kernel, levels_y), "final",
        [flow, yown, yleft, yright, side_0, side_1, packed, other] + sides,
        [(5, cells, columns)],
    )
    return result


def solution(mesh):
    in_specs = (P(None, "gx", "gy"), P(None, "gy"), P(None, "gx"))
    out_specs = P(None, "gx", "gy")
    return jax.shard_map(local, mesh=mesh, in_specs=in_specs, out_specs=out_specs, check_vma=False)
```

time: 155 us -> 34.3 us (0.22); the launches traced: 152 us -> 34.2 us
  other arithmetic: 65.2 us -> 0.2 us
  waiting for transfers between devices: 28.4 us -> 11.3 us
  local copies, waits for them, and re-layouts: 19.6 us -> 2.77 us
  between operations: 15.8 us -> 0.18 us
  blocking collectives: 13.6 us -> 0 us
  starting transfers between devices: 8.47 us -> 17.5 us
  Pallas kernels: 0 us -> 2.16 us
    dynamic_update_slice x48 -> x0, other arithmetic: 46.6 us -> none  [thomas_rows(): lax.scan(forward_step, (nothing, nothing), (lower_band, main_band, upper_...]
    all_gather x1 -> x0, waiting for transfers between devices: 22.7 us -> none  [gathered_join(): everything = lax.all_gather(stacked, 'gx', axis=0, tiled=True)]
    all_gather x1 -> x0, blocking collectives: 13.6 us -> none  [gathered_join(): everything = lax.all_gather(stacked, 'gy', axis=0, tiled=True)]
    ppermute x4 -> x9, starting transfers between devices: 8.47 us -> 17.5 us  [the longest x2 5.51 us: local(): other = lax.ppermute(rows, 'gx', pairs_at(count_x, level))]
    another operation x59 -> x4, local copies, waits for them, and re-layouts: 8.38 us -> 0.16 us  [edges(): jnp.stack([(1.0 - start) * ones, start * is_one[0], (1.0 - end) * ones, e...]
    add x21 -> x0, other arithmetic: 7.42 us -> none  [the longest x12 4.67 us: assemble(): piece_u + piece_p * first_value + piece_q * last_value]
    sub x17 -> x0, other arithmetic: 6.66 us -> none  [the longest x10 4.89 us: reduce_segment(): forward_value - uppers[back_at] * later_value]
    ppermute x4 -> x9, waiting for transfers between devices: 5.63 us -> 11.3 us  [the longest x2 4.07 us: local(): other = lax.ppermute(rows, 'gx', pairs_at(count_x, level))]
  transfers between devices with their start and end apart: 5 -> 9, of which waited for: 3 -> 5; matrix products, arithmetic and copies ran while one was open for 4% -> 2% of each run, Pallas kernels for 0% -> 0%
where the time goes in v1:
time: 34.3 us; the launch traced here: 34.2 us
  starting transfers between devices  17.5 us (51%)
  waiting for transfers between devices  11.3 us (33%)
  local copies, waits for them, and re-layouts  2.77 us (8%)
  Pallas kernels  2.16 us (6%)
    ppermute x2, starting transfers between devices, local(): other = lax.ppermute(rows, 'gx', pairs_at(count_x, level))  5.51 us
    ppermute x1, starting transfers between devices, local(): other = lax.ppermute(packed, 'gy', pairs_at(count_y, level))  4.46 us
    ppermute x2, waiting for transfers between devices, local(): other = lax.ppermute(rows, 'gx', pairs_at(count_x, level))  4.07 us
    ppermute x1, waiting for transfers between devices, local(): other = lax.ppermute(packed, 'gy', pairs_at(count_y, levels_y - 1))  3.13 us
    ppermute x1, starting transfers between devices, local(): one = lax.ppermute(one, 'gy', pairs_at(count_y, 0))  3.12 us
    ppermute x1, waiting for transfers between devices, local(): other = lax.ppermute(rows, 'gx', pairs_at(count_x, levels_x - 1))  2.24 us
    unnamed x8, local copies, waits for them, and re-layouts  2.19 us
    pallas_call x7, Pallas kernels, call(): pl.pallas_call(kernel, out_shape=[jax.ShapeDtypeStruct(shape, jnp.float32...  2.16 us
  transfers between devices with their start and end apart: 9, of which 5 were waited for; matrix products, arithmetic and copies ran while one was open for 2% of the time, Pallas kernels for 0%

profile of v1, /device:TPU:0, one launch (start us, length us, event | category | flops | bytes accessed | tf_op | source)
XLA Modules:
  0.0 34.2 jit_solution(4500890653057677923)
XLA Ops:
  0.0 0.9 %copy-done = f32[5,8,1024]{2,1,0:T(8,128)S(1)} copy-done((f32[5,8,1024]{2,1,0:T(8,128)S(1)}, f32[5,8,1024]{2,1,0:T(8,128)}, u32[]{:S(2)}) %copy-start) | copy-done | bytes 163864
  1.0 3.1 %collective-permute-start = (f32[5,8,128]{2,1,0:T(8,128)S(1)}, f32[5,8,128]{2,1,0:T(8,128)S(1)}, u32[]{:S(2)}, u32[]{:S(2)}) collective-permute-start(f32[5,8,128]{2,1,0:T(8,128)S(1)} %get-tuple-element.27), channel_id=1, source_target_pairs={{0,1},{1,0},{2,3},{3,2},{4,5},{5,4},{6,7},{7,6},{8,9},{9,8},{10,11... | collective-permute-start | bytes 61448 | tf_op jit(solution)/shard_map/ppermute | solution.py:501
  4.1 0.7 %collective-permute-start.1 = (f32[5,8,128]{2,1,0:T(8,128)S(1)}, f32[5,8,128]{2,1,0:T(8,128)S(1)}, u32[]{:S(2)}, u32[]{:S(2)}) collective-permute-start(f32[5,8,128]{2,1,0:T(8,128)S(1)} %get-tuple-element.28), channel_id=1, source_target_pairs={{1,2},{2,1},{5,6},{6,5},{9,10},{10,9},{13,14},{14,13},{17,18},{18,... | collective-permute-start | bytes 61448 | tf_op jit(solution)/shard_map/ppermute | solution.py:502
  4.8 0.7 %collective-permute-start.3 = (f32[5,8,128]{2,1,0:T(8,128)S(1)}, f32[5,8,128]{2,1,0:T(8,128)S(1)}, u32[]{:S(2)}, u32[]{:S(2)}) collective-permute-start(f32[5,8,128]{2,1,0:T(8,128)S(1)} %get-tuple-element.30), channel_id=1, source_target_pairs={{4,8},{12,16},{20,24},{8,4},{16,12},{24,20},{5,9},{13,17},{21,25},... | collective-permute-start | bytes 61448 | tf_op jit(solution)/shard_map/ppermute | solution.py:503
  5.5 0.1 pad.2.clone
  5.6 0.6 %copy-done.2 = s32[2,32]{1,0:T(2,128)S(1)} copy-done((s32[2,32]{1,0:T(2,128)S(1)}, s32[2,32]{1,0:T(2,128)}, u32[]{:S(2)}) %copy-start.2) | copy-done | bytes 280
  6.2 0.7 %copy-done.3 = s32[2,8]{1,0:T(2,128)S(1)} copy-done((s32[2,8]{1,0:T(2,128)S(1)}, s32[2,8]{1,0:T(2,128)}, u32[]{:S(2)}) %copy-start.3) | copy-done | bytes 88
  7.1 0.1 mul.65
  7.2 0.1 pad_maximum_fusion.edge_ref
  7.3 0.1 pad.6.clone
  7.4 0.4 %xsweep.1 = (f32[22,8,128]{2,1,0:T(8,128)S(1)}, f32[5,8,8,128]{3,2,1,0:T(8,128)S(1)}, f32[3,8,8,128]{3,2,1,0:T(8,128)S(1)}, f32[3,8,8,128]{3,2,1,0:T(8,128)S(1)}) custom-call(f32[5,8,1024]{2,1,0:T(8,128)S(1)} %copy-done.1, f32[5,64,128]{2,1,0:T(8,128)S(1)} %get-tuple-element.26.qx_ref.refs_1_, f32[5,8,128]{2,1,0:T(8,128)S(1)} %collective-permute-done.2.near_ref, ...), custom_call_target="tpu_custom_call" | custom-call | tf_op jit(solution)/shard_map/xsweep/pallas_call | solution.py:454
  7.9 3.1 %collective-permute-start.4 = (f32[22,8,128]{2,1,0:T(8,128)S(1)}, f32[22,8,128]{2,1,0:T(8,128)S(1)}, u32[]{:S(2)}, u32[]{:S(2)}) collective-permute-start(f32[22,8,128]{2,1,0:T(8,128)S(1)} %get-tuple-element.34.own_ref), channel_id=1, source_target_pairs={{0,4},{4,0},{8,12},{12,8},{16,20},{20,16},{24,28},{28,24},{1,5},{5... | collective-permute-start | bytes 270344 | tf_op jit(solution)/shard_map/ppermute | solution.py:521
  10.9 0.9 %collective-permute-done.4.other_ref = f32[22,8,128]{2,1,0:T(8,128)S(1)} collective-permute-done((f32[22,8,128]{2,1,0:T(8,128)S(1)}, f32[22,8,128]{2,1,0:T(8,128)S(1)}, u32[]{:S(2)}, u32[]{:S(2)}) %collective-permute-start.4) | collective-permute-done | bytes 90144 | tf_op jit(solution)/shard_map/ppermute | solution.py:521
  11.9 2.5 %collective-permute-start.5 = (f32[22,8,128]{2,1,0:T(8,128)S(1)}, f32[22,8,128]{2,1,0:T(8,128)S(1)}, u32[]{:S(2)}, u32[]{:S(2)}) collective-permute-start(f32[22,8,128]{2,1,0:T(8,128)S(1)} %get-tuple-element.35.own_ref), channel_id=1, source_target_pairs={{0,8},{4,12},{8,0},{12,4},{16,24},{20,28},{24,16},{28,20},{1,9},{5... | collective-permute-start | bytes 270344 | tf_op jit(solution)/shard_map/ppermute | solution.py:521
  14.4 3.1 %collective-permute-done.5.other_ref = f32[22,8,128]{2,1,0:T(8,128)S(1)} collective-permute-done((f32[22,8,128]{2,1,0:T(8,128)S(1)}, f32[22,8,128]{2,1,0:T(8,128)S(1)}, u32[]{:S(2)}, u32[]{:S(2)}) %collective-permute-start.5) | collective-permute-done | bytes 90144 | tf_op jit(solution)/shard_map/ppermute | solution.py:521
  17.5 1.5 %collective-permute-start.6 = (f32[8,8,128]{2,1,0:T(8,128)S(1)}, f32[8,8,128]{2,1,0:T(8,128)S(1)}, u32[]{:S(2)}, u32[]{:S(2)}) collective-permute-start(f32[8,8,128]{2,1,0:T(8,128)S(1)} %get-tuple-element.36.refs_8_), channel_id=1, source_target_pairs={{0,16},{4,20},{8,24},{12,28},{16,0},{20,4},{24,8},{28,12},{1,17},{... | collective-permute-start | bytes 98312 | tf_op jit(solution)/shard_map/ppermute | solution.py:528
  19.2 0.1 maximum_select_fusion.refs_4_
  19.3 2.2 %collective-permute-done.6.refs_9_ = f32[8,8,128]{2,1,0:T(8,128)S(1)} collective-permute-done((f32[8,8,128]{2,1,0:T(8,128)S(1)}, f32[8,8,128]{2,1,0:T(8,128)S(1)}, u32[]{:S(2)}, u32[]{:S(2)}) %collective-permute-start.6) | collective-permute-done | bytes 32800 | tf_op jit(solution)/shard_map/ppermute | solution.py:528
  21.5 0.6 %ysweep.1 = (f32[8,8,128]{2,1,0:T(8,128)S(1)}, f32[5,8,8,128]{3,2,1,0:T(8,128)S(1)}, f32[3,8,8,128]{3,2,1,0:T(8,128)S(1)}, f32[3,8,8,128]{3,2,1,0:T(8,128)S(1)},...) custom-call(f32[5,8,1024]{2,1,0:T(8,128)S(1)} %copy-done.1, f32[5,64,128]{2,1,0:T(8,128)S(1)} %get-tuple-element.26.qx_ref.refs_1_, ...), custom_call_target="tpu_custom_call" | custom-call | tf_op jit(solution)/shard_map/ysweep/pallas_call | solution.py:454
  22.1 4.5 %collective-permute-start.7 = (f32[8,8,128]{2,1,0:T(8,128)S(1)}, f32[8,8,128]{2,1,0:T(8,128)S(1)}, u32[]{:S(2)}, u32[]{:S(2)}) collective-permute-start(f32[8,8,128]{2,1,0:T(8,128)S(1)} %get-tuple-element.44.own_ref), channel_id=1, source_target_pairs={{0,1},{1,0},{2,3},{3,2},{4,5},{5,4},{6,7},{7,6},{8,9},{9,8},{10,11... | collective-permute-start | bytes 98312 | tf_op jit(solution)/shard_map/ppermute | solution.py:538
  26.6 1.9 %collective-permute-done.7.other_ref = f32[8,8,128]{2,1,0:T(8,128)S(1)} collective-permute-done((f32[8,8,128]{2,1,0:T(8,128)S(1)}, f32[8,8,128]{2,1,0:T(8,128)S(1)}, u32[]{:S(2)}, u32[]{:S(2)}) %collective-permute-start.7) | collective-permute-done | bytes 32800 | tf_op jit(solution)/shard_map/ppermute | solution.py:538
  28.5 1.5 %collective-permute-start.8 = (f32[3,8,128]{2,1,0:T(8,128)S(1)}, f32[3,8,128]{2,1,0:T(8,128)S(1)}, u32[]{:S(2)}, u32[]{:S(2)}) collective-permute-start(f32[3,8,128]{2,1,0:T(8,128)S(1)} %get-tuple-element.45.refs_6_), channel_id=1, source_target_pairs={{0,2},{1,3},{2,0},{3,1},{4,6},{5,7},{6,4},{7,5},{8,10},{9,11},{10,... | collective-permute-start | bytes 36872 | tf_op jit(solution)/shard_map/ppermute | solution.py:545
  30.0 3.1 %collective-permute-done.8.refs_7_ = f32[3,8,128]{2,1,0:T(8,128)S(1)} collective-permute-done((f32[3,8,128]{2,1,0:T(8,128)S(1)}, f32[3,8,128]{2,1,0:T(8,128)S(1)}, u32[]{:S(2)}, u32[]{:S(2)}) %collective-permute-start.8) | collective-permute-done | bytes 12320 | tf_op jit(solution)/shard_map/ppermute | solution.py:545
  33.1 1.0 %final.1 = f32[5,8,1024]{2,1,0:T(8,128)} custom-call(f32[5,8,1024]{2,1,0:T(8,128)S(1)} %copy-done.1, f32[5,8,8,128]{3,2,1,0:T(8,128)S(1)} %get-tuple-element.39.refs_1_, f32[3,8,8,128]{3,2,1,0:T(8,128)S(1)} %get-tuple-element.40.refs_2_, f32[3,8,8,128]{3,2,1,0:T(8,128)S(1)} %get-tuple-element.41.refs_3_, f32[11,8,128]{2,1,0:T(8,128)S(1)} %get-tuple-element.42.refs_4_, ...), custom_call_target="tpu_custom_call" | custom-call | tf_op jit(solution)/shard_map/final/pallas_call | solution.py:454
  (29 shorter events, 0.6 us)
Async XLA Ops:
  0.0 0.9 %copy-start = (f32[5,8,1024]{2,1,0:T(8,128)S(1)}, f32[5,8,1024]{2,1,0:T(8,128)}, u32[]{:S(2)}) copy-start(f32[5,8,1024]{2,1,0:T(8,128)} %refs_0_.3) | copy-start | bytes 491524
  0.9 6.5 %copy-start.1 = (f32[5,8,1024]{2,1,0:T(8,128)S(1)}, f32[5,8,1024]{2,1,0:T(8,128)}, u32[]{:S(2)}) copy-start(f32[5,8,1024]{2,1,0:T(8,128)} %refs_0_.3) | copy-start | bytes 491524
  1.0 6.4 %collective-permute-start = (f32[5,8,128]{2,1,0:T(8,128)S(1)}, f32[5,8,128]{2,1,0:T(8,128)S(1)}, u32[]{:S(2)}, u32[]{:S(2)}) collective-permute-start(f32[5,8,128]{2,1,0:T(8,128)S(1)} %get-tuple-element.27), channel_id=1, source_target_pairs={{0,1},{1,0},{2,3},{3,2},{4,5},{5,4},{6,7},{7,6},{8,9},{9,8},{10,11... | collective-permute-start | bytes 61448 | tf_op jit(solution)/shard_map/ppermute | solution.py:501
  4.1 3.3 %collective-permute-start.1 = (f32[5,8,128]{2,1,0:T(8,128)S(1)}, f32[5,8,128]{2,1,0:T(8,128)S(1)}, u32[]{:S(2)}, u32[]{:S(2)}) collective-permute-start(f32[5,8,128]{2,1,0:T(8,128)S(1)} %get-tuple-element.28), channel_id=1, source_target_pairs={{1,2},{2,1},{5,6},{6,5},{9,10},{10,9},{13,14},{14,13},{17,18},{18,... | collective-permute-start | bytes 61448 | tf_op jit(solution)/shard_map/ppermute | solution.py:502
  4.7 2.7 %collective-permute-start.2 = (f32[5,8,128]{2,1,0:T(8,128)S(1)}, f32[5,8,128]{2,1,0:T(8,128)S(1)}, u32[]{:S(2)}, u32[]{:S(2)}) collective-permute-start(f32[5,8,128]{2,1,0:T(8,128)S(1)} %get-tuple-element.29), channel_id=1, source_target_pairs={{0,4},{4,0},{8,12},{12,8},{16,20},{20,16},{24,28},{28,24},{1,5},{5... | collective-permute-start | bytes 61448 | tf_op jit(solution)/shard_map/ppermute | solution.py:504
  4.8 2.6 %collective-permute-start.3 = (f32[5,8,128]{2,1,0:T(8,128)S(1)}, f32[5,8,128]{2,1,0:T(8,128)S(1)}, u32[]{:S(2)}, u32[]{:S(2)}) collective-permute-start(f32[5,8,128]{2,1,0:T(8,128)S(1)} %get-tuple-element.30), channel_id=1, source_target_pairs={{4,8},{12,16},{20,24},{8,4},{16,12},{24,20},{5,9},{13,17},{21,25},... | collective-permute-start | bytes 61448 | tf_op jit(solution)/shard_map/ppermute | solution.py:503
  5.5 0.7 %copy-start.2 = (s32[2,32]{1,0:T(2,128)S(1)}, s32[2,32]{1,0:T(2,128)}, u32[]{:S(2)}) copy-start(s32[2,32]{1,0:T(2,128)} %param.4) | copy-start | bytes 772
  6.2 0.7 %copy-start.3 = (s32[2,8]{1,0:T(2,128)S(1)}, s32[2,8]{1,0:T(2,128)}, u32[]{:S(2)}) copy-start(s32[2,8]{1,0:T(2,128)} %param.5) | copy-start | bytes 196
  7.9 4.0 %collective-permute-start.4 = (f32[22,8,128]{2,1,0:T(8,128)S(1)}, f32[22,8,128]{2,1,0:T(8,128)S(1)}, u32[]{:S(2)}, u32[]{:S(2)}) collective-permute-start(f32[22,8,128]{2,1,0:T(8,128)S(1)} %get-tuple-element.34.own_ref), channel_id=1, source_target_pairs={{0,4},{4,0},{8,12},{12,8},{16,20},{20,16},{24,28},{28,24},{1,5},{5... | collective-permute-start | bytes 270344 | tf_op jit(solution)/shard_map/ppermute | solution.py:521
  11.9 5.6 %collective-permute-start.5 = (f32[22,8,128]{2,1,0:T(8,128)S(1)}, f32[22,8,128]{2,1,0:T(8,128)S(1)}, u32[]{:S(2)}, u32[]{:S(2)}) collective-permute-start(f32[22,8,128]{2,1,0:T(8,128)S(1)} %get-tuple-element.35.own_ref), channel_id=1, source_target_pairs={{0,8},{4,12},{8,0},{12,4},{16,24},{20,28},{24,16},{28,20},{1,9},{5... | collective-permute-start | bytes 270344 | tf_op jit(solution)/shard_map/ppermute | solution.py:521
  17.5 4.0 %collective-permute-start.6 = (f32[8,8,128]{2,1,0:T(8,128)S(1)}, f32[8,8,128]{2,1,0:T(8,128)S(1)}, u32[]{:S(2)}, u32[]{:S(2)}) collective-permute-start(f32[8,8,128]{2,1,0:T(8,128)S(1)} %get-tuple-element.36.refs_8_), channel_id=1, source_target_pairs={{0,16},{4,20},{8,24},{12,28},{16,0},{20,4},{24,8},{28,12},{1,17},{... | collective-permute-start | bytes 98312 | tf_op jit(solution)/shard_map/ppermute | solution.py:528
  22.1 6.4 %collective-permute-start.7 = (f32[8,8,128]{2,1,0:T(8,128)S(1)}, f32[8,8,128]{2,1,0:T(8,128)S(1)}, u32[]{:S(2)}, u32[]{:S(2)}) collective-permute-start(f32[8,8,128]{2,1,0:T(8,128)S(1)} %get-tuple-element.44.own_ref), channel_id=1, source_target_pairs={{0,1},{1,0},{2,3},{3,2},{4,5},{5,4},{6,7},{7,6},{8,9},{9,8},{10,11... | collective-permute-start | bytes 98312 | tf_op jit(solution)/shard_map/ppermute | solution.py:538
  28.5 4.7 %collective-permute-start.8 = (f32[3,8,128]{2,1,0:T(8,128)S(1)}, f32[3,8,128]{2,1,0:T(8,128)S(1)}, u32[]{:S(2)}, u32[]{:S(2)}) collective-permute-start(f32[3,8,128]{2,1,0:T(8,128)S(1)} %get-tuple-element.45.refs_6_), channel_id=1, source_target_pairs={{0,2},{1,3},{2,0},{3,1},{4,6},{5,7},{6,4},{7,5},{8,10},{9,11},{10,... | collective-permute-start | bytes 36872 | tf_op jit(solution)/shard_map/ppermute | solution.py:545

commit v2 on v1

v2 whole, which is shorter than its diff:
```python
import functools

import jax
import jax.numpy as jnp
from jax import lax
from jax.experimental import pallas as pl
from jax.experimental.pallas import tpu as pltpu
from jax.sharding import PartitionSpec as P

NZ = 32
GAMMA = 1.4
SIGMA = 0.5
DIFFUSE = 400.0
LANES = 128
GROUPS = LANES // NZ
SPEED_OF = (0, 1, 1, 1, 2)
COEFS = 12


def primitives(q):
    inverse = 1.0 / q[0]
    vel_u, vel_v, vel_w = q[1] * inverse, q[2] * inverse, q[3] * inverse
    kinetic = 0.5 * (vel_u * vel_u + vel_v * vel_v + vel_w * vel_w)
    pressure = (GAMMA - 1.0) * (q[4] - q[0] * kinetic)
    sound = jnp.sqrt(GAMMA * pressure * inverse)
    return inverse, vel_u, vel_v, vel_w, kinetic, pressure, sound


def flux_of(q, normal, speed, pressure):
    return [q[normal]] + [
        q[f] * speed + pressure if f == normal else q[f] * speed for f in (1, 2, 3)
    ] + [speed * (q[4] + pressure)]


def three_speeds(velocity, sound):
    return (velocity - sound, velocity, velocity + sound)


def x_characteristics(res, density, prim):
    inverse, vel_u, vel_v, vel_w, kinetic, pressure, sound = prim
    du = (res[1] - vel_u * res[0]) * inverse
    dv = (res[2] - vel_v * res[0]) * inverse
    dw = (res[3] - vel_w * res[0]) * inverse
    dp = (GAMMA - 1.0) * (
        res[4] - vel_u * res[1] - vel_v * res[2] - vel_w * res[3] + kinetic * res[0]
    )
    normal = density * sound * du
    return [dp - normal, sound * sound * res[0] - dp, dv, dw, dp + normal]


def factor(speeds, first, last, forced=False):
    cells = len(speeds) - 2
    inverses, lowers, ups, lefts = [], [], [], []
    for i in range(cells):
        parts = []
        for k in range(3):
            lower = -0.5 * SIGMA * speeds[i][k] - DIFFUSE
            upper = 0.5 * SIGMA * speeds[i + 2][k] - DIFFUSE
            main = 1.0 + 2.0 * DIFFUSE
            if i == 0:
                main = main + lower * first[1]
                lower = None if forced else lower * first[0]
            if i == cells - 1:
                main = main + upper * last[1]
                upper = None if forced else upper * last[0]
            pivot = main if i == 0 else main - lower * ups[-1][k]
            inverse = 1.0 / pivot
            scaled = -inverse if lower is None else lower * inverse
            left = -scaled if i == 0 else -scaled * lefts[-1][k]
            parts.append((inverse, scaled, -inverse if upper is None else upper * inverse, left))
        for out, values in zip((inverses, lowers, ups, lefts), zip(*parts)):
            out.append(list(values))
    rights = [None] * cells
    rights[-1] = [-u for u in ups[-1]]
    for i in range(cells - 2, -1, -1):
        lefts[i] = [lefts[i][k] - ups[i][k] * lefts[i + 1][k] for k in range(3)]
        rights[i] = [-ups[i][k] * rights[i + 1][k] for k in range(3)]
    return inverses, lowers, ups, lefts, rights


def substitute(inverses, lowers, ups, sources):
    cells = len(sources)
    owns = []
    for i in range(cells):
        own = [sources[i][f] * inverses[i][SPEED_OF[f]] for f in range(5)]
        if i:
            own = [own[f] - lowers[i][SPEED_OF[f]] * owns[-1][f] for f in range(5)]
        owns.append(own)
    for i in range(cells - 2, -1, -1):
        owns[i] = [owns[i][f] - ups[i][SPEED_OF[f]] * owns[i + 1][f] for f in range(5)]
    return owns


def unpack(rows, fields=5, speeds=3):
    out, at = [], 0
    for n in (fields, fields, speeds, speeds, speeds, speeds):
        out.append(rows[at : at + n])
        at += n
    return out


def join(before, after, speed_of):
    fields = len(speed_of)
    a_f, a_e, b_f, c_f, b_e, c_e = before
    speeds = len(b_f)
    a_g, a_h, b_g, c_g, b_h, c_h = after
    inv = [1.0 / (1.0 - c_e[k] * b_g[k]) for k in range(speeds)]
    e_1 = [b_e[k] * inv[k] for k in range(speeds)]
    f_2 = [c_g[k] * inv[k] for k in range(speeds)]
    e_2 = [c_e[k] * f_2[k] for k in range(speeds)]
    f_1 = [b_g[k] * e_1[k] for k in range(speeds)]
    e_0 = [(a_e[f] + c_e[speed_of[f]] * a_g[f]) * inv[speed_of[f]] for f in range(fields)]
    f_0 = [(a_g[f] + b_g[speed_of[f]] * a_e[f]) * inv[speed_of[f]] for f in range(fields)]
    joined = (
        [a_f[f] + c_f[speed_of[f]] * f_0[f] for f in range(fields)]
        + [a_h[f] + b_h[speed_of[f]] * e_0[f] for f in range(fields)]
        + [b_f[k] + c_f[k] * f_1[k] for k in range(speeds)]
        + [c_f[k] * f_2[k] for k in range(speeds)]
        + [b_h[k] * e_1[k] for k in range(speeds)]
        + [c_h[k] + b_h[k] * e_2[k] for k in range(speeds)]
    )
    return joined, e_0 + e_1 + e_2, f_0 + f_1 + f_2


def merge(low, own, other, speed_of):
    fields = len(speed_of)
    speeds = max(speed_of) + 1
    before = [jnp.where(low, a, b) for a, b in zip(own, other)]
    after = [jnp.where(low, b, a) for a, b in zip(own, other)]
    joined, e, f = join(unpack(before, fields, speeds), unpack(after, fields, speeds), speed_of)
    return joined, [jnp.where(low, b, a) for a, b in zip(e, f)]


def facing(low, rows, fields=5, speeds=3):
    a_f, a_e, b_f, c_f, b_e, c_e = unpack(rows, fields, speeds)
    return [jnp.where(low, e, f) for e, f in zip(a_e + c_e, a_f + b_f)]


def join_factors(q_before, q_after):
    prim_b, prim_a = primitives(q_before), primitives(q_after)
    flux_b = flux_of(q_before, 1, prim_b[1], prim_b[5])
    flux_a = flux_of(q_after, 1, prim_a[1], prim_a[5])
    change = [-0.5 * SIGMA * (a - b) for a, b in zip(flux_a, flux_b)]
    smooth = [DIFFUSE * (a - b) for a, b in zip(q_after, q_before)]
    h_b = x_characteristics([c + d for c, d in zip(change, smooth)], q_before[0], prim_b)
    h_a = x_characteristics([c - d for c, d in zip(change, smooth)], q_after[0], prim_a)
    u_b = [DIFFUSE - 0.5 * SIGMA * v for v in three_speeds(prim_a[1], prim_a[6])]
    l_a = [DIFFUSE + 0.5 * SIGMA * v for v in three_speeds(prim_b[1], prim_b[6])]
    return h_b, u_b, h_a, l_a


def merge_forced(low, own, other):
    before = [jnp.where(low, a, b) for a, b in zip(own, other)]
    after = [jnp.where(low, b, a) for a, b in zip(own, other)]
    q_before, q_after = before[-5:], after[-10:-5]
    h_b, u_b, h_a, l_a = join_factors(q_before, q_after)
    a_f, a_e, b_f, c_f, b_e, c_e = unpack(before)
    a_g, a_h, b_g, c_g, b_h, c_h = unpack(after)
    a_f, a_e = ([a[f] + c[SPEED_OF[f]] * h_b[f] for f in range(5)] for a, c in ((a_f, c_f), (a_e, c_e)))
    a_g, a_h = ([a[f] + b[SPEED_OF[f]] * h_a[f] for f in range(5)] for a, b in ((a_g, b_g), (a_h, b_h)))
    c_f, c_e = ([c[k] * u_b[k] for k in range(3)] for c in (c_f, c_e))
    b_g, b_h = ([b[k] * l_a[k] for k in range(3)] for b in (b_g, b_h))
    joined, e, f = join(
        (a_f, a_e, b_f, c_f, b_e, c_e), (a_g, a_h, b_g, c_g, b_h, c_h), SPEED_OF
    )
    to_low = [h_b[n] + u_b[SPEED_OF[n]] * f[n] for n in range(5)]
    to_low += [u_b[k] * f[5 + 3 * t + k] for t in range(2) for k in range(3)]
    to_high = [h_a[n] + l_a[SPEED_OF[n]] * e[n] for n in range(5)]
    to_high += [l_a[k] * e[5 + 3 * t + k] for t in range(2) for k in range(3)]
    return joined, [jnp.where(low, a, b) for a, b in zip(to_low, to_high)]


def merge_factors(low, own, other):
    before = [jnp.where(low, a, b) for a, b in zip(own, other)]
    after = [jnp.where(low, b, a) for a, b in zip(own, other)]
    prim_b, prim_a = (primitives(q) for q in (before[-5:], after[-10:-5]))
    u_b = [DIFFUSE - 0.5 * SIGMA * v for v in three_speeds(prim_a[1], prim_a[6])]
    l_a = [DIFFUSE + 0.5 * SIGMA * v for v in three_speeds(prim_b[1], prim_b[6])]
    b_f, c_f, b_e, c_e = (before[3 * n : 3 * n + 3] for n in range(4))
    b_g, c_g, b_h, c_h = (after[3 * n : 3 * n + 3] for n in range(4))
    c_f, c_e = ([c[k] * u_b[k] for k in range(3)] for c in (c_f, c_e))
    b_g, b_h = ([b[k] * l_a[k] for k in range(3)] for b in (b_g, b_h))
    joined, _, _ = join(([], [], b_f, c_f, b_e, c_e), ([], [], b_g, c_g, b_h, c_h), ())
    return joined, before[-10:-5], after[-5:]


def last_join(low, own, other, speed_of):
    fields = len(speed_of)
    result = []
    for f in range(fields):
        k = fields + speed_of[f]
        result.append((other[f] + other[k] * own[f]) / (1.0 - own[k] * other[k]))
    return result


def last_join_forced(low, own, other):
    before = [jnp.where(low, a, b) for a, b in zip(own, other)]
    after = [jnp.where(low, b, a) for a, b in zip(own, other)]
    h_b, u_b, h_a, l_a = join_factors(before[8:], after[8:])
    h_own = [jnp.where(low, a, b) for a, b in zip(h_b, h_a)]
    h_other = [jnp.where(low, b, a) for a, b in zip(h_b, h_a)]
    k_own = [jnp.where(low, a, b) for a, b in zip(u_b, l_a)]
    k_other = [jnp.where(low, b, a) for a, b in zip(u_b, l_a)]
    mine, theirs = [], []
    for rows, h, k, out in ((own, h_own, k_own, mine), (other, h_other, k_other, theirs)):
        out.extend(rows[f] + rows[5 + SPEED_OF[f]] * h[f] for f in range(5))
        out.extend(rows[5 + n] * k[n] for n in range(3))
    value = last_join(low, mine, theirs, SPEED_OF)
    return [h_own[f] + k_own[SPEED_OF[f]] * value[f] for f in range(5)]


def step_down(low, side, outer, speed_of):
    fields = len(speed_of)
    speeds = max(speed_of) + 1
    left, right = outer
    new = [
        side[f] + side[fields + speed_of[f]] * left[f] + side[fields + speeds + speed_of[f]] * right[f]
        for f in range(fields)
    ]
    return (
        [jnp.where(low, a, b) for a, b in zip(left, new)],
        [jnp.where(low, b, a) for a, b in zip(right, new)],
    )


def from_last(low, new):
    zero = jnp.zeros_like(new[0])
    return [jnp.where(low, zero, x) for x in new], [jnp.where(low, x, zero) for x in new]


def bit_low(axis, level):
    return (lax.axis_index(axis) >> level) % 2 == 0


def x_edges(codes_ref, shape):
    at, count = lax.axis_index("gx"), lax.axis_size("gx")
    lane = lax.broadcasted_iota(jnp.int32, shape, 1)
    sub = lax.broadcasted_iota(jnp.int32, shape, 0)
    width = codes_ref.shape[1]
    result = []
    place = lax.broadcasted_iota(jnp.int32, (shape[0], width), 1)
    row = lax.broadcasted_iota(jnp.int32, (shape[0], width), 0)
    for side, outer in ((0, at == 0), (1, at == count - 1)):
        codes = jnp.broadcast_to(codes_ref[side : side + 1, :], (shape[0], width))
        is_one = jnp.where(codes == 1, 1.0, 0.0)
        value = jnp.zeros(shape, jnp.float32)
        for g in range(GROUPS):
            mine = jnp.where(place == row * GROUPS + g, is_one, 0.0)
            column = jnp.sum(mine, axis=1, keepdims=True)
            value = jnp.where(lane // NZ == g, column, value)
        result.append(jnp.where(outer, value, 0.0))
    return result


def y_edges(codes_ref, shape):
    at, count = lax.axis_index("gy"), lax.axis_size("gy")
    group = lax.broadcasted_iota(jnp.int32, shape, 1) // NZ
    cells = shape[0]
    result = []
    place = lax.broadcasted_iota(jnp.int32, (cells, cells), 1)
    row = lax.broadcasted_iota(jnp.int32, (cells, cells), 0)
    for side, outer, face in ((0, at == 0, 0), (1, at == count - 1, GROUPS - 1)):
        codes = jnp.broadcast_to(codes_ref[side : side + 1, :], (cells, cells))
        mine = jnp.where(jnp.logical_and(codes == 1, place == row), 1.0, 0.0)
        value = jnp.broadcast_to(jnp.sum(mine, axis=1, keepdims=True), shape)
        at_face = jnp.logical_and(outer, group == face)
        result.append((jnp.where(at_face, 0.0, 1.0), jnp.where(at_face, value, 0.0)))
    return result


def pack_kernel(flow_ref, qx_ref, one_ref, two_ref):
    cells = flow_ref.shape[1]
    chunks = flow_ref.shape[2] // LANES
    even = bit_low("gx", 0)
    for f in range(5):
        down = flow_ref[f, :, 0:LANES]
        up = flow_ref[f, :, (chunks - 1) * LANES : chunks * LANES]
        one_ref[f] = jnp.where(even, up, down)
        two_ref[f] = jnp.where(even, down, up)
        for c in range(chunks):
            qx_ref[f, pl.ds(c, cells, stride=chunks), :] = flow_ref[f, :, c * LANES : (c + 1) * LANES]


def y_halos(flow_ref, one_ref, two_ref, f):
    chunks = flow_ref.shape[2] // LANES
    at, count = lax.axis_index("gy"), lax.axis_size("gy")
    even = bit_low("gx", 0)
    low = jnp.where(even, one_ref[f], two_ref[f])
    high = jnp.where(even, two_ref[f], one_ref[f])
    own_low = pltpu.roll(flow_ref[f, :, 0:LANES], LANES - NZ, 1)
    own_high = pltpu.roll(flow_ref[f, :, (chunks - 1) * LANES : chunks * LANES], NZ, 1)
    return jnp.where(at == 0, own_low, low), jnp.where(at == count - 1, own_high, high)


def x_factor_kernel(qx_ref, codes_ref, out_ref, inverse_ref, lower_ref, up_ref, left_ref, right_ref):
    cells = inverse_ref.shape[0]
    chunks = inverse_ref.shape[2]
    rows = [[qx_ref[f, i * chunks : (i + 1) * chunks, :] for f in range(5)] for i in range(cells)]
    speeds = []
    for q in rows:
        prim = primitives(q)
        speeds.append(three_speeds(prim[1], prim[6]))
    neumann = x_edges(codes_ref, (chunks, LANES))
    parts = factor(
        speeds[:1] + speeds + speeds[-1:], (None, neumann[0]), (None, neumann[1]), forced=True
    )
    for ref, values in zip((inverse_ref, lower_ref, up_ref, left_ref, right_ref), parts):
        for i in range(cells):
            store(ref.at[i], values[i])
    lefts, rights = parts[3:]
    store(out_ref, lefts[0] + rights[0] + lefts[-1] + rights[-1] + rows[0] + rows[-1])


def x_source_kernel(qx_ref, out_ref):
    cells = out_ref.shape[0]
    chunks = out_ref.shape[2]
    lane = lax.broadcasted_iota(jnp.int32, (chunks, LANES), 1)
    sub = lax.broadcasted_iota(jnp.int32, (chunks, LANES), 0)
    z_of = lane % NZ
    rows = [[qx_ref[f, i * chunks : (i + 1) * chunks, :] for f in range(5)] for i in range(cells)]
    prims = [primitives(q) for q in rows]
    fluxes = [flux_of(q, 1, p[1], p[5]) for q, p in zip(rows, prims)]
    rows, fluxes = (v[:1] + v + v[-1:] for v in (rows, fluxes))
    up_edge = jnp.logical_and(sub == chunks - 1, lane >= LANES - NZ)
    down_edge = jnp.logical_and(sub == 0, lane < NZ)

    def y_next(value):
        turned = pltpu.roll(value, LANES - NZ, 1)
        turned = jnp.where(lane >= LANES - NZ, pltpu.roll(turned, chunks - 1, 0), turned)
        return jnp.where(up_edge, value, turned)

    def y_before(value):
        turned = pltpu.roll(value, NZ, 1)
        turned = jnp.where(lane < NZ, pltpu.roll(turned, 1, 0), turned)
        return jnp.where(down_edge, value, turned)

    def z_change(value):
        after = jnp.where(z_of == NZ - 1, pltpu.roll(value, NZ - 1, 1), pltpu.roll(value, LANES - 1, 1))
        before = jnp.where(z_of == 0, pltpu.roll(value, LANES - NZ + 1, 1), pltpu.roll(value, 1, 1))
        return after - before

    for i in range(cells):
        q = rows[i + 1]
        inverse, vel_u, vel_v, vel_w, kinetic, pressure, sound = prims[i]
        after = [y_next(v) for v in list(q) + [vel_v, pressure]]
        before = [y_before(v) for v in list(q) + [vel_v, pressure]]
        flux_after = flux_of(after, 2, after[5], after[6])
        flux_before = flux_of(before, 2, before[5], before[6])
        flux_z = flux_of(q, 3, vel_w, pressure)
        res = []
        for f in range(5):
            change = (
                (fluxes[i + 2][f] - fluxes[i][f])
                + (flux_after[f] - flux_before[f])
                + z_change(flux_z[f])
            )
            smooth = rows[i + 2][f] + rows[i][f] + after[f] + before[f] - 4.0 * q[f]
            res.append(-0.5 * SIGMA * change + DIFFUSE * smooth)
        store(out_ref.at[i], x_characteristics(res, q[0], prims[i]))


def x_kernel(
    flow_ref, one_ref, two_ref, source_ref, inverse_ref, lower_ref, up_ref,
    rows_ref, own_ref, low_ref, high_ref,
):
    cells = flow_ref.shape[1]
    chunks = flow_ref.shape[2] // LANES
    lane = lax.broadcasted_iota(jnp.int32, (chunks, LANES), 1)
    sub = lax.broadcasted_iota(jnp.int32, (chunks, LANES), 0)
    up_edge = jnp.logical_and(sub == chunks - 1, lane >= LANES - NZ)
    down_edge = jnp.logical_and(sub == 0, lane < NZ)
    lows, highs = zip(*[y_halos(flow_ref, one_ref, two_ref, f) for f in range(5)])
    for ghosts, at, turn, sign, ref in (
        (lows, 0, NZ, 1.0, low_ref), (highs, chunks - 1, LANES - NZ, -1.0, high_ref)
    ):
        ghosts = [pltpu.roll(g, turn, 1) for g in ghosts]
        inner = [flow_ref[f, :, at * LANES : (at + 1) * LANES] for f in range(5)]
        ghost_prim, prim = primitives(ghosts), primitives(inner)
        ghost_flux = flux_of(ghosts, 2, ghost_prim[2], ghost_prim[5])
        inner_flux = flux_of(inner, 2, prim[2], prim[5])
        res = [
            sign * 0.5 * SIGMA * (ghost_flux[f] - inner_flux[f]) + DIFFUSE * (ghosts[f] - inner[f])
            for f in range(5)
        ]
        store(ref, x_characteristics(res, inner[0], prim))
    sources = []
    for i in range(cells):
        source = []
        for f in range(5):
            low = jnp.broadcast_to(low_ref[f, i : i + 1, :], (chunks, LANES))
            high = jnp.broadcast_to(high_ref[f, i : i + 1, :], (chunks, LANES))
            extra = jnp.where(down_edge, low, 0.0) + jnp.where(up_edge, high, 0.0)
            source.append(source_ref[i, f] + extra)
        sources.append(source)
    owns = substitute(*([load(ref.at[i]) for i in range(cells)] for ref in (inverse_ref, lower_ref, up_ref)), sources)
    for i in range(cells):
        store(own_ref.at[i], owns[i])
    store(rows_ref, owns[0] + owns[-1])


def load(ref):
    return [ref[n] for n in range(ref.shape[0])]


def store(ref, values):
    for n, value in enumerate(values):
        ref[n] = value


def x_merge_factor_kernel(level, final, own_ref, other_ref, out_ref):
    joined, q_first, q_last = merge_factors(bit_low("gx", level), load(own_ref), load(other_ref))
    if final:
        low = bit_low("gx", level + 1)
        b_f, c_f, b_e, c_e = (joined[3 * n : 3 * n + 3] for n in range(4))
        pairs = list(zip(c_e, b_f)) + list(zip(q_last, q_first))
        store(out_ref, [jnp.where(low, e, f) for e, f in pairs])
    else:
        store(out_ref, joined + q_first + q_last)


def x_merge_kernel(level, final, own_ref, other_ref, own_factor_ref, other_factor_ref, out_ref, side_ref):
    joined, side = merge_forced(
        bit_low("gx", level), load(own_ref) + load(own_factor_ref), load(other_ref) + load(other_factor_ref)
    )
    a_f, a_e = joined[:5], joined[5:10]
    if final:
        low = bit_low("gx", level + 1)
        store(out_ref, [jnp.where(low, e, f) for e, f in zip(a_e, a_f)])
    else:
        store(out_ref, a_f + a_e)
    store(side_ref, side)


def y_merge_kernel(level, final, own_ref, other_ref, out_ref, side_ref):
    joined, side = merge(bit_low("gy", level), load(own_ref), load(other_ref), PACKED_SPEED)
    if final:
        joined = facing(bit_low("gy", level + 1), joined, 2, 1)
    store(out_ref, joined)
    store(side_ref, side)


def outer_values(axis, levels, speed_of, own, other, side_refs):
    low = bit_low(axis, levels - 1)
    if axis == "gx":
        new = last_join_forced(low, own, other)
    else:
        new = last_join(low, own, other, speed_of)
    outer = from_last(low, new)
    for level in range(levels - 2, -1, -1):
        outer = step_down(bit_low(axis, level), load(side_refs[level]), outer, speed_of)
    return outer


PACKED_SPEED = (0, 0)


def regroup(parts, group):
    steps = len(parts)
    result = []
    for jj in range(steps):
        value = None
        for s in range(GROUPS):
            y = s * steps + jj
            piece = parts[y // GROUPS]
            shift = (s - y % GROUPS) * NZ % LANES
            piece = pltpu.roll(piece, shift, 1) if shift else piece
            value = piece if s == 0 else jnp.where(group == s, piece, value)
        result.append(value)
    return result


def lane_partner(values, group, level):
    if level == 0:
        return [
            jnp.where(group % 2 == 0, pltpu.roll(v, LANES - NZ, 1), pltpu.roll(v, NZ, 1)) for v in values
        ]
    return [pltpu.roll(v, LANES // 2, 1) for v in values]


def lane_low(group, level):
    return (group // 2 ** level) % 2 == 0


def y_factor_kernel(
    flow_ref, one_ref, two_ref, codes_ref,
    packed_ref, inverse_ref, lower_ref, up_ref, left_ref, right_ref, join_ref, side_ref,
):
    cells = flow_ref.shape[1]
    chunks = flow_ref.shape[2] // LANES
    lane = lax.broadcasted_iota(jnp.int32, (cells, LANES), 1)
    group = lane // NZ
    vels, sounds = [], []
    for c in range(chunks):
        prim = primitives([flow_ref[f, :, c * LANES : (c + 1) * LANES] for f in range(5)])
        vels.append(prim[2])
        sounds.append(prim[6])
    speeds = [three_speeds(v, c) for v, c in zip(regroup(vels, group), regroup(sounds, group))]
    lows, highs = zip(*[y_halos(flow_ref, one_ref, two_ref, f) for f in range(5)])
    low_prim, high_prim = primitives(lows), primitives(highs)
    low_speed = three_speeds(low_prim[2], low_prim[6])
    high_speed = three_speeds(high_prim[2], high_prim[6])
    before = tuple(
        pltpu.roll(jnp.where(group == GROUPS - 1, low_speed[k], speeds[-1][k]), NZ, 1) for k in range(3)
    )
    after = tuple(
        pltpu.roll(jnp.where(group == 0, high_speed[k], speeds[0][k]), LANES - NZ, 1) for k in range(3)
    )
    parts = factor([before] + speeds + [after], *y_edges(codes_ref, (cells, LANES)))
    for ref, values in zip((inverse_ref, lower_ref, up_ref, left_ref, right_ref), parts):
        for i in range(chunks):
            store(ref.at[i], values[i])
    lefts, rights = parts[3:]
    ends = lefts[0] + rights[0] + lefts[-1] + rights[-1]
    for level in range(2):
        low = lane_low(group, level)
        other = lane_partner(ends, group, level)
        before = [jnp.where(low, a, b) for a, b in zip(ends, other)]
        after = [jnp.where(low, b, a) for a, b in zip(ends, other)]
        b_f, c_f, b_e, c_e = (before[3 * n : 3 * n + 3] for n in range(4))
        b_g, c_g, b_h, c_h = (after[3 * n : 3 * n + 3] for n in range(4))
        inv = [1.0 / (1.0 - c_e[k] * b_g[k]) for k in range(3)]
        store(join_ref.at[level], inv + c_e + b_g + c_f + b_h)
        ends, e, f = join(([], [], b_f, c_f, b_e, c_e), ([], [], b_g, c_g, b_h, c_h), ())
        store(side_ref.at[level], [jnp.where(low, b, a) for a, b in zip(e, f)])
    store(packed_ref, [four(group, t[0], t[1], t[2], t[1]) for t in (ends[3 * n : 3 * n + 3] for n in range(4))])


def y_kernel(levels, *refs):
    (qx_ref, own_ref, left_ref, right_ref, mine_ref, other_ref, mine_factor_ref, other_factor_ref,
     packed_ref, inverse_ref, lower_ref, up_ref, join_ref) = refs[:13]
    sides = refs[13 : 13 + levels - 1]
    out_ref, yown_ref, side_ref, turn_ref = refs[13 + levels - 1 :]
    chunks = qx_ref.shape[1] // own_ref.shape[0]
    cells = own_ref.shape[0]
    steps = chunks
    mine, other = load(mine_ref) + load(mine_factor_ref), load(other_ref) + load(other_factor_ref)
    outer_l, outer_r = outer_values("gx", levels, SPEED_OF, mine, other, sides)
    for i in range(cells):
        q = [qx_ref[f, i * chunks : (i + 1) * chunks, :] for f in range(5)]
        sound = primitives(q)[6]
        wave = [
            own_ref[i, f] + left_ref[i, SPEED_OF[f]] * outer_l[f] + right_ref[i, SPEED_OF[f]] * outer_r[f]
            for f in range(5)
        ]
        impedance = q[0] * sound
        squared = sound * sound
        dp = 0.5 * (wave[0] + wave[4])
        du = (wave[4] - wave[0]) / (2.0 * impedance)
        dr = (wave[1] + dp) / squared
        normal = impedance * wave[2]
        values = [dp - normal, squared * dr - dp, du, wave[3], dp + normal]
        for n, value in enumerate(values):
            turn_ref[n, i * chunks : (i + 1) * chunks, :] = value
    lane = lax.broadcasted_iota(jnp.int32, (cells, LANES), 1)
    group = lane // NZ
    fields = [
        regroup([turn_ref[n, pl.ds(c, cells, stride=chunks), :] for c in range(chunks)], group)
        for n in range(5)
    ]
    sources = [[fields[f][jj] for f in range(5)] for jj in range(steps)]
    owns = substitute(*([load(ref.at[i]) for i in range(steps)] for ref in (inverse_ref, lower_ref, up_ref)), sources)
    for i in range(steps):
        store(yown_ref.at[i], owns[i])
    a_f, a_e = owns[0], owns[-1]
    for level in range(2):
        low = lane_low(group, level)
        other = lane_partner(a_f + a_e, group, level)
        parts = load(join_ref.at[level])
        inv, c_e, b_g, c_f, b_h = (parts[3 * n : 3 * n + 3] for n in range(5))
        before = [jnp.where(low, a, b) for a, b in zip(a_f + a_e, other)]
        after = [jnp.where(low, b, a) for a, b in zip(a_f + a_e, other)]
        e, f, new_f, new_e = [], [], [], []
        for n in range(5):
            k = SPEED_OF[n]
            e.append((before[5 + n] + c_e[k] * after[n]) * inv[k])
            f.append((after[n] + b_g[k] * before[5 + n]) * inv[k])
            new_f.append(before[n] + c_f[k] * f[n])
            new_e.append(after[5 + n] + b_h[k] * e[n])
        a_f, a_e = new_f, new_e
        store(side_ref.at[level], [jnp.where(low, b, a) for a, b in zip(e, f)])
    rows = []
    for a in (a_f, a_e):
        rows += [four(group, a[0], a[1], a[4], a[2]), a[3]]
    store(out_ref, rows + load(packed_ref))


def four(group, a, b, c, d):
    return jnp.where(group == 0, a, jnp.where(group == 1, b, jnp.where(group == 2, c, d)))


def spread(group, value, source):
    half = jnp.where(group // 2 == source // 2, value, pltpu.roll(value, LANES // 2, 1))
    down, up = pltpu.roll(half, NZ, 1), pltpu.roll(half, LANES - NZ, 1)
    if source % 2 == 0:
        return jnp.where(group % 2 == 0, half, down)
    return jnp.where(group % 2 == 1, half, up)


def final_kernel(levels, *refs):
    (flow_ref, yown_ref, yleft_ref, yright_ref, ends_ref, side_ref, mine_ref, other_ref) = refs[:8]
    sides = refs[8 : 8 + levels - 1]
    out_hbm, out_ref, sems = refs[8 + levels - 1 :]
    cells = flow_ref.shape[1]
    chunks = flow_ref.shape[2] // LANES
    steps = chunks
    lane = lax.broadcasted_iota(jnp.int32, (cells, LANES), 1)
    group = lane // NZ
    outer = outer_values("gy", levels, PACKED_SPEED, load(mine_ref), load(other_ref), sides)
    outer = tuple(
        [spread(group, v[0], 0), spread(group, v[0], 1), spread(group, v[0], 3),
         spread(group, v[1], 1), spread(group, v[0], 2)]
        for v in outer
    )
    for level in (1, 0):
        side = load(ends_ref.at[level]) + load(side_ref.at[level])
        outer = step_down(lane_low(group, level), side, outer, SPEED_OF)
    outer_l, outer_r = outer
    solved = [
        [
            yown_ref[j, f] + yleft_ref[j, SPEED_OF[f]] * outer_l[f] + yright_ref[j, SPEED_OF[f]] * outer_r[f]
            for f in range(5)
        ]
        for j in range(steps)
    ]
    copies = []
    for c in range(chunks):
        wave = []
        for f in range(5):
            value = None
            for g in range(GROUPS):
                y = c * GROUPS + g
                piece = solved[y % steps][f]
                shift = (g - y // steps) * NZ % LANES
                piece = pltpu.roll(piece, shift, 1) if shift else piece
                value = piece if g == 0 else jnp.where(group == g, piece, value)
            wave.append(value)
        q = [flow_ref[f, :, c * LANES : (c + 1) * LANES] for f in range(5)]
        inverse, vel_u, vel_v, vel_w, kinetic, pressure, sound = primitives(q)
        dp = 0.5 * (wave[0] + wave[4])
        dv = (wave[4] - wave[0]) / (2.0 * q[0] * sound)
        dr = (wave[1] + dp) / (sound * sound)
        du, dw = wave[2], wave[3]
        energy = (
            kinetic * dr + q[0] * (vel_u * du + vel_v * dv + vel_w * dw) + dp * (1.0 / (GAMMA - 1.0))
        )
        result = [dr, vel_u * dr + q[0] * du, vel_v * dr + q[0] * dv, vel_w * dr + q[0] * dw, energy]
        for f in range(5):
            out_ref[f, :, c * LANES : (c + 1) * LANES] = result[f]
        part = (slice(None), slice(None), slice(c * LANES, (c + 1) * LANES))
        copies.append(pltpu.make_async_copy(out_ref.at[part], out_hbm.at[part], sems.at[c]))
        copies[-1].start()
    for copy in copies:
        copy.wait()


def call(kernel, name, args, outs, scratch=(), out_hbm=False):
    vmem, hbm = (pl.BlockSpec(memory_space=space) for space in (pltpu.VMEM, pltpu.HBM))
    return pl.pallas_call(
        kernel,
        out_shape=[jax.ShapeDtypeStruct(shape, jnp.float32) for shape in outs],
        in_specs=[vmem] * len(args),
        out_specs=[hbm if out_hbm else vmem] * len(outs),
        scratch_shapes=list(scratch),
        compiler_params=pltpu.CompilerParams(vmem_limit_bytes=16 * 1024 * 1024),
        name=name,
    )(*args)


def pairs_at(count, level):
    return [(i, i ^ (1 << level)) for i in range(count)]


def pairs_across(count, level):
    return [(i, i ^ (1 << level) ^ (1 if level else 0)) for i in range(count)]


def snake(count_x, count_y):
    pairs = []
    for x in range(count_x):
        for y in range(count_y):
            to = y + 1 if x % 2 == 0 else y - 1
            inside = 0 <= to < count_y
            pairs.append((x * count_y + y, x * count_y + to if inside else (x ^ 1) * count_y + y))
    return pairs


def levels_of(count):
    levels = count.bit_length() - 1
    assert count == 1 << levels and levels >= 2
    return levels


def local(flow, x_codes, y_codes):
    cells = flow.shape[1]
    columns = flow.shape[2]
    chunks = columns // LANES
    count_x, count_y = lax.axis_size("gx"), lax.axis_size("gy")
    levels_x, levels_y = levels_of(count_x), levels_of(count_y)
    tile_x, tile_y = (chunks, LANES), (cells, LANES)

    qx, one, two = call(
        pack_kernel, "pack", [flow], [(5, cells * chunks, LANES), (5,) + tile_y, (5,) + tile_y]
    )
    round_trip = snake(count_x, count_y)
    one = lax.ppermute(one, ("gx", "gy"), round_trip)
    two = lax.ppermute(two, ("gx", "gy"), [(b, a) for a, b in round_trip])

    factors, inverse, lower, upper, left, right = call(
        x_factor_kernel, "xfactor", [qx, x_codes], [(COEFS + 10,) + tile_x] + [(cells, 3) + tile_x] * 5
    )
    (source,) = call(x_source_kernel, "xsource", [qx], [(cells, 5) + tile_x])
    all_factors = []
    for level in range(levels_x):
        other = lax.ppermute(factors, "gx", pairs_across(count_x, level))
        all_factors.append((factors, other))
        if level < levels_x - 1:
            final = level == levels_x - 2
            (factors,) = call(
                functools.partial(x_merge_factor_kernel, level, final), f"xfactor{level}",
                [factors, other], [(8 if final else COEFS + 10,) + tile_x],
            )
    rows, own = call(
        x_kernel, "xsweep", [flow, one, two, source, inverse, lower, upper],
        [(10,) + tile_x, (cells, 5) + tile_x],
        [pltpu.VMEM((5,) + tile_y, jnp.float32), pltpu.VMEM((5,) + tile_y, jnp.float32)],
    )
    sides = []
    for level in range(levels_x - 1):
        other = lax.ppermute(rows, "gx", pairs_across(count_x, level))
        final = level == levels_x - 2
        rows, side_rows = call(
            functools.partial(x_merge_kernel, level, final), f"xmerge{level}",
            [rows, other, *all_factors[level]], [(5 if final else 10,) + tile_x, (11,) + tile_x],
        )
        sides.append(side_rows)
    other = lax.ppermute(rows, "gx", pairs_across(count_x, levels_x - 1))
    y_factors, yinverse, ylower, yup, yleft, yright, yjoin, yside = call(
        y_factor_kernel, "yfactor", [flow, one, two, y_codes],
        [(4,) + tile_y] + [(chunks, 3) + tile_y] * 5 + [(2, 15) + tile_y, (2, 6) + tile_y],
    )
    packed, yown, yends = call(
        functools.partial(y_kernel, levels_x), "ysweep",
        [qx, own, left, right, rows, other, *all_factors[-1], y_factors, yinverse, ylower, yup, yjoin] + sides,
        [(8,) + tile_y, (chunks, 5) + tile_y, (2, 5) + tile_y],
        [pltpu.VMEM((5, cells * chunks, LANES), jnp.float32)],
    )
    sides = []
    for level in range(levels_y - 1):
        other = lax.ppermute(packed, "gy", pairs_at(count_y, level))
        final = level == levels_y - 2
        packed, side_rows = call(
            functools.partial(y_merge_kernel, level, final), f"ymerge{level}",
            [packed, other], [(3 if final else 8,) + tile_y, (4,) + tile_y],
        )
        sides.append(side_rows)
    other = lax.ppermute(packed, "gy", pairs_at(count_y, levels_y - 1))
    (result,) = call(
        functools.partial(final_kernel, levels_y), "final",
        [flow, yown, yleft, yright, yends, yside, packed, other] + sides,
        [(5, cells, columns)],
        [pltpu.VMEM((5, cells, columns), jnp.float32), pltpu.SemaphoreType.DMA((chunks,))],
        out_hbm=True,
    )
    return result


def solution(mesh):
    in_specs = (P(None, "gx", "gy"), P(None, "gy"), P(None, "gx"))
    out_specs = P(None, "gx", "gy")
    return jax.shard_map(local, mesh=mesh, in_specs=in_specs, out_specs=out_specs, check_vma=False)
```

time: 34.3 us -> 27.7 us (0.81)
  starting transfers between devices: 17.5 us -> 13.3 us
  waiting for transfers between devices: 11.3 us -> 9.48 us
  local copies, waits for them, and re-layouts: 2.77 us -> 1.6 us
  Pallas kernels: 2.16 us -> 3.03 us
    ppermute x1, starting transfers between devices: 4.46 us -> 1.64 us  [local(): other = lax.ppermute(packed, 'gy', pairs_at(count_y, level))]
    ppermute x7 -> x8, starting transfers between devices: 11.5 us -> 8.96 us  [the longest x3 3.62 us: local(): other = lax.ppermute(factors, 'gx', pairs_across(count_x, level))]
    ppermute x7 -> x8, waiting for transfers between devices: 6.32 us -> 5.14 us  [the longest x2 1.87 us: local(): other = lax.ppermute(rows, 'gx', pairs_across(count_x, level))]
    ppermute x1, starting transfers between devices: 1.53 us -> 2.65 us  [local(): other = lax.ppermute(packed, 'gy', pairs_at(count_y, levels_y - 1))]
    ppermute x1, waiting for transfers between devices: 3.13 us -> 2 us  [local(): other = lax.ppermute(packed, 'gy', pairs_at(count_y, levels_y - 1))]
    pallas_call x7 -> x12, Pallas kernels: 2.16 us -> 3.03 us  [call(): pl.pallas_call(kernel, out_shape=[jax.ShapeDtypeStruct(shape, jnp.float32...]
    unnamed x8, local copies, waits for them, and re-layouts: 2.19 us -> 1.6 us
    ppermute x1, waiting for transfers between devices: 1.89 us -> 2.34 us  [local(): other = lax.ppermute(packed, 'gy', pairs_at(count_y, level))]
  transfers between devices with their start and end apart: 9 -> 10, of which waited for: 5 -> 6; matrix products, arithmetic and copies ran while one was open for 2% -> 0% of each run, Pallas kernels for 0% -> 5%
where the time goes in v2:
time: 27.7 us; the launch traced here: 27.5 us
  starting transfers between devices  13.3 us (48%)
  waiting for transfers between devices  9.48 us (34%)
  Pallas kernels  3.03 us (11%)
  local copies, waits for them, and re-layouts  1.6 us (6%)
    ppermute x3, starting transfers between devices, local(): other = lax.ppermute(factors, 'gx', pairs_across(count_x, level))  3.62 us
    pallas_call x12, Pallas kernels, call(): pl.pallas_call(kernel, out_shape=[jax.ShapeDtypeStruct(shape, jnp.float32...  3.03 us
    ppermute x1, starting transfers between devices, local(): other = lax.ppermute(packed, 'gy', pairs_at(count_y, levels_y - 1))  2.65 us
    ppermute x1, starting transfers between devices, local(): one = lax.ppermute(one, ('gx', 'gy'), round_trip)  2.59 us
    ppermute x1, waiting for transfers between devices, local(): other = lax.ppermute(packed, 'gy', pairs_at(count_y, level))  2.34 us
    ppermute x1, waiting for transfers between devices, local(): other = lax.ppermute(packed, 'gy', pairs_at(count_y, levels_y - 1))  2 us
    ppermute x2, waiting for transfers between devices, local(): other = lax.ppermute(rows, 'gx', pairs_across(count_x, level))  1.87 us
    ppermute x1, waiting for transfers between devices, local(): two = lax.ppermute(two, ('gx', 'gy'), [(b, a) for a, b in round_trip])  1.81 us
  transfers between devices with their start and end apart: 10, of which 6 were waited for; matrix products, arithmetic and copies ran while one was open for 0% of the time, Pallas kernels for 5%

profile of v2, /device:TPU:0, one launch (start us, length us, event | category | flops | bytes accessed | tf_op | source)
XLA Modules:
  0.0 27.5 jit_solution(3395756186559506988)
XLA Ops:
  0.0 0.9 %copy-done = f32[5,8,1024]{2,1,0:T(8,128)S(1)} copy-done((f32[5,8,1024]{2,1,0:T(8,128)S(1)}, f32[5,8,1024]{2,1,0:T(8,128)}, u32[]{:S(2)}) %copy-start) | copy-done | bytes 163864
  1.0 0.7 %copy-done.2 = s32[2,32]{1,0:T(2,128)S(1)} copy-done((s32[2,32]{1,0:T(2,128)S(1)}, s32[2,32]{1,0:T(2,128)}, u32[]{:S(2)}) %copy-start.2) | copy-done | bytes 280
  1.6 0.2 xfactor.1
  1.8 0.6 %collective-permute-start.3 = (f32[22,8,128]{2,1,0:T(8,128)S(1)}, f32[22,8,128]{2,1,0:T(8,128)S(1)}, u32[]{:S(2)}, u32[]{:S(2)}) collective-permute-start(f32[22,8,128]{2,1,0:T(8,128)S(1)} %get-tuple-element.43.own_factor_ref.own_ref), channel_id=1, source_target_pairs={{0,4},{4,0},{8,12},{12,8},{16,20},{20,16},{24,28},{28,24},{1,5},{5... | collective-permute-start | bytes 270344 | tf_op jit(solution)/shard_map/ppermute | solution.py:714
  2.4 2.6 %collective-permute-start = (f32[5,8,128]{2,1,0:T(8,128)S(1)}, f32[5,8,128]{2,1,0:T(8,128)S(1)}, u32[]{:S(2)}, u32[]{:S(2)}) collective-permute-start(f32[5,8,128]{2,1,0:T(8,128)S(1)} %get-tuple-element.34), channel_id=1, source_target_pairs={{0,1},{1,2},{2,3},{3,7},{4,0},{5,4},{6,5},{7,6},{8,9},{9,10},{10,1... | collective-permute-start | bytes 61448 | tf_op jit(solution)/shard_map/ppermute | solution.py:705
  5.0 1.5 %collective-permute-start.5 = (f32[22,8,128]{2,1,0:T(8,128)S(1)}, f32[22,8,128]{2,1,0:T(8,128)S(1)}, u32[]{:S(2)}, u32[]{:S(2)}) collective-permute-start(f32[22,8,128]{2,1,0:T(8,128)S(1)} %xfactor0.1.own_factor_ref.own_ref), channel_id=1, source_target_pairs={{0,12},{4,8},{8,4},{12,0},{16,28},{20,24},{24,20},{28,16},{1,13},{... | collective-permute-start | bytes 270344 | tf_op jit(solution)/shard_map/ppermute | solution.py:714
  6.6 0.4 %xsource.1.source_ref = f32[8,5,8,128]{3,2,1,0:T(8,128)S(1)} custom-call(f32[5,64,128]{2,1,0:T(8,128)S(1)} %get-tuple-element.33.qx_ref.refs_0_), custom_call_target="tpu_custom_call" | custom-call | tf_op jit(solution)/shard_map/xsource/pallas_call | solution.py:658
  6.9 1.8 %collective-permute-done.1.two_ref = f32[5,8,128]{2,1,0:T(8,128)S(1)} collective-permute-done((f32[5,8,128]{2,1,0:T(8,128)S(1)}, f32[5,8,128]{2,1,0:T(8,128)S(1)}, u32[]{:S(2)}, u32[]{:S(2)}) %collective-permute-start.1) | collective-permute-done | bytes 20512 | tf_op jit(solution)/shard_map/ppermute | solution.py:706
  8.8 0.2 xsweep.1
  9.0 0.1 collective-permute-start.2
  9.1 1.2 %collective-permute-done.2.other_ref = f32[10,8,128]{2,1,0:T(8,128)S(1)} collective-permute-done((f32[10,8,128]{2,1,0:T(8,128)S(1)}, f32[10,8,128]{2,1,0:T(8,128)S(1)}, u32[]{:S(2)}, u32[]{:S(2)}) %collective-permute-start.2) | collective-permute-done | bytes 40992 | tf_op jit(solution)/shard_map/ppermute | solution.py:729
  10.3 1.3 %collective-permute-start.4 = (f32[10,8,128]{2,1,0:T(8,128)S(1)}, f32[10,8,128]{2,1,0:T(8,128)S(1)}, u32[]{:S(2)}, u32[]{:S(2)}) collective-permute-start(f32[10,8,128]{2,1,0:T(8,128)S(1)} %get-tuple-element.44.own_ref), channel_id=1, source_target_pairs={{0,12},{4,8},{8,4},{12,0},{16,28},{20,24},{24,20},{28,16},{1,13},{... | collective-permute-start | bytes 122888 | tf_op jit(solution)/shard_map/ppermute | solution.py:729
  11.7 1.5 %collective-permute-start.7 = (f32[8,8,128]{2,1,0:T(8,128)S(1)}, f32[8,8,128]{2,1,0:T(8,128)S(1)}, u32[]{:S(2)}, u32[]{:S(2)}) collective-permute-start(f32[8,8,128]{2,1,0:T(8,128)S(1)} %xfactor1.1.refs_6_), channel_id=1, source_target_pairs={{0,20},{4,16},{8,28},{12,24},{16,4},{20,0},{24,12},{28,8},{1,21},{... | collective-permute-start | bytes 98312 | tf_op jit(solution)/shard_map/ppermute | solution.py:714
  13.3 0.7 %collective-permute-done.4.other_ref = f32[10,8,128]{2,1,0:T(8,128)S(1)} collective-permute-done((f32[10,8,128]{2,1,0:T(8,128)S(1)}, f32[10,8,128]{2,1,0:T(8,128)S(1)}, u32[]{:S(2)}, u32[]{:S(2)}) %collective-permute-start.4) | collective-permute-done | bytes 40992 | tf_op jit(solution)/shard_map/ppermute | solution.py:729
  13.9 0.1 xmerge1.1
  14.0 1.4 %collective-permute-start.6 = (f32[5,8,128]{2,1,0:T(8,128)S(1)}, f32[5,8,128]{2,1,0:T(8,128)S(1)}, u32[]{:S(2)}, u32[]{:S(2)}) collective-permute-start(f32[5,8,128]{2,1,0:T(8,128)S(1)} %get-tuple-element.45.refs_4_), channel_id=1, source_target_pairs={{0,20},{4,16},{8,28},{12,24},{16,4},{20,0},{24,12},{28,8},{1,21},{... | collective-permute-start | bytes 61448 | tf_op jit(solution)/shard_map/ppermute | solution.py:736
  15.4 0.5 %yfactor.1 = (f32[4,8,128]{2,1,0:T(8,128)S(1)}, f32[8,3,8,128]{3,2,1,0:T(8,128)S(1)}, f32[8,3,8,128]{3,2,1,0:T(8,128)S(1)}, f32[8,3,8,128]{3,2,1,0:T(8,128)S(1)}...) custom-call(f32[5,8,1024]{2,1,0:T(8,128)S(1)} %copy-done.1, ...), custom_call_target="tpu_custom_call" | custom-call | tf_op jit(solution)/shard_map/yfactor/pallas_call | solution.py:658
  15.8 1.5 %collective-permute-done.6.refs_5_ = f32[5,8,128]{2,1,0:T(8,128)S(1)} collective-permute-done((f32[5,8,128]{2,1,0:T(8,128)S(1)}, f32[5,8,128]{2,1,0:T(8,128)S(1)}, u32[]{:S(2)}, u32[]{:S(2)}) %collective-permute-start.6) | collective-permute-done | bytes 20512 | tf_op jit(solution)/shard_map/ppermute | solution.py:736
  17.3 0.5 %ysweep.1 = (f32[8,8,128]{2,1,0:T(8,128)S(1)}, f32[8,5,8,128]{3,2,1,0:T(8,128)S(1)}, f32[2,5,8,128]{3,2,1,0:T(8,128)S(1)}) custom-call(f32[5,64,128]{2,1,0:T(8,128)S(1)} %get-tuple-element.33.qx_ref.refs_0_, f32[8,5,8,128]{3,2,1,0:T(8,128)S(1)} %get-tuple-element.39.refs_1_, f32[8,3,8,128]{3,2,1,0:T(8,128)S(1)} %get-tuple-element.40.refs_2_, ...), custom_call_target="tpu_custom_call" | custom-call | tf_op jit(solution)/shard_map/ysweep/pallas_call | solution.py:658
  17.8 1.6 %collective-permute-start.8 = (f32[8,8,128]{2,1,0:T(8,128)S(1)}, f32[8,8,128]{2,1,0:T(8,128)S(1)}, u32[]{:S(2)}, u32[]{:S(2)}) collective-permute-start(f32[8,8,128]{2,1,0:T(8,128)S(1)} %get-tuple-element.58.own_ref), channel_id=1, source_target_pairs={{0,1},{1,0},{2,3},{3,2},{4,5},{5,4},{6,7},{7,6},{8,9},{9,8},{10,11... | collective-permute-start | bytes 98312 | tf_op jit(solution)/shard_map/ppermute | solution.py:749
  19.4 2.3 %collective-permute-done.8.other_ref = f32[8,8,128]{2,1,0:T(8,128)S(1)} collective-permute-done((f32[8,8,128]{2,1,0:T(8,128)S(1)}, f32[8,8,128]{2,1,0:T(8,128)S(1)}, u32[]{:S(2)}, u32[]{:S(2)}) %collective-permute-start.8) | collective-permute-done | bytes 32800 | tf_op jit(solution)/shard_map/ppermute | solution.py:749
  21.8 2.7 %collective-permute-start.9 = (f32[3,8,128]{2,1,0:T(8,128)S(1)}, f32[3,8,128]{2,1,0:T(8,128)S(1)}, u32[]{:S(2)}, u32[]{:S(2)}) collective-permute-start(f32[3,8,128]{2,1,0:T(8,128)S(1)} %get-tuple-element.59.refs_6_), channel_id=1, source_target_pairs={{0,2},{1,3},{2,0},{3,1},{4,6},{5,7},{6,4},{7,5},{8,10},{9,11},{10,... | collective-permute-start | bytes 36872 | tf_op jit(solution)/shard_map/ppermute | solution.py:756
  24.4 2.0 %collective-permute-done.9.refs_7_ = f32[3,8,128]{2,1,0:T(8,128)S(1)} collective-permute-done((f32[3,8,128]{2,1,0:T(8,128)S(1)}, f32[3,8,128]{2,1,0:T(8,128)S(1)}, u32[]{:S(2)}, u32[]{:S(2)}) %collective-permute-start.9) | collective-permute-done | bytes 12320 | tf_op jit(solution)/shard_map/ppermute | solution.py:756
  26.4 1.0 %final.1 = f32[5,8,1024]{2,1,0:T(8,128)} custom-call(f32[5,8,1024]{2,1,0:T(8,128)S(1)} %copy-done.1, f32[8,5,8,128]{3,2,1,0:T(8,128)S(1)} %get-tuple-element.53.refs_1_, f32[8,3,8,128]{3,2,1,0:T(8,128)S(1)} %get-tuple-element.54.refs_2_, f32[8,3,8,128]{3,2,1,0:T(8,128)S(1)} %get-tuple-element.55.refs_3_, f32[2,5,8,128]{3,2,1,0:T(8,128)S(1)} %get-tuple-element.56.refs_4_, ...), custom_call_target="tpu_custom_call" | custom-call | tf_op jit(solution)/shard_map/final/pallas_call | solution.py:658
  (16 shorter events, 0.2 us)
Async XLA Ops:
  0.0 0.9 %copy-start = (f32[5,8,1024]{2,1,0:T(8,128)S(1)}, f32[5,8,1024]{2,1,0:T(8,128)}, u32[]{:S(2)}) copy-start(f32[5,8,1024]{2,1,0:T(8,128)} %refs_0_.1) | copy-start | bytes 491524
  1.0 0.7 %copy-start.2 = (s32[2,32]{1,0:T(2,128)S(1)}, s32[2,32]{1,0:T(2,128)}, u32[]{:S(2)}) copy-start(s32[2,32]{1,0:T(2,128)} %codes_ref.2) | copy-start | bytes 772
  1.8 3.2 %collective-permute-start.3 = (f32[22,8,128]{2,1,0:T(8,128)S(1)}, f32[22,8,128]{2,1,0:T(8,128)S(1)}, u32[]{:S(2)}, u32[]{:S(2)}) collective-permute-start(f32[22,8,128]{2,1,0:T(8,128)S(1)} %get-tuple-element.43.own_factor_ref.own_ref), channel_id=1, source_target_pairs={{0,4},{4,0},{8,12},{12,8},{16,20},{20,16},{24,28},{28,24},{1,5},{5... | collective-permute-start | bytes 270344 | tf_op jit(solution)/shard_map/ppermute | solution.py:714
  2.4 4.6 %collective-permute-start = (f32[5,8,128]{2,1,0:T(8,128)S(1)}, f32[5,8,128]{2,1,0:T(8,128)S(1)}, u32[]{:S(2)}, u32[]{:S(2)}) collective-permute-start(f32[5,8,128]{2,1,0:T(8,128)S(1)} %get-tuple-element.34), channel_id=1, source_target_pairs={{0,1},{1,2},{2,3},{3,7},{4,0},{5,4},{6,5},{7,6},{8,9},{9,10},{10,1... | collective-permute-start | bytes 61448 | tf_op jit(solution)/shard_map/ppermute | solution.py:705
  5.0 3.8 %collective-permute-start.1 = (f32[5,8,128]{2,1,0:T(8,128)S(1)}, f32[5,8,128]{2,1,0:T(8,128)S(1)}, u32[]{:S(2)}, u32[]{:S(2)}) collective-permute-start(f32[5,8,128]{2,1,0:T(8,128)S(1)} %get-tuple-element.35), channel_id=1, source_target_pairs={{1,0},{2,1},{3,2},{7,3},{0,4},{4,5},{5,6},{6,7},{9,8},{10,9},{11,1... | collective-permute-start | bytes 61448 | tf_op jit(solution)/shard_map/ppermute | solution.py:706
  5.0 3.7 %copy-start.1 = (f32[5,8,1024]{2,1,0:T(8,128)S(1)}, f32[5,8,1024]{2,1,0:T(8,128)}, u32[]{:S(2)}) copy-start(f32[5,8,1024]{2,1,0:T(8,128)} %refs_0_.1) | copy-start | bytes 491524
  5.0 6.6 %collective-permute-start.5 = (f32[22,8,128]{2,1,0:T(8,128)S(1)}, f32[22,8,128]{2,1,0:T(8,128)S(1)}, u32[]{:S(2)}, u32[]{:S(2)}) collective-permute-start(f32[22,8,128]{2,1,0:T(8,128)S(1)} %xfactor0.1.own_factor_ref.own_ref), channel_id=1, source_target_pairs={{0,12},{4,8},{8,4},{12,0},{16,28},{20,24},{24,20},{28,16},{1,13},{... | collective-permute-start | bytes 270344 | tf_op jit(solution)/shard_map/ppermute | solution.py:714
  9.0 1.3 %collective-permute-start.2 = (f32[10,8,128]{2,1,0:T(8,128)S(1)}, f32[10,8,128]{2,1,0:T(8,128)S(1)}, u32[]{:S(2)}, u32[]{:S(2)}) collective-permute-start(f32[10,8,128]{2,1,0:T(8,128)S(1)} %get-tuple-element.42.own_ref), channel_id=1, source_target_pairs={{0,4},{4,0},{8,12},{12,8},{16,20},{20,16},{24,28},{28,24},{1,5},{5... | collective-permute-start | bytes 122888 | tf_op jit(solution)/shard_map/ppermute | solution.py:729
  10.3 3.6 %collective-permute-start.4 = (f32[10,8,128]{2,1,0:T(8,128)S(1)}, f32[10,8,128]{2,1,0:T(8,128)S(1)}, u32[]{:S(2)}, u32[]{:S(2)}) collective-permute-start(f32[10,8,128]{2,1,0:T(8,128)S(1)} %get-tuple-element.44.own_ref), channel_id=1, source_target_pairs={{0,12},{4,8},{8,4},{12,0},{16,28},{20,24},{24,20},{28,16},{1,13},{... | collective-permute-start | bytes 122888 | tf_op jit(solution)/shard_map/ppermute | solution.py:729
  11.7 5.6 %collective-permute-start.7 = (f32[8,8,128]{2,1,0:T(8,128)S(1)}, f32[8,8,128]{2,1,0:T(8,128)S(1)}, u32[]{:S(2)}, u32[]{:S(2)}) collective-permute-start(f32[8,8,128]{2,1,0:T(8,128)S(1)} %xfactor1.1.refs_6_), channel_id=1, source_target_pairs={{0,20},{4,16},{8,28},{12,24},{16,4},{20,0},{24,12},{28,8},{1,21},{... | collective-permute-start | bytes 98312 | tf_op jit(solution)/shard_map/ppermute | solution.py:714
  14.0 1.4 %copy-start.3 = (s32[2,8]{1,0:T(2,128)S(1)}, s32[2,8]{1,0:T(2,128)}, u32[]{:S(2)}) copy-start(s32[2,8]{1,0:T(2,128)} %codes_ref.3) | copy-start | bytes 196
  14.0 3.3 %collective-permute-start.6 = (f32[5,8,128]{2,1,0:T(8,128)S(1)}, f32[5,8,128]{2,1,0:T(8,128)S(1)}, u32[]{:S(2)}, u32[]{:S(2)}) collective-permute-start(f32[5,8,128]{2,1,0:T(8,128)S(1)} %get-tuple-element.45.refs_4_), channel_id=1, source_target_pairs={{0,20},{4,16},{8,28},{12,24},{16,4},{20,0},{24,12},{28,8},{1,21},{... | collective-permute-start | bytes 61448 | tf_op jit(solution)/shard_map/ppermute | solution.py:736
  17.8 4.0 %collective-permute-start.8 = (f32[8,8,128]{2,1,0:T(8,128)S(1)}, f32[8,8,128]{2,1,0:T(8,128)S(1)}, u32[]{:S(2)}, u32[]{:S(2)}) collective-permute-start(f32[8,8,128]{2,1,0:T(8,128)S(1)} %get-tuple-element.58.own_ref), channel_id=1, source_target_pairs={{0,1},{1,0},{2,3},{3,2},{4,5},{5,4},{6,7},{7,6},{8,9},{9,8},{10,11... | collective-permute-start | bytes 98312 | tf_op jit(solution)/shard_map/ppermute | solution.py:749
  21.8 4.7 %collective-permute-start.9 = (f32[3,8,128]{2,1,0:T(8,128)S(1)}, f32[3,8,128]{2,1,0:T(8,128)S(1)}, u32[]{:S(2)}, u32[]{:S(2)}) collective-permute-start(f32[3,8,128]{2,1,0:T(8,128)S(1)} %get-tuple-element.59.refs_6_), channel_id=1, source_target_pairs={{0,2},{1,3},{2,0},{3,1},{4,6},{5,7},{6,4},{7,5},{8,10},{9,11},{10,... | collective-permute-start | bytes 36872 | tf_op jit(solution)/shard_map/ppermute | solution.py:756

commit v3 on v2

--- a/solution.py
+++ b/solution.py
@@ -6,6 +6,7 @@
 from jax.experimental import pallas as pl
 from jax.experimental.pallas import tpu as pltpu
 from jax.sharding import PartitionSpec as P
+
 
 NZ = 32
 GAMMA = 1.4
@@ -37,7 +38,7 @@
 
 
 def x_characteristics(res, density, prim):
-    inverse, vel_u, vel_v, vel_w, kinetic, pressure, sound = prim
+    inverse, vel_u, vel_v, vel_w, kinetic, _, sound = prim
     du = (res[1] - vel_u * res[0]) * inverse
     dv = (res[2] - vel_v * res[0]) * inverse
     dw = (res[3] - vel_w * res[0]) * inverse
@@ -132,7 +133,7 @@
 
 
 def facing(low, rows, fields=5, speeds=3):
-    a_f, a_e, b_f, c_f, b_e, c_e = unpack(rows, fields, speeds)
+    a_f, a_e, b_f, _, _, c_e = unpack(rows, fields, speeds)
     return [jnp.where(low, e, f) for e, f in zip(a_e + c_e, a_f + b_f)]
 
 
@@ -184,7 +185,7 @@
     return joined, before[-10:-5], after[-5:]
 
 
-def last_join(low, own, other, speed_of):
+def last_join(own, other, speed_of):
     fields = len(speed_of)
     result = []
     for f in range(fields):
@@ -205,7 +206,7 @@
     for rows, h, k, out in ((own, h_own, k_own, mine), (other, h_other, k_other, theirs)):
         out.extend(rows[f] + rows[5 + SPEED_OF[f]] * h[f] for f in range(5))
         out.extend(rows[5 + n] * k[n] for n in range(3))
-    value = last_join(low, mine, theirs, SPEED_OF)
+    value = last_join(mine, theirs, SPEED_OF)
     return [h_own[f] + k_own[SPEED_OF[f]] * value[f] for f in range(5)]
 
 
@@ -217,6 +218,8 @@
         side[f] + side[fields + speed_of[f]] * left[f] + side[fields + speeds + speed_of[f]] * right[f]
         for f in range(fields)
     ]
+    if isinstance(low, bool):
+        return (left, new) if low else (new, right)
     return (
         [jnp.where(low, a, b) for a, b in zip(left, new)],
         [jnp.where(low, b, a) for a, b in zip(right, new)],
@@ -268,15 +271,29 @@
     return result
 
 
+def to_group(value, source, target):
+    shift = (target - source) * NZ % LANES
+    return pltpu.roll(value, shift, 1) if shift else value
+
+
 def pack_kernel(flow_ref, qx_ref, one_ref, two_ref):
     cells = flow_ref.shape[1]
     chunks = flow_ref.shape[2] // LANES
     even = bit_low("gx", 0)
+    group = lax.broadcasted_iota(jnp.int32, (cells, LANES), 1) // NZ
+    downs, ups = [], []
     for f in range(5):
-        down = flow_ref[f, :, 0:LANES]
-        up = flow_ref[f, :, (chunks - 1) * LANES : chunks * LANES]
-        one_ref[f] = jnp.where(even, up, down)
-        two_ref[f] = jnp.where(even, down, up)
+        down = to_group(flow_ref[f, :, 0:LANES], 0, f % GROUPS)
+        up = to_group(flow_ref[f, :, (chunks - 1) * LANES : chunks * LANES], GROUPS - 1, f % GROUPS)
+        for rows, value in ((downs, down), (ups, up)):
+            if f % GROUPS:
+                rows[-1] = jnp.where(group == f % GROUPS, value, rows[-1])
+            else:
+                rows.append(value)
+    for n, (down, up) in enumerate(zip(downs, ups)):
+        one_ref[n] = jnp.where(even, up, down)
+        two_ref[n] = jnp.where(even, down, up)
+    for f in range(5):
         for c in range(chunks):
             qx_ref[f, pl.ds(c, cells, stride=chunks), :] = flow_ref[f, :, c * LANES : (c + 1) * LANES]
 
@@ -285,21 +302,28 @@
     chunks = flow_ref.shape[2] // LANES
     at, count = lax.axis_index("gy"), lax.axis_size("gy")
     even = bit_low("gx", 0)
-    low = jnp.where(even, one_ref[f], two_ref[f])
-    high = jnp.where(even, two_ref[f], one_ref[f])
-    own_low = pltpu.roll(flow_ref[f, :, 0:LANES], LANES - NZ, 1)
-    own_high = pltpu.roll(flow_ref[f, :, (chunks - 1) * LANES : chunks * LANES], NZ, 1)
+    low = jnp.where(even, one_ref[f // GROUPS], two_ref[f // GROUPS])
+    high = jnp.where(even, two_ref[f // GROUPS], one_ref[f // GROUPS])
+    low, high = to_group(low, f % GROUPS, GROUPS - 1), to_group(high, f % GROUPS, 0)
+    own_low = to_group(flow_ref[f, :, 0:LANES], 0, GROUPS - 1)
+    own_high = to_group(flow_ref[f, :, (chunks - 1) * LANES : chunks * LANES], GROUPS - 1, 0)
     return jnp.where(at == 0, own_low, low), jnp.where(at == count - 1, own_high, high)
 
 
-def x_factor_kernel(qx_ref, codes_ref, out_ref, inverse_ref, lower_ref, up_ref, left_ref, right_ref):
+def x_factor_kernel(
+    qx_ref, codes_ref, out_ref, inverse_ref, lower_ref, up_ref, left_ref, right_ref, points_ref
+):
     cells = inverse_ref.shape[0]
     chunks = inverse_ref.shape[2]
     rows = [[qx_ref[f, i * chunks : (i + 1) * chunks, :] for f in range(5)] for i in range(cells)]
-    speeds = []
+    speeds, points = [], []
     for q in rows:
         prim = primitives(q)
         speeds.append(three_speeds(prim[1], prim[6]))
+        impedance = q[0] * prim[6]
+        points.append([impedance, 0.5 / impedance])
+    for i in range(cells):
+        store(points_ref.at[i], points[i])
     neumann = x_edges(codes_ref, (chunks, LANES))
     parts = factor(
         speeds[:1] + speeds + speeds[-1:], (None, neumann[0]), (None, neumann[1]), forced=True
@@ -341,7 +365,7 @@
 
     for i in range(cells):
         q = rows[i + 1]
-        inverse, vel_u, vel_v, vel_w, kinetic, pressure, sound = prims[i]
+        _, _, vel_v, vel_w, _, pressure, _ = prims[i]
         after = [y_next(v) for v in list(q) + [vel_v, pressure]]
         before = [y_before(v) for v in list(q) + [vel_v, pressure]]
         flux_after = flux_of(after, 2, after[5], after[6])
@@ -411,7 +435,7 @@
     joined, q_first, q_last = merge_factors(bit_low("gx", level), load(own_ref), load(other_ref))
     if final:
         low = bit_low("gx", level + 1)
-        b_f, c_f, b_e, c_e = (joined[3 * n : 3 * n + 3] for n in range(4))
+        b_f, _, _, c_e = (joined[3 * n : 3 * n + 3] for n in range(4))
         pairs = list(zip(c_e, b_f)) + list(zip(q_last, q_first))
         store(out_ref, [jnp.where(low, e, f) for e, f in pairs])
     else:
@@ -444,7 +468,7 @@
     if axis == "gx":
         new = last_join_forced(low, own, other)
     else:
-        new = last_join(low, own, other, speed_of)
+        new = last_join(own, other, speed_of)
     outer = from_last(low, new)
     for level in range(levels - 2, -1, -1):
         outer = step_down(bit_low(axis, level), load(side_refs[level]), outer, speed_of)
@@ -526,29 +550,25 @@
 
 
 def y_kernel(levels, *refs):
-    (qx_ref, own_ref, left_ref, right_ref, mine_ref, other_ref, mine_factor_ref, other_factor_ref,
+    (points_ref, own_ref, left_ref, right_ref, mine_ref, other_ref, mine_factor_ref, other_factor_ref,
      packed_ref, inverse_ref, lower_ref, up_ref, join_ref) = refs[:13]
     sides = refs[13 : 13 + levels - 1]
     out_ref, yown_ref, side_ref, turn_ref = refs[13 + levels - 1 :]
-    chunks = qx_ref.shape[1] // own_ref.shape[0]
+    chunks = own_ref.shape[2]
     cells = own_ref.shape[0]
     steps = chunks
     mine, other = load(mine_ref) + load(mine_factor_ref), load(other_ref) + load(other_factor_ref)
     outer_l, outer_r = outer_values("gx", levels, SPEED_OF, mine, other, sides)
     for i in range(cells):
-        q = [qx_ref[f, i * chunks : (i + 1) * chunks, :] for f in range(5)]
-        sound = primitives(q)[6]
+        impedance, half_admittance = load(points_ref.at[i])
         wave = [
             own_ref[i, f] + left_ref[i, SPEED_OF[f]] * outer_l[f] + right_ref[i, SPEED_OF[f]] * outer_r[f]
             for f in range(5)
         ]
-        impedance = q[0] * sound
-        squared = sound * sound
         dp = 0.5 * (wave[0] + wave[4])
-        du = (wave[4] - wave[0]) / (2.0 * impedance)
-        dr = (wave[1] + dp) / squared
+        du = (wave[4] - wave[0]) * half_admittance
         normal = impedance * wave[2]
-        values = [dp - normal, squared * dr - dp, du, wave[3], dp + normal]
+        values = [dp - normal, wave[1], du, wave[3], dp + normal]
         for n, value in enumerate(values):
             turn_ref[n, i * chunks : (i + 1) * chunks, :] = value
     lane = lax.broadcasted_iota(jnp.int32, (cells, LANES), 1)
@@ -596,64 +616,86 @@
     return jnp.where(group % 2 == 1, half, up)
 
 
-def final_kernel(levels, *refs):
-    (flow_ref, yown_ref, yleft_ref, yright_ref, ends_ref, side_ref, mine_ref, other_ref) = refs[:8]
-    sides = refs[8 : 8 + levels - 1]
-    out_hbm, out_ref, sems = refs[8 + levels - 1 :]
+def ungroup(values, c, group):
+    steps = len(values)
+    result = None
+    for g in range(GROUPS):
+        y = c * GROUPS + g
+        piece = to_group(values[y % steps], y // steps, g)
+        result = piece if g == 0 else jnp.where(group == g, piece, result)
+    return result
+
+
+def prepare_kernel(
+    flow_ref, yown_ref, yleft_ref, yright_ref, ends_ref, side_ref,
+    terms_ref, points_ref, half_ref, quarter_ref,
+):
     cells = flow_ref.shape[1]
     chunks = flow_ref.shape[2] // LANES
-    steps = chunks
-    lane = lax.broadcasted_iota(jnp.int32, (cells, LANES), 1)
-    group = lane // NZ
+    group = lax.broadcasted_iota(jnp.int32, (cells, LANES), 1) // NZ
+    columns = [
+        [ref[j, n] for j in range(chunks)]
+        for ref in (yown_ref, yleft_ref, yright_ref) for n in range(ref.shape[1])
+    ]
+    for c in range(chunks):
+        store(terms_ref.at[c], [ungroup(column, c, group) for column in columns])
+        q = [flow_ref[f, :, c * LANES : (c + 1) * LANES] for f in range(5)]
+        _, vel_u, vel_v, vel_w, kinetic, _, sound = primitives(q)
+        store(
+            points_ref.at[c],
+            [vel_u, vel_v, vel_w, kinetic, 1.0 / (2.0 * q[0] * sound), 1.0 / (sound * sound)],
+        )
+    for level, ref, count in ((1, half_ref, 2), (0, quarter_ref, GROUPS)):
+        rows = load(ends_ref.at[level]) + load(side_ref.at[level])
+        for n in range(count):
+            store(ref.at[n], [spread(group, row, n * GROUPS // count) for row in rows])
+
+
+def final_kernel(levels, *refs):
+    (flow_ref, terms_ref, points_ref, half_ref, quarter_ref, mine_ref, other_ref) = refs[:7]
+    sides = refs[7 : 7 + levels - 1]
+    out_hbm, out_ref, sems = refs[7 + levels - 1 :]
+    cells = flow_ref.shape[1]
+    chunks = flow_ref.shape[2] // LANES
+    group = lax.broadcasted_iota(jnp.int32, (cells, LANES), 1) // NZ
     outer = outer_values("gy", levels, PACKED_SPEED, load(mine_ref), load(other_ref), sides)
     outer = tuple(
         [spread(group, v[0], 0), spread(group, v[0], 1), spread(group, v[0], 3),
          spread(group, v[1], 1), spread(group, v[0], 2)]
         for v in outer
     )
-    for level in (1, 0):
-        side = load(ends_ref.at[level]) + load(side_ref.at[level])
-        outer = step_down(lane_low(group, level), side, outer, SPEED_OF)
-    outer_l, outer_r = outer
-    solved = [
-        [
-            yown_ref[j, f] + yleft_ref[j, SPEED_OF[f]] * outer_l[f] + yright_ref[j, SPEED_OF[f]] * outer_r[f]
-            for f in range(5)
-        ]
-        for j in range(steps)
-    ]
     copies = []
-    for c in range(chunks):
-        wave = []
-        for f in range(5):
-            value = None
-            for g in range(GROUPS):
-                y = c * GROUPS + g
-                piece = solved[y % steps][f]
-                shift = (g - y // steps) * NZ % LANES
-                piece = pltpu.roll(piece, shift, 1) if shift else piece
-                value = piece if g == 0 else jnp.where(group == g, piece, value)
-            wave.append(value)
-        q = [flow_ref[f, :, c * LANES : (c + 1) * LANES] for f in range(5)]
-        inverse, vel_u, vel_v, vel_w, kinetic, pressure, sound = primitives(q)
-        dp = 0.5 * (wave[0] + wave[4])
-        dv = (wave[4] - wave[0]) / (2.0 * q[0] * sound)
-        dr = (wave[1] + dp) / (sound * sound)
-        du, dw = wave[2], wave[3]
-        energy = (
-            kinetic * dr + q[0] * (vel_u * du + vel_v * dv + vel_w * dw) + dp * (1.0 / (GAMMA - 1.0))
-        )
-        result = [dr, vel_u * dr + q[0] * du, vel_v * dr + q[0] * dv, vel_w * dr + q[0] * dw, energy]
-        for f in range(5):
-            out_ref[f, :, c * LANES : (c + 1) * LANES] = result[f]
-        part = (slice(None), slice(None), slice(c * LANES, (c + 1) * LANES))
-        copies.append(pltpu.make_async_copy(out_ref.at[part], out_hbm.at[part], sems.at[c]))
+    for s in range(GROUPS):
+        half = step_down(s < GROUPS // 2, load(half_ref.at[s * 2 // GROUPS]), outer, SPEED_OF)
+        outer_l, outer_r = step_down(s % 2 == 0, load(quarter_ref.at[s]), half, SPEED_OF)
+        for c in range(s * chunks // GROUPS, (s + 1) * chunks // GROUPS):
+            wave = [
+                terms_ref[c, f] + terms_ref[c, 5 + SPEED_OF[f]] * outer_l[f]
+                + terms_ref[c, 8 + SPEED_OF[f]] * outer_r[f]
+                for f in range(5)
+            ]
+            density = flow_ref[0, :, c * LANES : (c + 1) * LANES]
+            vel_u, vel_v, vel_w, kinetic, half_admittance, inverse_squared = load(points_ref.at[c])
+            dp = 0.5 * (wave[0] + wave[4])
+            dv = (wave[4] - wave[0]) * half_admittance
+            dr = (wave[1] + dp) * inverse_squared
+            du, dw = wave[2], wave[3]
+            energy = (
+                kinetic * dr + density * (vel_u * du + vel_v * dv + vel_w * dw)
+                + dp * (1.0 / (GAMMA - 1.0))
+            )
+            result = [dr, vel_u * dr + density * du, vel_v * dr + density * dv, vel_w * dr + density * dw, energy]
+            for f in range(5):
+                out_ref[f, :, c * LANES : (c + 1) * LANES] = result[f]
+        width = chunks // GROUPS * LANES
+        part = (slice(None), slice(None), slice(s * width, (s + 1) * width))
+        copies.append(pltpu.make_async_copy(out_ref.at[part], out_hbm.at[part], sems.at[s]))
         copies[-1].start()
     for copy in copies:
         copy.wait()
 
 
-def call(kernel, name, args, outs, scratch=(), out_hbm=False):
+def call(kernel, args, outs, scratch=(), out_hbm=False):
     vmem, hbm = (pl.BlockSpec(memory_space=space) for space in (pltpu.VMEM, pltpu.HBM))
     return pl.pallas_call(
         kernel,
@@ -662,7 +704,6 @@
         out_specs=[hbm if out_hbm else vmem] * len(outs),
         scratch_shapes=list(scratch),
         compiler_params=pltpu.CompilerParams(vmem_limit_bytes=16 * 1024 * 1024),
-        name=name,
     )(*args)
 
 
@@ -698,17 +739,16 @@
     levels_x, levels_y = levels_of(count_x), levels_of(count_y)
     tile_x, tile_y = (chunks, LANES), (cells, LANES)
 
-    qx, one, two = call(
-        pack_kernel, "pack", [flow], [(5, cells * chunks, LANES), (5,) + tile_y, (5,) + tile_y]
-    )
+    qx, one, two = call(pack_kernel, [flow], [(5, cells * chunks, LANES), (2,) + tile_y, (2,) + tile_y])
     round_trip = snake(count_x, count_y)
     one = lax.ppermute(one, ("gx", "gy"), round_trip)
     two = lax.ppermute(two, ("gx", "gy"), [(b, a) for a, b in round_trip])
 
-    factors, inverse, lower, upper, left, right = call(
-        x_factor_kernel, "xfactor", [qx, x_codes], [(COEFS + 10,) + tile_x] + [(cells, 3) + tile_x] * 5
-    )
-    (source,) = call(x_source_kernel, "xsource", [qx], [(cells, 5) + tile_x])
+    factors, inverse, lower, upper, left, right, xpoints = call(
+        x_factor_kernel, [qx, x_codes],
+        [(COEFS + 10,) + tile_x] + [(cells, 3) + tile_x] * 5 + [(cells, 2) + tile_x],
+    )
+    (source,) = call(x_source_kernel, [qx], [(cells, 5) + tile_x])
     all_factors = []
     for level in range(levels_x):
         other = lax.ppermute(factors, "gx", pairs_across(count_x, level))
@@ -716,11 +756,11 @@
         if level < levels_x - 1:
             final = level == levels_x - 2
             (factors,) = call(
-                functools.partial(x_merge_factor_kernel, level, final), f"xfactor{level}",
+                functools.partial(x_merge_factor_kernel, level, final),
                 [factors, other], [(8 if final else COEFS + 10,) + tile_x],
             )
     rows, own = call(
-        x_kernel, "xsweep", [flow, one, two, source, inverse, lower, upper],
+        x_kernel, [flow, one, two, source, inverse, lower, upper],
         [(10,) + tile_x, (cells, 5) + tile_x],
         [pltpu.VMEM((5,) + tile_y, jnp.float32), pltpu.VMEM((5,) + tile_y, jnp.float32)],
     )
@@ -729,36 +769,40 @@
         other = lax.ppermute(rows, "gx", pairs_across(count_x, level))
         final = level == levels_x - 2
         rows, side_rows = call(
-            functools.partial(x_merge_kernel, level, final), f"xmerge{level}",
+            functools.partial(x_merge_kernel, level, final),
             [rows, other, *all_factors[level]], [(5 if final else 10,) + tile_x, (11,) + tile_x],
         )
         sides.append(side_rows)
     other = lax.ppermute(rows, "gx", pairs_across(count_x, levels_x - 1))
     y_factors, yinverse, ylower, yup, yleft, yright, yjoin, yside = call(
-        y_factor_kernel, "yfactor", [flow, one, two, y_codes],
+        y_factor_kernel, [flow, one, two, y_codes],
         [(4,) + tile_y] + [(chunks, 3) + tile_y] * 5 + [(2, 15) + tile_y, (2, 6) + tile_y],
     )
     packed, yown, yends = call(
-        functools.partial(y_kernel, levels_x), "ysweep",
-        [qx, own, left, right, rows, other, *all_factors[-1], y_factors, yinverse, ylower, yup, yjoin] + sides,
+        functools.partial(y_kernel, levels_x),
+        [xpoints, own, left, right, rows, other, *all_factors[-1], y_factors, yinverse, ylower, yup, yjoin] + sides,
         [(8,) + tile_y, (chunks, 5) + tile_y, (2, 5) + tile_y],
         [pltpu.VMEM((5, cells * chunks, LANES), jnp.float32)],
+    )
+    prepared = call(
+        prepare_kernel, [flow, yown, yleft, yright, yends, yside],
+        [(chunks, 11) + tile_y, (chunks, 6) + tile_y, (2, 11) + tile_y, (GROUPS, 11) + tile_y],
     )
     sides = []
     for level in range(levels_y - 1):
         other = lax.ppermute(packed, "gy", pairs_at(count_y, level))
         final = level == levels_y - 2
         packed, side_rows = call(
-            functools.partial(y_merge_kernel, level, final), f"ymerge{level}",
+            functools.partial(y_merge_kernel, level, final),
             [packed, other], [(3 if final else 8,) + tile_y, (4,) + tile_y],
         )
         sides.append(side_rows)
     other = lax.ppermute(packed, "gy", pairs_at(count_y, levels_y - 1))
     (result,) = call(
-        functools.partial(final_kernel, levels_y), "final",
-        [flow, yown, yleft, yright, yends, yside, packed, other] + sides,
+        functools.partial(final_kernel, levels_y),
+        [flow, *prepared, packed, other] + sides,
         [(5, cells, columns)],
-        [pltpu.VMEM((5, cells, columns), jnp.float32), pltpu.SemaphoreType.DMA((chunks,))],
+        [pltpu.VMEM((5, cells, columns), jnp.float32), pltpu.SemaphoreType.DMA((GROUPS,))],
         out_hbm=True,
     )
     return result

time: 27.7 us -> 30 us (1.083)
  waiting for transfers between devices: 9.48 us -> 12.1 us
  starting transfers between devices: 13.3 us -> 12.6 us
  Pallas kernels: 3.03 us -> 3.48 us
    ppermute x3, starting transfers between devices: 3.62 us -> 4.75 us  [local(): other = lax.ppermute(factors, 'gx', pairs_across(count_x, level))]
    ppermute x1, starting transfers between devices: 2.59 us -> 1.58 us  [local(): one = lax.ppermute(one, ('gx', 'gy'), round_trip)]
    ppermute x1, waiting for transfers between devices: 0.01 us -> 1 us  [local(): one = lax.ppermute(one, ('gx', 'gy'), round_trip)]
    ppermute x2, starting transfers between devices: 1.39 us -> 0.44 us  [local(): other = lax.ppermute(rows, 'gx', pairs_across(count_x, level))]
    ppermute x2, waiting for transfers between devices: 1.87 us -> 2.83 us  [local(): other = lax.ppermute(rows, 'gx', pairs_across(count_x, level))]
    ppermute x3, waiting for transfers between devices: 0.01 us -> 0.94 us  [local(): other = lax.ppermute(factors, 'gx', pairs_across(count_x, level))]
    ppermute x1, waiting for transfers between devices: 2 us -> 1.45 us  [local(): other = lax.ppermute(packed, 'gy', pairs_at(count_y, levels_y - 1))]
    ppermute x1, waiting for transfers between devices: 1.81 us -> 2.29 us  [local(): two = lax.ppermute(two, ('gx', 'gy'), [(b, a) for a, b in round_trip])]
  transfers between devices with their start and end apart: 10 -> 10, of which waited for: 6 -> 8; matrix products, arithmetic and copies ran while one was open for 0% -> 0% of each run, Pallas kernels for 5% -> 6%
where the time goes in v3:
time: 30 us; the launch traced here: 29.9 us
  starting transfers between devices  12.6 us (42%)
  waiting for transfers between devices  12.1 us (40%)
  Pallas kernels  3.48 us (12%)
  local copies, waits for them, and re-layouts  1.61 us (5%)
    ppermute x3, starting transfers between devices, local(): other = lax.ppermute(factors, 'gx', pairs_across(count_x, level))  4.75 us
    pallas_call x13, Pallas kernels, call(): pl.pallas_call(kernel, out_shape=[jax.ShapeDtypeStruct(shape, jnp.float32...  3.48 us
    ppermute x2, waiting for transfers between devices, local(): other = lax.ppermute(rows, 'gx', pairs_across(count_x, level))  2.83 us
    ppermute x1, starting transfers between devices, local(): other = lax.ppermute(packed, 'gy', pairs_at(count_y, levels_y - 1))  2.65 us
    ppermute x1, waiting for transfers between devices, local(): other = lax.ppermute(packed, 'gy', pairs_at(count_y, level))  2.34 us
    ppermute x1, waiting for transfers between devices, local(): two = lax.ppermute(two, ('gx', 'gy'), [(b, a) for a, b in round_trip])  2.29 us
    ppermute x1, starting transfers between devices, local(): other = lax.ppermute(packed, 'gy', pairs_at(count_y, level))  1.64 us
    unnamed x8, local copies, waits for them, and re-layouts  1.61 us
  transfers between devices with their start and end apart: 10, of which 8 were waited for; matrix products, arithmetic and copies ran while one was open for 0% of the time, Pallas kernels for 6%

profile of v3, /device:TPU:0, one launch (start us, length us, event | category | flops | bytes accessed | tf_op | source)
XLA Modules:
  0.0 29.9 jit_solution(3503019708270571743)
XLA Ops:
  0.0 0.9 %copy-done = f32[5,8,1024]{2,1,0:T(8,128)S(1)} copy-done((f32[5,8,1024]{2,1,0:T(8,128)S(1)}, f32[5,8,1024]{2,1,0:T(8,128)}, u32[]{:S(2)}) %copy-start) | copy-done | bytes 163864
  1.0 0.7 %copy-done.2 = s32[2,32]{1,0:T(2,128)S(1)} copy-done((s32[2,32]{1,0:T(2,128)S(1)}, s32[2,32]{1,0:T(2,128)}, u32[]{:S(2)}) %copy-start.2) | copy-done | bytes 280
  1.9 0.6 %collective-permute-start.3 = (f32[22,8,128]{2,1,0:T(8,128)S(1)}, f32[22,8,128]{2,1,0:T(8,128)S(1)}, u32[]{:S(2)}, u32[]{:S(2)}) collective-permute-start(f32[22,8,128]{2,1,0:T(8,128)S(1)} %get-tuple-element.49.own_factor_ref.own_ref), channel_id=1, source_target_pairs={{0,4},{4,0},{8,12},{12,8},{16,20},{20,16},{24,28},{28,24},{1,5},{5... | collective-permute-start | bytes 270344 | tf_op jit(solution)/shard_map/ppermute | solution.py:754
  2.4 0.9 %collective-permute-done.3.other_factor_ref.other_ref = f32[22,8,128]{2,1,0:T(8,128)S(1)} collective-permute-done((f32[22,8,128]{2,1,0:T(8,128)S(1)}, f32[22,8,128]{2,1,0:T(8,128)S(1)}, u32[]{:S(2)}, u32[]{:S(2)}) %collective-permute-start.3) | collective-permute-done | bytes 90144 | tf_op jit(solution)/shard_map/ppermute | solution.py:754
  3.4 2.7 %collective-permute-start.5 = (f32[22,8,128]{2,1,0:T(8,128)S(1)}, f32[22,8,128]{2,1,0:T(8,128)S(1)}, u32[]{:S(2)}, u32[]{:S(2)}) collective-permute-start(f32[22,8,128]{2,1,0:T(8,128)S(1)} %shard_map.42.own_factor_ref.own_ref), channel_id=1, source_target_pairs={{0,12},{4,8},{8,4},{12,0},{16,28},{20,24},{24,20},{28,16},{1,13},{... | collective-permute-start | bytes 270344 | tf_op jit(solution)/shard_map/ppermute | solution.py:754
  6.1 1.6 %collective-permute-start = (f32[2,8,128]{2,1,0:T(8,128)S(1)}, f32[2,8,128]{2,1,0:T(8,128)S(1)}, u32[]{:S(2)}, u32[]{:S(2)}) collective-permute-start(f32[2,8,128]{2,1,0:T(8,128)S(1)} %get-tuple-element.40), channel_id=1, source_target_pairs={{0,1},{1,2},{2,3},{3,7},{4,0},{5,4},{6,5},{7,6},{8,9},{9,10},{10,1... | collective-permute-start | bytes 24584 | tf_op jit(solution)/shard_map/ppermute | solution.py:744
  7.6 0.4 %shard_map.39.source_ref = f32[8,5,8,128]{3,2,1,0:T(8,128)S(1)} custom-call(f32[5,64,128]{2,1,0:T(8,128)S(1)} %get-tuple-element.38.qx_ref), custom_call_target="tpu_custom_call" | custom-call | tf_op jit(solution)/shard_map/pallas_call | solution.py:700
  8.0 1.0 %collective-permute-done.one_ref = f32[2,8,128]{2,1,0:T(8,128)S(1)} collective-permute-done((f32[2,8,128]{2,1,0:T(8,128)S(1)}, f32[2,8,128]{2,1,0:T(8,128)S(1)}, u32[]{:S(2)}, u32[]{:S(2)}) %collective-permute-start) | collective-permute-done | bytes 8224 | tf_op jit(solution)/shard_map/ppermute | solution.py:744
  9.0 2.3 %collective-permute-done.1.two_ref = f32[2,8,128]{2,1,0:T(8,128)S(1)} collective-permute-done((f32[2,8,128]{2,1,0:T(8,128)S(1)}, f32[2,8,128]{2,1,0:T(8,128)S(1)}, u32[]{:S(2)}, u32[]{:S(2)}) %collective-permute-start.1) | collective-permute-done | bytes 8224 | tf_op jit(solution)/shard_map/ppermute | solution.py:745
  11.3 0.2 shard_map.40
  11.6 1.2 %collective-permute-done.2.other_ref = f32[10,8,128]{2,1,0:T(8,128)S(1)} collective-permute-done((f32[10,8,128]{2,1,0:T(8,128)S(1)}, f32[10,8,128]{2,1,0:T(8,128)S(1)}, u32[]{:S(2)}, u32[]{:S(2)}) %collective-permute-start.2) | collective-permute-done | bytes 40992 | tf_op jit(solution)/shard_map/ppermute | solution.py:769
  12.9 0.4 %collective-permute-start.4 = (f32[10,8,128]{2,1,0:T(8,128)S(1)}, f32[10,8,128]{2,1,0:T(8,128)S(1)}, u32[]{:S(2)}, u32[]{:S(2)}) collective-permute-start(f32[10,8,128]{2,1,0:T(8,128)S(1)} %get-tuple-element.50.own_ref), channel_id=1, source_target_pairs={{0,12},{4,8},{8,4},{12,0},{16,28},{20,24},{24,20},{28,16},{1,13},{... | collective-permute-start | bytes 122888 | tf_op jit(solution)/shard_map/ppermute | solution.py:769
  13.3 1.5 %collective-permute-start.7 = (f32[8,8,128]{2,1,0:T(8,128)S(1)}, f32[8,8,128]{2,1,0:T(8,128)S(1)}, u32[]{:S(2)}, u32[]{:S(2)}) collective-permute-start(f32[8,8,128]{2,1,0:T(8,128)S(1)} %shard_map.44.refs_6_), channel_id=1, source_target_pairs={{0,20},{4,16},{8,28},{12,24},{16,4},{20,0},{24,12},{28,8},{1,21},{... | collective-permute-start | bytes 98312 | tf_op jit(solution)/shard_map/ppermute | solution.py:754
  14.9 1.6 %collective-permute-done.4.other_ref = f32[10,8,128]{2,1,0:T(8,128)S(1)} collective-permute-done((f32[10,8,128]{2,1,0:T(8,128)S(1)}, f32[10,8,128]{2,1,0:T(8,128)S(1)}, u32[]{:S(2)}, u32[]{:S(2)}) %collective-permute-start.4) | collective-permute-done | bytes 40992 | tf_op jit(solution)/shard_map/ppermute | solution.py:769
  16.6 1.6 %collective-permute-start.6 = (f32[5,8,128]{2,1,0:T(8,128)S(1)}, f32[5,8,128]{2,1,0:T(8,128)S(1)}, u32[]{:S(2)}, u32[]{:S(2)}) collective-permute-start(f32[5,8,128]{2,1,0:T(8,128)S(1)} %get-tuple-element.51.refs_4_), channel_id=1, source_target_pairs={{0,20},{4,16},{8,28},{12,24},{16,4},{20,0},{24,12},{28,8},{1,21},{... | collective-permute-start | bytes 61448 | tf_op jit(solution)/shard_map/ppermute | solution.py:776
  18.1 0.5 %shard_map.45 = (f32[4,8,128]{2,1,0:T(8,128)S(1)}, f32[8,3,8,128]{3,2,1,0:T(8,128)S(1)}, f32[8,3,8,128]{3,2,1,0:T(8,128)S(1)}, f32[8,3,8,128]{3,2,1,0:T(8,128)S(...) custom-call(f32[5,8,1024]{2,1,0:T(8,128)S(1)} %copy-done.1, ...), custom_call_target="tpu_custom_call" | custom-call | tf_op jit(solution)/shard_map/pallas_call | solution.py:700
  18.6 1.2 %collective-permute-done.6.refs_5_ = f32[5,8,128]{2,1,0:T(8,128)S(1)} collective-permute-done((f32[5,8,128]{2,1,0:T(8,128)S(1)}, f32[5,8,128]{2,1,0:T(8,128)S(1)}, u32[]{:S(2)}, u32[]{:S(2)}) %collective-permute-start.6) | collective-permute-done | bytes 20512 | tf_op jit(solution)/shard_map/ppermute | solution.py:776
  19.9 0.4 %shard_map.46 = (f32[8,8,128]{2,1,0:T(8,128)S(1)}, f32[8,5,8,128]{3,2,1,0:T(8,128)S(1)}, f32[2,5,8,128]{3,2,1,0:T(8,128)S(1)}) custom-call(f32[8,2,8,128]{3,2,1,0:T(8,128)S(1)} %get-tuple-element.39.refs_0_, f32[8,5,8,128]{3,2,1,0:T(8,128)S(1)} %get-tuple-element.45.refs_1_, f32[8,3,8,128]{3,2,1,0:T(8,128)S(1)} %get-tuple-element.46.refs_2_, ...), custom_call_target="tpu_custom_call" | custom-call | tf_op jit(solution)/shard_map/pallas_call | solution.py:700
  20.3 1.6 %collective-permute-start.8 = (f32[8,8,128]{2,1,0:T(8,128)S(1)}, f32[8,8,128]{2,1,0:T(8,128)S(1)}, u32[]{:S(2)}, u32[]{:S(2)}) collective-permute-start(f32[8,8,128]{2,1,0:T(8,128)S(1)} %get-tuple-element.68.own_ref), channel_id=1, source_target_pairs={{0,1},{1,0},{2,3},{3,2},{4,5},{5,4},{6,7},{7,6},{8,9},{9,8},{10,11... | collective-permute-start | bytes 98312 | tf_op jit(solution)/shard_map/ppermute | solution.py:793
  22.0 2.3 %collective-permute-done.8.other_ref = f32[8,8,128]{2,1,0:T(8,128)S(1)} collective-permute-done((f32[8,8,128]{2,1,0:T(8,128)S(1)}, f32[8,8,128]{2,1,0:T(8,128)S(1)}, u32[]{:S(2)}, u32[]{:S(2)}) %collective-permute-start.8) | collective-permute-done | bytes 32800 | tf_op jit(solution)/shard_map/ppermute | solution.py:793
  24.3 2.7 %collective-permute-start.9 = (f32[3,8,128]{2,1,0:T(8,128)S(1)}, f32[3,8,128]{2,1,0:T(8,128)S(1)}, u32[]{:S(2)}, u32[]{:S(2)}) collective-permute-start(f32[3,8,128]{2,1,0:T(8,128)S(1)} %get-tuple-element.69.refs_5_), channel_id=1, source_target_pairs={{0,2},{1,3},{2,0},{3,1},{4,6},{5,7},{6,4},{7,5},{8,10},{9,11},{10,... | collective-permute-start | bytes 36872 | tf_op jit(solution)/shard_map/ppermute | solution.py:800
  27.0 0.5 %shard_map.47 = (f32[8,11,8,128]{3,2,1,0:T(8,128)S(1)}, f32[8,6,8,128]{3,2,1,0:T(8,128)S(1)}, f32[2,11,8,128]{3,2,1,0:T(8,128)S(1)}, f32[4,11,8,128]{3,2,1,0:T(8,128)S(1)}) custom-call(f32[5,8,1024]{2,1,0:T(8,128)S(1)} %copy-done.1, f32[8,5,8,128]{3,2,1,0:T(8,128)S(1)} %get-tuple-element.59.yown_ref, f32[8,3,8,128]{3,2,1,0:T(8,128)S(1)} %get-tuple-element.60.yleft_ref, ...), custom_call_target="tpu_custom_call" | custom-call | tf_op jit(solution)/shard_map/pallas_call | solution.py:700
  27.5 1.5 %collective-permute-done.9.refs_6_ = f32[3,8,128]{2,1,0:T(8,128)S(1)} collective-permute-done((f32[3,8,128]{2,1,0:T(8,128)S(1)}, f32[3,8,128]{2,1,0:T(8,128)S(1)}, u32[]{:S(2)}, u32[]{:S(2)}) %collective-permute-start.9) | collective-permute-done | bytes 12320 | tf_op jit(solution)/shard_map/ppermute | solution.py:800
  29.0 0.9 %shard_map.49 = f32[5,8,1024]{2,1,0:T(8,128)} custom-call(f32[5,8,1024]{2,1,0:T(8,128)S(1)} %copy-done.1, f32[8,11,8,128]{3,2,1,0:T(8,128)S(1)} %get-tuple-element.64.refs_1_, f32[8,6,8,128]{3,2,1,0:T(8,128)S(1)} %get-tuple-element.65.refs_2_, f32[2,11,8,128]{3,2,1,0:T(8,128)S(1)} %get-tuple-element.66.refs_3_, ...), custom_call_target="tpu_custom_call" | custom-call | tf_op jit(solution)/shard_map/pallas_call | solution.py:700
  (17 shorter events, 0.6 us)
Async XLA Ops:
  0.0 0.9 %copy-start = (f32[5,8,1024]{2,1,0:T(8,128)S(1)}, f32[5,8,1024]{2,1,0:T(8,128)}, u32[]{:S(2)}) copy-start(f32[5,8,1024]{2,1,0:T(8,128)} %refs_0_.1) | copy-start | bytes 491524
  1.0 0.7 %copy-start.2 = (s32[2,32]{1,0:T(2,128)S(1)}, s32[2,32]{1,0:T(2,128)}, u32[]{:S(2)}) copy-start(s32[2,32]{1,0:T(2,128)} %codes_ref.2) | copy-start | bytes 772
  1.9 1.5 %collective-permute-start.3 = (f32[22,8,128]{2,1,0:T(8,128)S(1)}, f32[22,8,128]{2,1,0:T(8,128)S(1)}, u32[]{:S(2)}, u32[]{:S(2)}) collective-permute-start(f32[22,8,128]{2,1,0:T(8,128)S(1)} %get-tuple-element.49.own_factor_ref.own_ref), channel_id=1, source_target_pairs={{0,4},{4,0},{8,12},{12,8},{16,20},{20,16},{24,28},{28,24},{1,5},{5... | collective-permute-start | bytes 270344 | tf_op jit(solution)/shard_map/ppermute | solution.py:754
  3.4 9.9 %collective-permute-start.5 = (f32[22,8,128]{2,1,0:T(8,128)S(1)}, f32[22,8,128]{2,1,0:T(8,128)S(1)}, u32[]{:S(2)}, u32[]{:S(2)}) collective-permute-start(f32[22,8,128]{2,1,0:T(8,128)S(1)} %shard_map.42.own_factor_ref.own_ref), channel_id=1, source_target_pairs={{0,12},{4,8},{8,4},{12,0},{16,28},{20,24},{24,20},{28,16},{1,13},{... | collective-permute-start | bytes 270344 | tf_op jit(solution)/shard_map/ppermute | solution.py:754
  6.1 2.9 %collective-permute-start = (f32[2,8,128]{2,1,0:T(8,128)S(1)}, f32[2,8,128]{2,1,0:T(8,128)S(1)}, u32[]{:S(2)}, u32[]{:S(2)}) collective-permute-start(f32[2,8,128]{2,1,0:T(8,128)S(1)} %get-tuple-element.40), channel_id=1, source_target_pairs={{0,1},{1,2},{2,3},{3,7},{4,0},{5,4},{6,5},{7,6},{8,9},{9,10},{10,1... | collective-permute-start | bytes 24584 | tf_op jit(solution)/shard_map/ppermute | solution.py:744
  7.6 3.7 %copy-start.1 = (f32[5,8,1024]{2,1,0:T(8,128)S(1)}, f32[5,8,1024]{2,1,0:T(8,128)}, u32[]{:S(2)}) copy-start(f32[5,8,1024]{2,1,0:T(8,128)} %refs_0_.1) | copy-start | bytes 491524
  7.6 3.7 %collective-permute-start.1 = (f32[2,8,128]{2,1,0:T(8,128)S(1)}, f32[2,8,128]{2,1,0:T(8,128)S(1)}, u32[]{:S(2)}, u32[]{:S(2)}) collective-permute-start(f32[2,8,128]{2,1,0:T(8,128)S(1)} %get-tuple-element.41), channel_id=1, source_target_pairs={{1,0},{2,1},{3,2},{7,3},{0,4},{4,5},{5,6},{6,7},{9,8},{10,9},{11,1... | collective-permute-start | bytes 24584 | tf_op jit(solution)/shard_map/ppermute | solution.py:745
  11.6 1.3 %collective-permute-start.2 = (f32[10,8,128]{2,1,0:T(8,128)S(1)}, f32[10,8,128]{2,1,0:T(8,128)S(1)}, u32[]{:S(2)}, u32[]{:S(2)}) collective-permute-start(f32[10,8,128]{2,1,0:T(8,128)S(1)} %get-tuple-element.48.own_ref), channel_id=1, source_target_pairs={{0,4},{4,0},{8,12},{12,8},{16,20},{20,16},{24,28},{28,24},{1,5},{5... | collective-permute-start | bytes 122888 | tf_op jit(solution)/shard_map/ppermute | solution.py:769
  12.9 3.6 %collective-permute-start.4 = (f32[10,8,128]{2,1,0:T(8,128)S(1)}, f32[10,8,128]{2,1,0:T(8,128)S(1)}, u32[]{:S(2)}, u32[]{:S(2)}) collective-permute-start(f32[10,8,128]{2,1,0:T(8,128)S(1)} %get-tuple-element.50.own_ref), channel_id=1, source_target_pairs={{0,12},{4,8},{8,4},{12,0},{16,28},{20,24},{24,20},{28,16},{1,13},{... | collective-permute-start | bytes 122888 | tf_op jit(solution)/shard_map/ppermute | solution.py:769
  13.3 6.5 %collective-permute-start.7 = (f32[8,8,128]{2,1,0:T(8,128)S(1)}, f32[8,8,128]{2,1,0:T(8,128)S(1)}, u32[]{:S(2)}, u32[]{:S(2)}) collective-permute-start(f32[8,8,128]{2,1,0:T(8,128)S(1)} %shard_map.44.refs_6_), channel_id=1, source_target_pairs={{0,20},{4,16},{8,28},{12,24},{16,4},{20,0},{24,12},{28,8},{1,21},{... | collective-permute-start | bytes 98312 | tf_op jit(solution)/shard_map/ppermute | solution.py:754
  16.6 1.6 %copy-start.3 = (s32[2,8]{1,0:T(2,128)S(1)}, s32[2,8]{1,0:T(2,128)}, u32[]{:S(2)}) copy-start(s32[2,8]{1,0:T(2,128)} %codes_ref.3) | copy-start | bytes 196
  16.6 3.3 %collective-permute-start.6 = (f32[5,8,128]{2,1,0:T(8,128)S(1)}, f32[5,8,128]{2,1,0:T(8,128)S(1)}, u32[]{:S(2)}, u32[]{:S(2)}) collective-permute-start(f32[5,8,128]{2,1,0:T(8,128)S(1)} %get-tuple-element.51.refs_4_), channel_id=1, source_target_pairs={{0,20},{4,16},{8,28},{12,24},{16,4},{20,0},{24,12},{28,8},{1,21},{... | collective-permute-start | bytes 61448 | tf_op jit(solution)/shard_map/ppermute | solution.py:776
  20.3 4.0 %collective-permute-start.8 = (f32[8,8,128]{2,1,0:T(8,128)S(1)}, f32[8,8,128]{2,1,0:T(8,128)S(1)}, u32[]{:S(2)}, u32[]{:S(2)}) collective-permute-start(f32[8,8,128]{2,1,0:T(8,128)S(1)} %get-tuple-element.68.own_ref), channel_id=1, source_target_pairs={{0,1},{1,0},{2,3},{3,2},{4,5},{5,4},{6,7},{7,6},{8,9},{9,8},{10,11... | collective-permute-start | bytes 98312 | tf_op jit(solution)/shard_map/ppermute | solution.py:793
  24.3 4.7 %collective-permute-start.9 = (f32[3,8,128]{2,1,0:T(8,128)S(1)}, f32[3,8,128]{2,1,0:T(8,128)S(1)}, u32[]{:S(2)}, u32[]{:S(2)}) collective-permute-start(f32[3,8,128]{2,1,0:T(8,128)S(1)} %get-tuple-element.69.refs_5_), channel_id=1, source_target_pairs={{0,2},{1,3},{2,0},{3,1},{4,6},{5,7},{6,4},{7,5},{8,10},{9,11},{10,... | collective-permute-start | bytes 36872 | tf_op jit(solution)/shard_map/ppermute | solution.py:800

commit v4 on v3

--- a/solution.py
+++ b/solution.py
@@ -130,11 +130,6 @@
     after = [jnp.where(low, b, a) for a, b in zip(own, other)]
     joined, e, f = join(unpack(before, fields, speeds), unpack(after, fields, speeds), speed_of)
     return joined, [jnp.where(low, b, a) for a, b in zip(e, f)]
-
-
-def facing(low, rows, fields=5, speeds=3):
-    a_f, a_e, b_f, _, _, c_e = unpack(rows, fields, speeds)
-    return [jnp.where(low, e, f) for e, f in zip(a_e + c_e, a_f + b_f)]
 
 
 def join_factors(q_before, q_after):
@@ -455,24 +450,48 @@
     store(side_ref, side)
 
 
-def y_merge_kernel(level, final, own_ref, other_ref, out_ref, side_ref):
+def y_merge_kernel(level, own_ref, other_ref, out_ref, side_ref):
     joined, side = merge(bit_low("gy", level), load(own_ref), load(other_ref), PACKED_SPEED)
-    if final:
-        joined = facing(bit_low("gy", level + 1), joined, 2, 1)
     store(out_ref, joined)
     store(side_ref, side)
 
 
-def outer_values(axis, levels, speed_of, own, other, side_refs):
-    low = bit_low(axis, levels - 1)
-    if axis == "gx":
-        new = last_join_forced(low, own, other)
-    else:
-        new = last_join(own, other, speed_of)
-    outer = from_last(low, new)
+def outer_values(levels, own, other, side_refs):
+    low = bit_low("gx", levels - 1)
+    outer = from_last(low, last_join_forced(low, own, other))
     for level in range(levels - 2, -1, -1):
-        outer = step_down(bit_low(axis, level), load(side_refs[level]), outer, speed_of)
+        outer = step_down(bit_low("gx", level), load(side_refs[level]), outer, SPEED_OF)
     return outer
+
+
+def pick(place, values):
+    return [
+        functools.reduce(lambda old, n: jnp.where(place == n, items[n], old), range(1, len(items)), items[0])
+        for items in zip(*values)
+    ]
+
+
+def outer_of_four(place, own, arrived, speed_of):
+    fields, speeds = len(speed_of), max(speed_of) + 1
+    ring = [own] + arrived
+    segments = [unpack(pick((place - n) % 4, ring), fields, speeds) for n in range(4)]
+    left, e_left, f_left = join(segments[0], segments[1], speed_of)
+    right, e_right, f_right = join(segments[2], segments[3], speed_of)
+    a_e, c_e = (unpack(left, fields, speeds)[n] for n in (1, 5))
+    a_f, b_f = (unpack(right, fields, speeds)[n] for n in (0, 2))
+    e_mid, f_mid, zero = [], [], jnp.zeros_like(a_e[0])
+    inverse = [1.0 / (1.0 - c_e[k] * b_f[k]) for k in range(speeds)]
+    for n in range(fields):
+        k = speed_of[n]
+        e_mid.append((a_e[n] + c_e[k] * a_f[n]) * inverse[k])
+        f_mid.append((a_f[n] + b_f[k] * a_e[n]) * inverse[k])
+
+    def inner(terms, outer, side):
+        return [terms[n] + terms[fields + side * speeds + speed_of[n]] * outer[n] for n in range(fields)]
+
+    lefts = [[zero] * fields, inner(e_left, f_mid, 1), e_mid, inner(e_right, e_mid, 0)]
+    rights = [inner(f_left, f_mid, 1), f_mid, inner(f_right, e_mid, 0), [zero] * fields]
+    return pick(place, lefts), pick(place, rights)
 
 
 PACKED_SPEED = (0, 0)
@@ -558,7 +577,7 @@
     cells = own_ref.shape[0]
     steps = chunks
     mine, other = load(mine_ref) + load(mine_factor_ref), load(other_ref) + load(other_factor_ref)
-    outer_l, outer_r = outer_values("gx", levels, SPEED_OF, mine, other, sides)
+    outer_l, outer_r = outer_values(levels, mine, other, sides)
     for i in range(cells):
         impedance, half_admittance = load(points_ref.at[i])
         wave = [
@@ -652,13 +671,16 @@
 
 
 def final_kernel(levels, *refs):
-    (flow_ref, terms_ref, points_ref, half_ref, quarter_ref, mine_ref, other_ref) = refs[:7]
-    sides = refs[7 : 7 + levels - 1]
-    out_hbm, out_ref, sems = refs[7 + levels - 1 :]
+    (flow_ref, terms_ref, points_ref, half_ref, quarter_ref, mine_ref) = refs[:6]
+    arrived, sides = refs[6:9], refs[9 : 9 + levels]
+    out_hbm, out_ref, sems = refs[9 + levels :]
     cells = flow_ref.shape[1]
     chunks = flow_ref.shape[2] // LANES
     group = lax.broadcasted_iota(jnp.int32, (cells, LANES), 1) // NZ
-    outer = outer_values("gy", levels, PACKED_SPEED, load(mine_ref), load(other_ref), sides)
+    place = (lax.axis_index("gy") >> levels) % 4
+    outer = outer_of_four(place, load(mine_ref), [load(ref) for ref in arrived], PACKED_SPEED)
+    for level in range(levels - 1, -1, -1):
+        outer = step_down(bit_low("gy", level), load(sides[level]), outer, PACKED_SPEED)
     outer = tuple(
         [spread(group, v[0], 0), spread(group, v[0], 1), spread(group, v[0], 3),
          spread(group, v[1], 1), spread(group, v[0], 2)]
@@ -725,6 +747,11 @@
     return pairs
 
 
+def ring_of_four(count, step):
+    width = count // 4
+    return [(i, (i + step * width) % count) for i in range(count)]
+
+
 def levels_of(count):
     levels = count.bit_length() - 1
     assert count == 1 << levels and levels >= 2
@@ -789,18 +816,19 @@
         [(chunks, 11) + tile_y, (chunks, 6) + tile_y, (2, 11) + tile_y, (GROUPS, 11) + tile_y],
     )
     sides = []
-    for level in range(levels_y - 1):
+    for level in range(levels_y - 2):
         other = lax.ppermute(packed, "gy", pairs_at(count_y, level))
-        final = level == levels_y - 2
         packed, side_rows = call(
-            functools.partial(y_merge_kernel, level, final),
-            [packed, other], [(3 if final else 8,) + tile_y, (4,) + tile_y],
+            functools.partial(y_merge_kernel, level),
+            [packed, other], [(8,) + tile_y, (4,) + tile_y],
         )
         sides.append(side_rows)
-    other = lax.ppermute(packed, "gy", pairs_at(count_y, levels_y - 1))
+    arrived = []
+    for step in range(1, 4):
+        arrived.append(lax.ppermute(packed, "gy", ring_of_four(count_y, step)))
     (result,) = call(
-        functools.partial(final_kernel, levels_y),
-        [flow, *prepared, packed, other] + sides,
+        functools.partial(final_kernel, levels_y - 2),
+        [flow, *prepared, packed, *arrived] + sides,
         [(5, cells, columns)],
         [pltpu.VMEM((5, cells, columns), jnp.float32), pltpu.SemaphoreType.DMA((GROUPS,))],
         out_hbm=True,

time: 30 us -> 30.2 us (level)
  starting transfers between devices: 12.6 us -> 13 us
    ppermute x2 -> x3, starting transfers between devices: 4.3 us -> 4.67 us  [local(): arrived.append(lax.ppermute(packed, 'gy', ring_of_four(count_y, step)))]
    ppermute x2 -> x3, waiting for transfers between devices: 3.79 us -> 3.57 us  [local(): arrived.append(lax.ppermute(packed, 'gy', ring_of_four(count_y, step)))]
    pallas_call x13 -> x12, Pallas kernels: 3.48 us -> 3.49 us  [call(): pl.pallas_call(kernel, out_shape=[jax.ShapeDtypeStruct(shape, jnp.float32...]
  transfers between devices with their start and end apart: 10 -> 11, of which waited for: 8 -> 8; matrix products, arithmetic and copies ran while one was open for 0% -> 0% of each run, Pallas kernels for 6% -> 6%
where the time goes in v4:
time: 30.2 us; the launch traced here: 30.1 us
  starting transfers between devices  13 us (43%)
  waiting for transfers between devices  11.9 us (39%)
  Pallas kernels  3.49 us (12%)
  local copies, waits for them, and re-layouts  1.61 us (5%)
    ppermute x3, starting transfers between devices, local(): other = lax.ppermute(factors, 'gx', pairs_across(count_x, level))  4.75 us
    ppermute x3, starting transfers between devices, local(): arrived.append(lax.ppermute(packed, 'gy', ring_of_four(count_y, step)))  4.67 us
    ppermute x3, waiting for transfers between devices, local(): arrived.append(lax.ppermute(packed, 'gy', ring_of_four(count_y, step)))  3.57 us
    pallas_call x12, Pallas kernels, call(): pl.pallas_call(kernel, out_shape=[jax.ShapeDtypeStruct(shape, jnp.float32...  3.49 us
    ppermute x2, waiting for transfers between devices, local(): other = lax.ppermute(rows, 'gx', pairs_across(count_x, level))  2.83 us
    ppermute x1, waiting for transfers between devices, local(): two = lax.ppermute(two, ('gx', 'gy'), [(b, a) for a, b in round_trip])  2.29 us
    unnamed x8, local copies, waits for them, and re-layouts  1.61 us
    ppermute x1, starting transfers between devices, local(): one = lax.ppermute(one, ('gx', 'gy'), round_trip)  1.58 us
  transfers between devices with their start and end apart: 11, of which 8 were waited for; matrix products, arithmetic and copies ran while one was open for 0% of the time, Pallas kernels for 6%

profile of v4, /device:TPU:0, one launch (start us, length us, event | category | flops | bytes accessed | tf_op | source)
XLA Modules:
  0.0 30.1 jit_solution(5167905888505177394)
XLA Ops:
  0.0 0.9 %copy-done = f32[5,8,1024]{2,1,0:T(8,128)S(1)} copy-done((f32[5,8,1024]{2,1,0:T(8,128)S(1)}, f32[5,8,1024]{2,1,0:T(8,128)}, u32[]{:S(2)}) %copy-start) | copy-done | bytes 163864
  1.0 0.7 %copy-done.2 = s32[2,32]{1,0:T(2,128)S(1)} copy-done((s32[2,32]{1,0:T(2,128)S(1)}, s32[2,32]{1,0:T(2,128)}, u32[]{:S(2)}) %copy-start.2) | copy-done | bytes 280
  1.9 0.6 %collective-permute-start.3 = (f32[22,8,128]{2,1,0:T(8,128)S(1)}, f32[22,8,128]{2,1,0:T(8,128)S(1)}, u32[]{:S(2)}, u32[]{:S(2)}) collective-permute-start(f32[22,8,128]{2,1,0:T(8,128)S(1)} %get-tuple-element.47.own_factor_ref.own_ref), channel_id=1, source_target_pairs={{0,4},{4,0},{8,12},{12,8},{16,20},{20,16},{24,28},{28,24},{1,5},{5... | collective-permute-start | bytes 270344 | tf_op jit(solution)/shard_map/ppermute | solution.py:781
  2.4 0.9 %collective-permute-done.3.other_factor_ref.other_ref = f32[22,8,128]{2,1,0:T(8,128)S(1)} collective-permute-done((f32[22,8,128]{2,1,0:T(8,128)S(1)}, f32[22,8,128]{2,1,0:T(8,128)S(1)}, u32[]{:S(2)}, u32[]{:S(2)}) %collective-permute-start.3) | collective-permute-done | bytes 90144 | tf_op jit(solution)/shard_map/ppermute | solution.py:781
  3.4 2.7 %collective-permute-start.5 = (f32[22,8,128]{2,1,0:T(8,128)S(1)}, f32[22,8,128]{2,1,0:T(8,128)S(1)}, u32[]{:S(2)}, u32[]{:S(2)}) collective-permute-start(f32[22,8,128]{2,1,0:T(8,128)S(1)} %shard_map.42.own_factor_ref.own_ref), channel_id=1, source_target_pairs={{0,12},{4,8},{8,4},{12,0},{16,28},{20,24},{24,20},{28,16},{1,13},{... | collective-permute-start | bytes 270344 | tf_op jit(solution)/shard_map/ppermute | solution.py:781
  6.1 1.6 %collective-permute-start = (f32[2,8,128]{2,1,0:T(8,128)S(1)}, f32[2,8,128]{2,1,0:T(8,128)S(1)}, u32[]{:S(2)}, u32[]{:S(2)}) collective-permute-start(f32[2,8,128]{2,1,0:T(8,128)S(1)} %get-tuple-element.38), channel_id=1, source_target_pairs={{0,1},{1,2},{2,3},{3,7},{4,0},{5,4},{6,5},{7,6},{8,9},{9,10},{10,1... | collective-permute-start | bytes 24584 | tf_op jit(solution)/shard_map/ppermute | solution.py:771
  7.6 0.4 %shard_map.39.source_ref = f32[8,5,8,128]{3,2,1,0:T(8,128)S(1)} custom-call(f32[5,64,128]{2,1,0:T(8,128)S(1)} %get-tuple-element.36.qx_ref), custom_call_target="tpu_custom_call" | custom-call | tf_op jit(solution)/shard_map/pallas_call | solution.py:722
  8.0 1.0 %collective-permute-done.one_ref = f32[2,8,128]{2,1,0:T(8,128)S(1)} collective-permute-done((f32[2,8,128]{2,1,0:T(8,128)S(1)}, f32[2,8,128]{2,1,0:T(8,128)S(1)}, u32[]{:S(2)}, u32[]{:S(2)}) %collective-permute-start) | collective-permute-done | bytes 8224 | tf_op jit(solution)/shard_map/ppermute | solution.py:771
  9.0 2.3 %collective-permute-done.1.two_ref = f32[2,8,128]{2,1,0:T(8,128)S(1)} collective-permute-done((f32[2,8,128]{2,1,0:T(8,128)S(1)}, f32[2,8,128]{2,1,0:T(8,128)S(1)}, u32[]{:S(2)}, u32[]{:S(2)}) %collective-permute-start.1) | collective-permute-done | bytes 8224 | tf_op jit(solution)/shard_map/ppermute | solution.py:772
  11.6 1.2 %collective-permute-done.2.other_ref = f32[10,8,128]{2,1,0:T(8,128)S(1)} collective-permute-done((f32[10,8,128]{2,1,0:T(8,128)S(1)}, f32[10,8,128]{2,1,0:T(8,128)S(1)}, u32[]{:S(2)}, u32[]{:S(2)}) %collective-permute-start.2) | collective-permute-done | bytes 40992 | tf_op jit(solution)/shard_map/ppermute | solution.py:796
  12.9 0.4 %collective-permute-start.4 = (f32[10,8,128]{2,1,0:T(8,128)S(1)}, f32[10,8,128]{2,1,0:T(8,128)S(1)}, u32[]{:S(2)}, u32[]{:S(2)}) collective-permute-start(f32[10,8,128]{2,1,0:T(8,128)S(1)} %get-tuple-element.48.own_ref), channel_id=1, source_target_pairs={{0,12},{4,8},{8,4},{12,0},{16,28},{20,24},{24,20},{28,16},{1,13},{... | collective-permute-start | bytes 122888 | tf_op jit(solution)/shard_map/ppermute | solution.py:796
  13.3 1.5 %collective-permute-start.7 = (f32[8,8,128]{2,1,0:T(8,128)S(1)}, f32[8,8,128]{2,1,0:T(8,128)S(1)}, u32[]{:S(2)}, u32[]{:S(2)}) collective-permute-start(f32[8,8,128]{2,1,0:T(8,128)S(1)} %shard_map.44.refs_6_), channel_id=1, source_target_pairs={{0,20},{4,16},{8,28},{12,24},{16,4},{20,0},{24,12},{28,8},{1,21},{... | collective-permute-start | bytes 98312 | tf_op jit(solution)/shard_map/ppermute | solution.py:781
  14.9 1.6 %collective-permute-done.4.other_ref = f32[10,8,128]{2,1,0:T(8,128)S(1)} collective-permute-done((f32[10,8,128]{2,1,0:T(8,128)S(1)}, f32[10,8,128]{2,1,0:T(8,128)S(1)}, u32[]{:S(2)}, u32[]{:S(2)}) %collective-permute-start.4) | collective-permute-done | bytes 40992 | tf_op jit(solution)/shard_map/ppermute | solution.py:796
  16.6 1.6 %collective-permute-start.6 = (f32[5,8,128]{2,1,0:T(8,128)S(1)}, f32[5,8,128]{2,1,0:T(8,128)S(1)}, u32[]{:S(2)}, u32[]{:S(2)}) collective-permute-start(f32[5,8,128]{2,1,0:T(8,128)S(1)} %get-tuple-element.49.refs_4_), channel_id=1, source_target_pairs={{0,20},{4,16},{8,28},{12,24},{16,4},{20,0},{24,12},{28,8},{1,21},{... | collective-permute-start | bytes 61448 | tf_op jit(solution)/shard_map/ppermute | solution.py:803
  18.1 0.5 %shard_map.45 = (f32[4,8,128]{2,1,0:T(8,128)S(1)}, f32[8,3,8,128]{3,2,1,0:T(8,128)S(1)}, f32[8,3,8,128]{3,2,1,0:T(8,128)S(1)}, f32[8,3,8,128]{3,2,1,0:T(8,128)S(...) custom-call(f32[5,8,1024]{2,1,0:T(8,128)S(1)} %copy-done.1, ...), custom_call_target="tpu_custom_call" | custom-call | tf_op jit(solution)/shard_map/pallas_call | solution.py:722
  18.6 1.2 %collective-permute-done.6.refs_5_ = f32[5,8,128]{2,1,0:T(8,128)S(1)} collective-permute-done((f32[5,8,128]{2,1,0:T(8,128)S(1)}, f32[5,8,128]{2,1,0:T(8,128)S(1)}, u32[]{:S(2)}, u32[]{:S(2)}) %collective-permute-start.6) | collective-permute-done | bytes 20512 | tf_op jit(solution)/shard_map/ppermute | solution.py:803
  19.9 0.4 %shard_map.46 = (f32[8,8,128]{2,1,0:T(8,128)S(1)}, f32[8,5,8,128]{3,2,1,0:T(8,128)S(1)}, f32[2,5,8,128]{3,2,1,0:T(8,128)S(1)}) custom-call(f32[8,2,8,128]{3,2,1,0:T(8,128)S(1)} %get-tuple-element.37.refs_0_, f32[8,5,8,128]{3,2,1,0:T(8,128)S(1)} %get-tuple-element.43.refs_1_, f32[8,3,8,128]{3,2,1,0:T(8,128)S(1)} %get-tuple-element.44.refs_2_, ...), custom_call_target="tpu_custom_call" | custom-call | tf_op jit(solution)/shard_map/pallas_call | solution.py:722
  20.3 2.1 %collective-permute-start.10 = (f32[8,8,128]{2,1,0:T(8,128)S(1)}, f32[8,8,128]{2,1,0:T(8,128)S(1)}, u32[]{:S(2)}, u32[]{:S(2)}) collective-permute-start(f32[8,8,128]{2,1,0:T(8,128)S(1)} %get-tuple-element.66.refs_5_), channel_id=1, source_target_pairs={{0,3},{1,0},{2,1},{3,2},{4,7},{5,4},{6,5},{7,6},{8,11},{9,8},{10,9... | collective-permute-start | bytes 98312 | tf_op jit(solution)/shard_map/ppermute | solution.py:828
  22.4 1.0 %collective-permute-start.9 = (f32[8,8,128]{2,1,0:T(8,128)S(1)}, f32[8,8,128]{2,1,0:T(8,128)S(1)}, u32[]{:S(2)}, u32[]{:S(2)}) collective-permute-start(f32[8,8,128]{2,1,0:T(8,128)S(1)} %get-tuple-element.66.refs_5_), channel_id=1, source_target_pairs={{0,2},{1,3},{2,0},{3,1},{4,6},{5,7},{6,4},{7,5},{8,10},{9,11},{10,... | collective-permute-start | bytes 98312 | tf_op jit(solution)/shard_map/ppermute | solution.py:828
  23.4 1.6 %collective-permute-start.8 = (f32[8,8,128]{2,1,0:T(8,128)S(1)}, f32[8,8,128]{2,1,0:T(8,128)S(1)}, u32[]{:S(2)}, u32[]{:S(2)}) collective-permute-start(f32[8,8,128]{2,1,0:T(8,128)S(1)} %get-tuple-element.66.refs_5_), channel_id=1, source_target_pairs={{0,1},{1,2},{2,3},{3,0},{4,5},{5,6},{6,7},{7,4},{8,9},{9,10},{10,1... | collective-permute-start | bytes 98312 | tf_op jit(solution)/shard_map/ppermute | solution.py:828
  25.0 0.5 %shard_map.47 = (f32[8,11,8,128]{3,2,1,0:T(8,128)S(1)}, f32[8,6,8,128]{3,2,1,0:T(8,128)S(1)}, f32[2,11,8,128]{3,2,1,0:T(8,128)S(1)}, f32[4,11,8,128]{3,2,1,0:T(8,128)S(1)}) custom-call(f32[5,8,1024]{2,1,0:T(8,128)S(1)} %copy-done.1, f32[8,5,8,128]{3,2,1,0:T(8,128)S(1)} %get-tuple-element.57.yown_ref, f32[8,3,8,128]{3,2,1,0:T(8,128)S(1)} %get-tuple-element.58.yleft_ref, ...), custom_call_target="tpu_custom_call" | custom-call | tf_op jit(solution)/shard_map/pallas_call | solution.py:722
  25.5 1.7 %collective-permute-done.9.refs_7_ = f32[8,8,128]{2,1,0:T(8,128)S(1)} collective-permute-done((f32[8,8,128]{2,1,0:T(8,128)S(1)}, f32[8,8,128]{2,1,0:T(8,128)S(1)}, u32[]{:S(2)}, u32[]{:S(2)}) %collective-permute-start.9) | collective-permute-done | bytes 32800 | tf_op jit(solution)/shard_map/ppermute | solution.py:828
  27.2 1.9 %collective-permute-done.8.refs_6_ = f32[8,8,128]{2,1,0:T(8,128)S(1)} collective-permute-done((f32[8,8,128]{2,1,0:T(8,128)S(1)}, f32[8,8,128]{2,1,0:T(8,128)S(1)}, u32[]{:S(2)}, u32[]{:S(2)}) %collective-permute-start.8) | collective-permute-done | bytes 32800 | tf_op jit(solution)/shard_map/ppermute | solution.py:828
  29.1 0.9 %shard_map.48 = f32[5,8,1024]{2,1,0:T(8,128)} custom-call(f32[5,8,1024]{2,1,0:T(8,128)S(1)} %copy-done.1, f32[8,11,8,128]{3,2,1,0:T(8,128)S(1)} %get-tuple-element.62.refs_1_, f32[8,6,8,128]{3,2,1,0:T(8,128)S(1)} %get-tuple-element.63.refs_2_, f32[2,11,8,128]{3,2,1,0:T(8,128)S(1)} %get-tuple-element.64.refs_3_, ...), custom_call_target="tpu_custom_call" | custom-call | tf_op jit(solution)/shard_map/pallas_call | solution.py:722
  (18 shorter events, 0.8 us)
Async XLA Ops:
  0.0 0.9 %copy-start = (f32[5,8,1024]{2,1,0:T(8,128)S(1)}, f32[5,8,1024]{2,1,0:T(8,128)}, u32[]{:S(2)}) copy-start(f32[5,8,1024]{2,1,0:T(8,128)} %refs_0_.1) | copy-start | bytes 491524
  1.0 0.7 %copy-start.2 = (s32[2,32]{1,0:T(2,128)S(1)}, s32[2,32]{1,0:T(2,128)}, u32[]{:S(2)}) copy-start(s32[2,32]{1,0:T(2,128)} %codes_ref.2) | copy-start | bytes 772
  1.9 1.5 %collective-permute-start.3 = (f32[22,8,128]{2,1,0:T(8,128)S(1)}, f32[22,8,128]{2,1,0:T(8,128)S(1)}, u32[]{:S(2)}, u32[]{:S(2)}) collective-permute-start(f32[22,8,128]{2,1,0:T(8,128)S(1)} %get-tuple-element.47.own_factor_ref.own_ref), channel_id=1, source_target_pairs={{0,4},{4,0},{8,12},{12,8},{16,20},{20,16},{24,28},{28,24},{1,5},{5... | collective-permute-start | bytes 270344 | tf_op jit(solution)/shard_map/ppermute | solution.py:781
  3.4 9.9 %collective-permute-start.5 = (f32[22,8,128]{2,1,0:T(8,128)S(1)}, f32[22,8,128]{2,1,0:T(8,128)S(1)}, u32[]{:S(2)}, u32[]{:S(2)}) collective-permute-start(f32[22,8,128]{2,1,0:T(8,128)S(1)} %shard_map.42.own_factor_ref.own_ref), channel_id=1, source_target_pairs={{0,12},{4,8},{8,4},{12,0},{16,28},{20,24},{24,20},{28,16},{1,13},{... | collective-permute-start | bytes 270344 | tf_op jit(solution)/shard_map/ppermute | solution.py:781
  6.1 2.9 %collective-permute-start = (f32[2,8,128]{2,1,0:T(8,128)S(1)}, f32[2,8,128]{2,1,0:T(8,128)S(1)}, u32[]{:S(2)}, u32[]{:S(2)}) collective-permute-start(f32[2,8,128]{2,1,0:T(8,128)S(1)} %get-tuple-element.38), channel_id=1, source_target_pairs={{0,1},{1,2},{2,3},{3,7},{4,0},{5,4},{6,5},{7,6},{8,9},{9,10},{10,1... | collective-permute-start | bytes 24584 | tf_op jit(solution)/shard_map/ppermute | solution.py:771
  7.6 3.7 %copy-start.1 = (f32[5,8,1024]{2,1,0:T(8,128)S(1)}, f32[5,8,1024]{2,1,0:T(8,128)}, u32[]{:S(2)}) copy-start(f32[5,8,1024]{2,1,0:T(8,128)} %refs_0_.1) | copy-start | bytes 491524
  7.6 3.7 %collective-permute-start.1 = (f32[2,8,128]{2,1,0:T(8,128)S(1)}, f32[2,8,128]{2,1,0:T(8,128)S(1)}, u32[]{:S(2)}, u32[]{:S(2)}) collective-permute-start(f32[2,8,128]{2,1,0:T(8,128)S(1)} %get-tuple-element.39), channel_id=1, source_target_pairs={{1,0},{2,1},{3,2},{7,3},{0,4},{4,5},{5,6},{6,7},{9,8},{10,9},{11,1... | collective-permute-start | bytes 24584 | tf_op jit(solution)/shard_map/ppermute | solution.py:772
  11.6 1.3 %collective-permute-start.2 = (f32[10,8,128]{2,1,0:T(8,128)S(1)}, f32[10,8,128]{2,1,0:T(8,128)S(1)}, u32[]{:S(2)}, u32[]{:S(2)}) collective-permute-start(f32[10,8,128]{2,1,0:T(8,128)S(1)} %get-tuple-element.46.own_ref), channel_id=1, source_target_pairs={{0,4},{4,0},{8,12},{12,8},{16,20},{20,16},{24,28},{28,24},{1,5},{5... | collective-permute-start | bytes 122888 | tf_op jit(solution)/shard_map/ppermute | solution.py:796
  12.9 3.6 %collective-permute-start.4 = (f32[10,8,128]{2,1,0:T(8,128)S(1)}, f32[10,8,128]{2,1,0:T(8,128)S(1)}, u32[]{:S(2)}, u32[]{:S(2)}) collective-permute-start(f32[10,8,128]{2,1,0:T(8,128)S(1)} %get-tuple-element.48.own_ref), channel_id=1, source_target_pairs={{0,12},{4,8},{8,4},{12,0},{16,28},{20,24},{24,20},{28,16},{1,13},{... | collective-permute-start | bytes 122888 | tf_op jit(solution)/shard_map/ppermute | solution.py:796
  13.3 6.5 %collective-permute-start.7 = (f32[8,8,128]{2,1,0:T(8,128)S(1)}, f32[8,8,128]{2,1,0:T(8,128)S(1)}, u32[]{:S(2)}, u32[]{:S(2)}) collective-permute-start(f32[8,8,128]{2,1,0:T(8,128)S(1)} %shard_map.44.refs_6_), channel_id=1, source_target_pairs={{0,20},{4,16},{8,28},{12,24},{16,4},{20,0},{24,12},{28,8},{1,21},{... | collective-permute-start | bytes 98312 | tf_op jit(solution)/shard_map/ppermute | solution.py:781
  16.6 1.6 %copy-start.3 = (s32[2,8]{1,0:T(2,128)S(1)}, s32[2,8]{1,0:T(2,128)}, u32[]{:S(2)}) copy-start(s32[2,8]{1,0:T(2,128)} %codes_ref.3) | copy-start | bytes 196
  16.6 3.3 %collective-permute-start.6 = (f32[5,8,128]{2,1,0:T(8,128)S(1)}, f32[5,8,128]{2,1,0:T(8,128)S(1)}, u32[]{:S(2)}, u32[]{:S(2)}) collective-permute-start(f32[5,8,128]{2,1,0:T(8,128)S(1)} %get-tuple-element.49.refs_4_), channel_id=1, source_target_pairs={{0,20},{4,16},{8,28},{12,24},{16,4},{20,0},{24,12},{28,8},{1,21},{... | collective-permute-start | bytes 61448 | tf_op jit(solution)/shard_map/ppermute | solution.py:803
  20.3 5.2 %collective-permute-start.10 = (f32[8,8,128]{2,1,0:T(8,128)S(1)}, f32[8,8,128]{2,1,0:T(8,128)S(1)}, u32[]{:S(2)}, u32[]{:S(2)}) collective-permute-start(f32[8,8,128]{2,1,0:T(8,128)S(1)} %get-tuple-element.66.refs_5_), channel_id=1, source_target_pairs={{0,3},{1,0},{2,1},{3,2},{4,7},{5,4},{6,5},{7,6},{8,11},{9,8},{10,9... | collective-permute-start | bytes 98312 | tf_op jit(solution)/shard_map/ppermute | solution.py:828
  22.4 4.8 %collective-permute-start.9 = (f32[8,8,128]{2,1,0:T(8,128)S(1)}, f32[8,8,128]{2,1,0:T(8,128)S(1)}, u32[]{:S(2)}, u32[]{:S(2)}) collective-permute-start(f32[8,8,128]{2,1,0:T(8,128)S(1)} %get-tuple-element.66.refs_5_), channel_id=1, source_target_pairs={{0,2},{1,3},{2,0},{3,1},{4,6},{5,7},{6,4},{7,5},{8,10},{9,11},{10,... | collective-permute-start | bytes 98312 | tf_op jit(solution)/shard_map/ppermute | solution.py:828
  23.4 5.7 %collective-permute-start.8 = (f32[8,8,128]{2,1,0:T(8,128)S(1)}, f32[8,8,128]{2,1,0:T(8,128)S(1)}, u32[]{:S(2)}, u32[]{:S(2)}) collective-permute-start(f32[8,8,128]{2,1,0:T(8,128)S(1)} %get-tuple-element.66.refs_5_), channel_id=1, source_target_pairs={{0,1},{1,2},{2,3},{3,0},{4,5},{5,6},{6,7},{7,4},{8,9},{9,10},{10,1... | collective-permute-start | bytes 98312 | tf_op jit(solution)/shard_map/ppermute | solution.py:828

commit v5 on v4

--- a/solution.py
+++ b/solution.py
@@ -180,29 +180,25 @@
     return joined, before[-10:-5], after[-5:]
 
 
-def last_join(own, other, speed_of):
-    fields = len(speed_of)
-    result = []
-    for f in range(fields):
-        k = fields + speed_of[f]
-        result.append((other[f] + other[k] * own[f]) / (1.0 - own[k] * other[k]))
-    return result
-
-
-def last_join_forced(low, own, other):
+def last_factors_kernel(level, own_ref, other_ref, out_ref):
+    low = bit_low("gx", level)
+    own, other = load(own_ref), load(other_ref)
     before = [jnp.where(low, a, b) for a, b in zip(own, other)]
     after = [jnp.where(low, b, a) for a, b in zip(own, other)]
-    h_b, u_b, h_a, l_a = join_factors(before[8:], after[8:])
+    h_b, u_b, h_a, l_a = join_factors(before[3:], after[3:])
     h_own = [jnp.where(low, a, b) for a, b in zip(h_b, h_a)]
     h_other = [jnp.where(low, b, a) for a, b in zip(h_b, h_a)]
     k_own = [jnp.where(low, a, b) for a, b in zip(u_b, l_a)]
     k_other = [jnp.where(low, b, a) for a, b in zip(u_b, l_a)]
-    mine, theirs = [], []
-    for rows, h, k, out in ((own, h_own, k_own, mine), (other, h_other, k_other, theirs)):
-        out.extend(rows[f] + rows[5 + SPEED_OF[f]] * h[f] for f in range(5))
-        out.extend(rows[5 + n] * k[n] for n in range(3))
-    value = last_join(mine, theirs, SPEED_OF)
-    return [h_own[f] + k_own[SPEED_OF[f]] * value[f] for f in range(5)]
+    mine = [own[k] * k_own[k] for k in range(3)]
+    theirs = [other[k] * k_other[k] for k in range(3)]
+    of_other = [k_own[k] / (1.0 - mine[k] * theirs[k]) for k in range(3)]
+    of_own = [of_other[k] * theirs[k] for k in range(3)]
+    constant = []
+    for f in range(5):
+        k = SPEED_OF[f]
+        constant.append(h_own[f] + of_other[k] * (other[k] * h_other[f]) + of_own[k] * (own[k] * h_own[f]))
+    store(out_ref, constant + of_other + of_own)
 
 
 def step_down(low, side, outer, speed_of):
@@ -306,7 +302,7 @@
 
 
 def x_factor_kernel(
-    qx_ref, codes_ref, out_ref, inverse_ref, lower_ref, up_ref, left_ref, right_ref, points_ref
+    qx_ref, codes_ref, out_ref, inverse_ref, lower_ref, up_ref, left_ref, right_ref, points_ref, weight_ref
 ):
     cells = inverse_ref.shape[0]
     chunks = inverse_ref.shape[2]
@@ -326,11 +322,14 @@
     for ref, values in zip((inverse_ref, lower_ref, up_ref, left_ref, right_ref), parts):
         for i in range(cells):
             store(ref.at[i], values[i])
+    weights = [part_weights(*parts[:3], k) for k in range(3)]
+    for i in range(cells):
+        store(weight_ref.at[i], [weights[k][side][i] for side in range(2) for k in range(3)])
     lefts, rights = parts[3:]
     store(out_ref, lefts[0] + rights[0] + lefts[-1] + rights[-1] + rows[0] + rows[-1])
 
 
-def x_source_kernel(qx_ref, out_ref):
+def x_source_kernel(qx_ref, weight_ref, out_ref, ends_ref):
     cells = out_ref.shape[0]
     chunks = out_ref.shape[2]
     lane = lax.broadcasted_iota(jnp.int32, (chunks, LANES), 1)
@@ -358,6 +357,7 @@
         before = jnp.where(z_of == 0, pltpu.roll(value, LANES - NZ + 1, 1), pltpu.roll(value, 1, 1))
         return after - before
 
+    ends = None
     for i in range(cells):
         q = rows[i + 1]
         _, _, vel_v, vel_w, _, pressure, _ = prims[i]
@@ -375,23 +375,26 @@
             )
             smooth = rows[i + 2][f] + rows[i][f] + after[f] + before[f] - 4.0 * q[f]
             res.append(-0.5 * SIGMA * change + DIFFUSE * smooth)
-        store(out_ref.at[i], x_characteristics(res, q[0], prims[i]))
-
-
-def x_kernel(
-    flow_ref, one_ref, two_ref, source_ref, inverse_ref, lower_ref, up_ref,
-    rows_ref, own_ref, low_ref, high_ref,
-):
+        source = x_characteristics(res, q[0], prims[i])
+        store(out_ref.at[i], source)
+        parts = [weight_ref[i, 3 * side + SPEED_OF[f]] * source[f] for side in range(2) for f in range(5)]
+        ends = parts if ends is None else [a + b for a, b in zip(ends, parts)]
+    store(ends_ref, ends)
+
+
+def y_edge_mask(chunks):
+    lane = lax.broadcasted_iota(jnp.int32, (chunks, LANES), 1)
+    sub = lax.broadcasted_iota(jnp.int32, (chunks, LANES), 0)
+    high = jnp.logical_and(sub == chunks - 1, lane >= LANES - NZ)
+    return jnp.logical_or(high, jnp.logical_and(sub == 0, lane < NZ))
+
+
+def x_kernel(flow_ref, one_ref, two_ref, weight_ref, ends_ref, rows_ref, extra_ref):
     cells = flow_ref.shape[1]
     chunks = flow_ref.shape[2] // LANES
-    lane = lax.broadcasted_iota(jnp.int32, (chunks, LANES), 1)
-    sub = lax.broadcasted_iota(jnp.int32, (chunks, LANES), 0)
-    up_edge = jnp.logical_and(sub == chunks - 1, lane >= LANES - NZ)
-    down_edge = jnp.logical_and(sub == 0, lane < NZ)
     lows, highs = zip(*[y_halos(flow_ref, one_ref, two_ref, f) for f in range(5)])
-    for ghosts, at, turn, sign, ref in (
-        (lows, 0, NZ, 1.0, low_ref), (highs, chunks - 1, LANES - NZ, -1.0, high_ref)
-    ):
+    extras = []
+    for ghosts, at, turn, sign in ((lows, 0, NZ, 1.0), (highs, chunks - 1, LANES - NZ, -1.0)):
         ghosts = [pltpu.roll(g, turn, 1) for g in ghosts]
         inner = [flow_ref[f, :, at * LANES : (at + 1) * LANES] for f in range(5)]
         ghost_prim, prim = primitives(ghosts), primitives(inner)
@@ -401,20 +404,28 @@
             sign * 0.5 * SIGMA * (ghost_flux[f] - inner_flux[f]) + DIFFUSE * (ghosts[f] - inner[f])
             for f in range(5)
         ]
-        store(ref, x_characteristics(res, inner[0], prim))
+        extras.append(x_characteristics(res, inner[0], prim))
+    lane = lax.broadcasted_iota(jnp.int32, (cells, LANES), 1)
+    store(extra_ref, [jnp.where(lane < LANES // 2, low, high) for low, high in zip(*extras)])
+    edge = y_edge_mask(chunks)
+    added = None
+    for i in range(cells):
+        extra = [jnp.broadcast_to(extra_ref[f, i : i + 1, :], (chunks, LANES)) for f in range(5)]
+        parts = [weight_ref[i, 3 * side + SPEED_OF[f]] * extra[f] for side in range(2) for f in range(5)]
+        added = parts if added is None else [a + b for a, b in zip(added, parts)]
+    store(rows_ref, [ends_ref[n] + jnp.where(edge, value, 0.0) for n, value in enumerate(added)])
+
+
+def x_own_kernel(source_ref, extra_ref, inverse_ref, lower_ref, up_ref, own_ref):
+    cells, chunks = source_ref.shape[0], source_ref.shape[2]
+    edge = y_edge_mask(chunks)
     sources = []
     for i in range(cells):
-        source = []
-        for f in range(5):
-            low = jnp.broadcast_to(low_ref[f, i : i + 1, :], (chunks, LANES))
-            high = jnp.broadcast_to(high_ref[f, i : i + 1, :], (chunks, LANES))
-            extra = jnp.where(down_edge, low, 0.0) + jnp.where(up_edge, high, 0.0)
-            source.append(source_ref[i, f] + extra)
-        sources.append(source)
+        extra = [jnp.broadcast_to(extra_ref[f, i : i + 1, :], (chunks, LANES)) for f in range(5)]
+        sources.append([source_ref[i, f] + jnp.where(edge, extra[f], 0.0) for f in range(5)])
     owns = substitute(*([load(ref.at[i]) for i in range(cells)] for ref in (inverse_ref, lower_ref, up_ref)), sources)
     for i in range(cells):
         store(own_ref.at[i], owns[i])
-    store(rows_ref, owns[0] + owns[-1])
 
 
 def load(ref):
@@ -456,9 +467,12 @@
     store(side_ref, side)
 
 
-def outer_values(levels, own, other, side_refs):
+def outer_values(levels, own, other, factors, side_refs):
     low = bit_low("gx", levels - 1)
-    outer = from_last(low, last_join_forced(low, own, other))
+    new = [
+        factors[f] + factors[5 + SPEED_OF[f]] * other[f] + factors[8 + SPEED_OF[f]] * own[f] for f in range(5)
+    ]
+    outer = from_last(low, new)
     for level in range(levels - 2, -1, -1):
         outer = step_down(bit_low("gx", level), load(side_refs[level]), outer, SPEED_OF)
     return outer
@@ -526,7 +540,7 @@
 
 def y_factor_kernel(
     flow_ref, one_ref, two_ref, codes_ref,
-    packed_ref, inverse_ref, lower_ref, up_ref, left_ref, right_ref, join_ref, side_ref,
+    packed_ref, inverse_ref, lower_ref, up_ref, left_ref, right_ref, join_ref, side_ref, weight_ref,
 ):
     cells = flow_ref.shape[1]
     chunks = flow_ref.shape[2] // LANES
@@ -566,18 +580,63 @@
         ends, e, f = join(([], [], b_f, c_f, b_e, c_e), ([], [], b_g, c_g, b_h, c_h), ())
         store(side_ref.at[level], [jnp.where(low, b, a) for a, b in zip(e, f)])
     store(packed_ref, [four(group, t[0], t[1], t[2], t[1]) for t in (ends[3 * n : 3 * n + 3] for n in range(4))])
+    weights = end_weights(group, parts, [load(join_ref.at[level]) for level in range(2)])
+    for c in range(chunks):
+        store(weight_ref.at[c], [ungroup(column, c, group) for column in weights])
+
+
+def part_weights(inverses, lowers, ups, k):
+    steps = len(inverses)
+    reach = [None] * steps
+    passed = None
+    for i in range(steps):
+        reach[i] = passed
+        passed = -ups[i][k] if passed is None else -passed * ups[i][k]
+    first_w, last_w = [None] * steps, [None] * steps
+    ahead_first, ahead_last = reach[-1], None
+    for i in range(steps - 1, -1, -1):
+        if i == steps - 1:
+            last_w[i] = inverses[i][k]
+        else:
+            ahead_first = -lowers[i + 1][k] * ahead_first
+            ahead_first = ahead_first + (1.0 if i == 0 else reach[i])
+            ahead_last = -lowers[i + 1][k] if ahead_last is None else -lowers[i + 1][k] * ahead_last
+            last_w[i] = ahead_last * inverses[i][k]
+        first_w[i] = ahead_first * inverses[i][k]
+    return first_w, last_w
+
+
+def end_weights(group, parts, joins):
+    columns = []
+    for k in range(3):
+        first_w, last_w = part_weights(*parts[:3], k)
+        steps = len(first_w)
+        shares = []
+        for level in range(2):
+            inv, c_e, b_g, c_f, b_h = (joins[level][3 * n + k] for n in range(5))
+            low = lane_low(group, level)
+            one, zero = jnp.ones_like(inv), jnp.zeros_like(inv)
+            shares.append((
+                jnp.where(low, one, c_f * inv),
+                jnp.where(low, c_f * b_g * inv, zero),
+                jnp.where(low, zero, b_h * c_e * inv),
+                jnp.where(low, b_h * inv, one),
+            ))
+        (ff, lf, fl, ll), (top_ff, top_lf, top_fl, top_ll) = shares
+        for top_first, top_last in ((top_ff, top_lf), (top_fl, top_ll)):
+            share_first = top_first * ff + top_last * fl
+            share_last = top_first * lf + top_last * ll
+            columns.append([share_first * first_w[i] + share_last * last_w[i] for i in range(steps)])
+    return columns[0::2] + columns[1::2]
 
 
 def y_kernel(levels, *refs):
-    (points_ref, own_ref, left_ref, right_ref, mine_ref, other_ref, mine_factor_ref, other_factor_ref,
-     packed_ref, inverse_ref, lower_ref, up_ref, join_ref) = refs[:13]
-    sides = refs[13 : 13 + levels - 1]
-    out_ref, yown_ref, side_ref, turn_ref = refs[13 + levels - 1 :]
+    (points_ref, own_ref, left_ref, right_ref, mine_ref, other_ref, last_ref, packed_ref, weight_ref) = refs[:9]
+    sides = refs[9 : 9 + levels - 1]
+    out_ref, turn_ref = refs[9 + levels - 1 :]
     chunks = own_ref.shape[2]
     cells = own_ref.shape[0]
-    steps = chunks
-    mine, other = load(mine_ref) + load(mine_factor_ref), load(other_ref) + load(other_factor_ref)
-    outer_l, outer_r = outer_values(levels, mine, other, sides)
+    outer_l, outer_r = outer_values(levels, load(mine_ref), load(other_ref), load(last_ref), sides)
     for i in range(cells):
         impedance, half_admittance = load(points_ref.at[i])
         wave = [
@@ -590,17 +649,35 @@
         values = [dp - normal, wave[1], du, wave[3], dp + normal]
         for n, value in enumerate(values):
             turn_ref[n, i * chunks : (i + 1) * chunks, :] = value
-    lane = lax.broadcasted_iota(jnp.int32, (cells, LANES), 1)
-    group = lane // NZ
+    group = lax.broadcasted_iota(jnp.int32, (cells, LANES), 1) // NZ
+    ends = []
+    for side in range(2):
+        for f in range(5):
+            terms = [
+                turn_ref[f, pl.ds(c, cells, stride=chunks), :] * weight_ref[c, 3 * side + SPEED_OF[f]]
+                for c in range(chunks)
+            ]
+            while len(terms) > 1:
+                terms = [a + b for a, b in zip(terms[0::2], terms[1::2])] + terms[len(terms) // 2 * 2 :]
+            ends.append(terms[0])
+    ends = [v + pltpu.roll(v, LANES // 2, 1) for v in ends]
+    ends = [v + pltpu.roll(v, NZ, 1) for v in ends]
+    rows = []
+    for a in (ends[:5], ends[5:]):
+        rows += [four(group, a[0], a[1], a[4], a[2]), a[3]]
+    store(out_ref, rows + load(packed_ref))
+
+
+def y_sweep(turn_ref, cells, group, factor_refs, join_ref):
+    chunks = turn_ref.shape[1] // cells
     fields = [
         regroup([turn_ref[n, pl.ds(c, cells, stride=chunks), :] for c in range(chunks)], group)
         for n in range(5)
     ]
-    sources = [[fields[f][jj] for f in range(5)] for jj in range(steps)]
-    owns = substitute(*([load(ref.at[i]) for i in range(steps)] for ref in (inverse_ref, lower_ref, up_ref)), sources)
-    for i in range(steps):
-        store(yown_ref.at[i], owns[i])
+    sources = [[fields[f][jj] for f in range(5)] for jj in range(chunks)]
+    owns = substitute(*([load(ref.at[i]) for i in range(chunks)] for ref in factor_refs), sources)
     a_f, a_e = owns[0], owns[-1]
+    sides = []
     for level in range(2):
         low = lane_low(group, level)
         other = lane_partner(a_f + a_e, group, level)
@@ -616,11 +693,8 @@
             new_f.append(before[n] + c_f[k] * f[n])
             new_e.append(after[5 + n] + b_h[k] * e[n])
         a_f, a_e = new_f, new_e
-        store(side_ref.at[level], [jnp.where(low, b, a) for a, b in zip(e, f)])
-    rows = []
-    for a in (a_f, a_e):
-        rows += [four(group, a[0], a[1], a[4], a[2]), a[3]]
-    store(out_ref, rows + load(packed_ref))
+        sides.append([jnp.where(low, b, a) for a, b in zip(e, f)])
+    return owns, sides
 
 
 def four(group, a, b, c, d):
@@ -646,15 +720,15 @@
 
 
 def prepare_kernel(
-    flow_ref, yown_ref, yleft_ref, yright_ref, ends_ref, side_ref,
+    flow_ref, turn_ref, inverse_ref, lower_ref, up_ref, join_ref, yleft_ref, yright_ref, side_ref,
     terms_ref, points_ref, half_ref, quarter_ref,
 ):
     cells = flow_ref.shape[1]
     chunks = flow_ref.shape[2] // LANES
     group = lax.broadcasted_iota(jnp.int32, (cells, LANES), 1) // NZ
-    columns = [
-        [ref[j, n] for j in range(chunks)]
-        for ref in (yown_ref, yleft_ref, yright_ref) for n in range(ref.shape[1])
+    owns, ends = y_sweep(turn_ref, cells, group, (inverse_ref, lower_ref, up_ref), join_ref)
+    columns = [[own[n] for own in owns] for n in range(5)] + [
+        [ref[j, n] for j in range(chunks)] for ref in (yleft_ref, yright_ref) for n in range(3)
     ]
     for c in range(chunks):
         store(terms_ref.at[c], [ungroup(column, c, group) for column in columns])
@@ -665,7 +739,7 @@
             [vel_u, vel_v, vel_w, kinetic, 1.0 / (2.0 * q[0] * sound), 1.0 / (sound * sound)],
         )
     for level, ref, count in ((1, half_ref, 2), (0, quarter_ref, GROUPS)):
-        rows = load(ends_ref.at[level]) + load(side_ref.at[level])
+        rows = ends[level] + load(side_ref.at[level])
         for n in range(count):
             store(ref.at[n], [spread(group, row, n * GROUPS // count) for row in rows])
 
@@ -771,11 +845,11 @@
     one = lax.ppermute(one, ("gx", "gy"), round_trip)
     two = lax.ppermute(two, ("gx", "gy"), [(b, a) for a, b in round_trip])
 
-    factors, inverse, lower, upper, left, right, xpoints = call(
+    factors, inverse, lower, upper, left, right, xpoints, xweight = call(
         x_factor_kernel, [qx, x_codes],
-        [(COEFS + 10,) + tile_x] + [(cells, 3) + tile_x] * 5 + [(cells, 2) + tile_x],
-    )
-    (source,) = call(x_source_kernel, [qx], [(cells, 5) + tile_x])
+        [(COEFS + 10,) + tile_x] + [(cells, 3) + tile_x] * 5 + [(cells, 2) + tile_x, (cells, 6) + tile_x],
+    )
+    source, ends = call(x_source_kernel, [qx, xweight], [(cells, 5) + tile_x, (10,) + tile_x])
     all_factors = []
     for level in range(levels_x):
         other = lax.ppermute(factors, "gx", pairs_across(count_x, level))
@@ -786,10 +860,11 @@
                 functools.partial(x_merge_factor_kernel, level, final),
                 [factors, other], [(8 if final else COEFS + 10,) + tile_x],
             )
-    rows, own = call(
-        x_kernel, [flow, one, two, source, inverse, lower, upper],
-        [(10,) + tile_x, (cells, 5) + tile_x],
-        [pltpu.VMEM((5,) + tile_y, jnp.float32), pltpu.VMEM((5,) + tile_y, jnp.float32)],
+    rows, extra = call(x_kernel, [flow, one, two, xweight, ends], [(10,) + tile_x, (5,) + tile_y])
+    (own,) = call(x_own_kernel, [source, extra, inverse, lower, upper], [(cells, 5) + tile_x])
+    (last,) = call(
+        functools.partial(last_factors_kernel, levels_x - 1), [*all_factors[-1]],
+        [(11,) + tile_x],
     )
     sides = []
     for level in range(levels_x - 1):
@@ -801,18 +876,17 @@
         )
         sides.append(side_rows)
     other = lax.ppermute(rows, "gx", pairs_across(count_x, levels_x - 1))
-    y_factors, yinverse, ylower, yup, yleft, yright, yjoin, yside = call(
+    y_factors, yinverse, ylower, yup, yleft, yright, yjoin, yside, yweight = call(
         y_factor_kernel, [flow, one, two, y_codes],
-        [(4,) + tile_y] + [(chunks, 3) + tile_y] * 5 + [(2, 15) + tile_y, (2, 6) + tile_y],
-    )
-    packed, yown, yends = call(
+        [(4,) + tile_y] + [(chunks, 3) + tile_y] * 5 + [(2, 15) + tile_y, (2, 6) + tile_y, (chunks, 6) + tile_y],
+    )
+    packed, turn = call(
         functools.partial(y_kernel, levels_x),
-        [xpoints, own, left, right, rows, other, *all_factors[-1], y_factors, yinverse, ylower, yup, yjoin] + sides,
-        [(8,) + tile_y, (chunks, 5) + tile_y, (2, 5) + tile_y],
-        [pltpu.VMEM((5, cells * chunks, LANES), jnp.float32)],
+        [xpoints, own, left, right, rows, other, last, y_factors, yweight] + sides,
+        [(8,) + tile_y, (5, cells * chunks, LANES)],
     )
     prepared = call(
-        prepare_kernel, [flow, yown, yleft, yright, yends, yside],
+        prepare_kernel, [flow, turn, yinverse, ylower, yup, yjoin, yleft, yright, yside],
         [(chunks, 11) + tile_y, (chunks, 6) + tile_y, (2, 11) + tile_y, (GROUPS, 11) + tile_y],
     )
     sides = []

time: 30.2 us -> 30 us (level)
  waiting for transfers between devices: 11.9 us -> 10.7 us
  local copies, waits for them, and re-layouts: 1.61 us -> 2.21 us
  Pallas kernels: 3.49 us -> 3.86 us
    ppermute x1, waiting for transfers between devices: 1.24 us -> 0.32 us  [local(): other = lax.ppermute(rows, 'gx', pairs_across(count_x, levels_x - 1))]
    unnamed x8, local copies, waits for them, and re-layouts: 1.61 us -> 2.21 us
    pallas_call x12 -> x14, Pallas kernels: 3.49 us -> 3.86 us  [call(): pl.pallas_call(kernel, out_shape=[jax.ShapeDtypeStruct(shape, jnp.float32...]
  transfers between devices with their start and end apart: 11 -> 11, of which waited for: 8 -> 8; matrix products, arithmetic and copies ran while one was open for 0% -> 0% of each run, Pallas kernels for 6% -> 8%
where the time goes in v5:
time: 30 us; the launch traced here: 29.8 us
  starting transfers between devices  13 us (43%)
  waiting for transfers between devices  10.7 us (36%)
  Pallas kernels  3.86 us (13%)
  local copies, waits for them, and re-layouts  2.21 us (7%)
    ppermute x3, starting transfers between devices, local(): other = lax.ppermute(factors, 'gx', pairs_across(count_x, level))  4.75 us
    ppermute x3, starting transfers between devices, local(): arrived.append(lax.ppermute(packed, 'gy', ring_of_four(count_y, step)))  4.64 us
    pallas_call x14, Pallas kernels, call(): pl.pallas_call(kernel, out_shape=[jax.ShapeDtypeStruct(shape, jnp.float32...  3.86 us
    ppermute x3, waiting for transfers between devices, local(): arrived.append(lax.ppermute(packed, 'gy', ring_of_four(count_y, step)))  3.31 us
    ppermute x2, waiting for transfers between devices, local(): other = lax.ppermute(rows, 'gx', pairs_across(count_x, level))  2.83 us
    ppermute x1, waiting for transfers between devices, local(): two = lax.ppermute(two, ('gx', 'gy'), [(b, a) for a, b in round_trip])  2.28 us
    unnamed x8, local copies, waits for them, and re-layouts  2.21 us
    ppermute x1, starting transfers between devices, local(): one = lax.ppermute(one, ('gx', 'gy'), round_trip)  1.58 us
  transfers between devices with their start and end apart: 11, of which 8 were waited for; matrix products, arithmetic and copies ran while one was open for 0% of the time, Pallas kernels for 8%

profile of v5, /device:TPU:0, one launch (start us, length us, event | category | flops | bytes accessed | tf_op | source)
XLA Modules:
  0.0 29.8 jit_solution(2471426547489766756)
XLA Ops:
  0.0 0.9 %copy-done = f32[5,8,1024]{2,1,0:T(8,128)S(1)} copy-done((f32[5,8,1024]{2,1,0:T(8,128)S(1)}, f32[5,8,1024]{2,1,0:T(8,128)}, u32[]{:S(2)}) %copy-start) | copy-done | bytes 163864
  1.0 0.7 %copy-done.2 = s32[2,32]{1,0:T(2,128)S(1)} copy-done((s32[2,32]{1,0:T(2,128)S(1)}, s32[2,32]{1,0:T(2,128)}, u32[]{:S(2)}) %copy-start.2) | copy-done | bytes 280
  1.9 0.6 %collective-permute-start.3 = (f32[22,8,128]{2,1,0:T(8,128)S(1)}, f32[22,8,128]{2,1,0:T(8,128)S(1)}, u32[]{:S(2)}, u32[]{:S(2)}) collective-permute-start(f32[22,8,128]{2,1,0:T(8,128)S(1)} %get-tuple-element.53.own_factor_ref.own_ref), channel_id=1, source_target_pairs={{0,4},{4,0},{8,12},{12,8},{16,20},{20,16},{24,28},{28,24},{1,5},{5... | collective-permute-start | bytes 270344 | tf_op jit(solution)/shard_map/ppermute | solution.py:855
  2.4 0.9 %collective-permute-done.3.other_factor_ref.other_ref = f32[22,8,128]{2,1,0:T(8,128)S(1)} collective-permute-done((f32[22,8,128]{2,1,0:T(8,128)S(1)}, f32[22,8,128]{2,1,0:T(8,128)S(1)}, u32[]{:S(2)}, u32[]{:S(2)}) %collective-permute-start.3) | collective-permute-done | bytes 90144 | tf_op jit(solution)/shard_map/ppermute | solution.py:855
  3.4 2.7 %collective-permute-start.5 = (f32[22,8,128]{2,1,0:T(8,128)S(1)}, f32[22,8,128]{2,1,0:T(8,128)S(1)}, u32[]{:S(2)}, u32[]{:S(2)}) collective-permute-start(f32[22,8,128]{2,1,0:T(8,128)S(1)} %shard_map.43.own_factor_ref.own_ref), channel_id=1, source_target_pairs={{0,12},{4,8},{8,4},{12,0},{16,28},{20,24},{24,20},{28,16},{1,13},{... | collective-permute-start | bytes 270344 | tf_op jit(solution)/shard_map/ppermute | solution.py:855
  6.1 1.6 %collective-permute-start = (f32[2,8,128]{2,1,0:T(8,128)S(1)}, f32[2,8,128]{2,1,0:T(8,128)S(1)}, u32[]{:S(2)}, u32[]{:S(2)}) collective-permute-start(f32[2,8,128]{2,1,0:T(8,128)S(1)} %get-tuple-element.43), channel_id=1, source_target_pairs={{0,1},{1,2},{2,3},{3,7},{4,0},{5,4},{6,5},{7,6},{8,9},{9,10},{10,1... | collective-permute-start | bytes 24584 | tf_op jit(solution)/shard_map/ppermute | solution.py:845
  7.7 0.4 %shard_map.39 = (f32[8,5,8,128]{3,2,1,0:T(8,128)S(1)}, f32[10,8,128]{2,1,0:T(8,128)S(1)}) custom-call(f32[5,64,128]{2,1,0:T(8,128)S(1)} %get-tuple-element.39.qx_ref, f32[8,6,8,128]{3,2,1,0:T(8,128)S(1)} %get-tuple-element.41.weight_ref), custom_call_target="tpu_custom_call" | custom-call | tf_op jit(solution)/shard_map/pallas_call | solution.py:796
  8.0 1.0 %collective-permute-done.one_ref = f32[2,8,128]{2,1,0:T(8,128)S(1)} collective-permute-done((f32[2,8,128]{2,1,0:T(8,128)S(1)}, f32[2,8,128]{2,1,0:T(8,128)S(1)}, u32[]{:S(2)}, u32[]{:S(2)}) %collective-permute-start) | collective-permute-done | bytes 8224 | tf_op jit(solution)/shard_map/ppermute | solution.py:845
  9.0 2.3 %collective-permute-done.1.two_ref = f32[2,8,128]{2,1,0:T(8,128)S(1)} collective-permute-done((f32[2,8,128]{2,1,0:T(8,128)S(1)}, f32[2,8,128]{2,1,0:T(8,128)S(1)}, u32[]{:S(2)}, u32[]{:S(2)}) %collective-permute-start.1) | collective-permute-done | bytes 8224 | tf_op jit(solution)/shard_map/ppermute | solution.py:846
  11.6 1.2 %collective-permute-done.2.other_ref = f32[10,8,128]{2,1,0:T(8,128)S(1)} collective-permute-done((f32[10,8,128]{2,1,0:T(8,128)S(1)}, f32[10,8,128]{2,1,0:T(8,128)S(1)}, u32[]{:S(2)}, u32[]{:S(2)}) %collective-permute-start.2) | collective-permute-done | bytes 40992 | tf_op jit(solution)/shard_map/ppermute | solution.py:871
  12.9 0.4 %collective-permute-start.4 = (f32[10,8,128]{2,1,0:T(8,128)S(1)}, f32[10,8,128]{2,1,0:T(8,128)S(1)}, u32[]{:S(2)}, u32[]{:S(2)}) collective-permute-start(f32[10,8,128]{2,1,0:T(8,128)S(1)} %get-tuple-element.54.own_ref), channel_id=1, source_target_pairs={{0,12},{4,8},{8,4},{12,0},{16,28},{20,24},{24,20},{28,16},{1,13},{... | collective-permute-start | bytes 122888 | tf_op jit(solution)/shard_map/ppermute | solution.py:871
  13.3 1.5 %collective-permute-start.7 = (f32[8,8,128]{2,1,0:T(8,128)S(1)}, f32[8,8,128]{2,1,0:T(8,128)S(1)}, u32[]{:S(2)}, u32[]{:S(2)}) collective-permute-start(f32[8,8,128]{2,1,0:T(8,128)S(1)} %shard_map.45.own_ref), channel_id=1, source_target_pairs={{0,20},{4,16},{8,28},{12,24},{16,4},{20,0},{24,12},{28,8},{1,21},{... | collective-permute-start | bytes 98312 | tf_op jit(solution)/shard_map/ppermute | solution.py:855
  14.9 1.6 %collective-permute-done.4.other_ref = f32[10,8,128]{2,1,0:T(8,128)S(1)} collective-permute-done((f32[10,8,128]{2,1,0:T(8,128)S(1)}, f32[10,8,128]{2,1,0:T(8,128)S(1)}, u32[]{:S(2)}, u32[]{:S(2)}) %collective-permute-start.4) | collective-permute-done | bytes 40992 | tf_op jit(solution)/shard_map/ppermute | solution.py:871
  16.5 1.6 %collective-permute-start.6 = (f32[5,8,128]{2,1,0:T(8,128)S(1)}, f32[5,8,128]{2,1,0:T(8,128)S(1)}, u32[]{:S(2)}, u32[]{:S(2)}) collective-permute-start(f32[5,8,128]{2,1,0:T(8,128)S(1)} %get-tuple-element.55.refs_4_), channel_id=1, source_target_pairs={{0,20},{4,16},{8,28},{12,24},{16,4},{20,0},{24,12},{28,8},{1,21},{... | collective-permute-start | bytes 61448 | tf_op jit(solution)/shard_map/ppermute | solution.py:878
  18.2 0.6 %copy-done.3 = s32[2,8]{1,0:T(2,128)S(1)} copy-done((s32[2,8]{1,0:T(2,128)S(1)}, s32[2,8]{1,0:T(2,128)}, u32[]{:S(2)}) %copy-start.3) | copy-done | bytes 88
  18.8 0.6 %shard_map.47 = (f32[4,8,128]{2,1,0:T(8,128)S(1)}, f32[8,3,8,128]{3,2,1,0:T(8,128)S(1)}, f32[8,3,8,128]{3,2,1,0:T(8,128)S(1)}, f32[8,3,8,128]{3,2,1,0:T(8,128)S(...) custom-call(f32[5,8,1024]{2,1,0:T(8,128)S(1)} %copy-done.1, ...), custom_call_target="tpu_custom_call" | custom-call | tf_op jit(solution)/shard_map/pallas_call | solution.py:796
  19.5 0.3 %collective-permute-done.6.refs_5_ = f32[5,8,128]{2,1,0:T(8,128)S(1)} collective-permute-done((f32[5,8,128]{2,1,0:T(8,128)S(1)}, f32[5,8,128]{2,1,0:T(8,128)S(1)}, u32[]{:S(2)}, u32[]{:S(2)}) %collective-permute-start.6) | collective-permute-done | bytes 20512 | tf_op jit(solution)/shard_map/ppermute | solution.py:878
  20.1 2.1 %collective-permute-start.10 = (f32[8,8,128]{2,1,0:T(8,128)S(1)}, f32[8,8,128]{2,1,0:T(8,128)S(1)}, u32[]{:S(2)}, u32[]{:S(2)}) collective-permute-start(f32[8,8,128]{2,1,0:T(8,128)S(1)} %get-tuple-element.72.refs_5_), channel_id=1, source_target_pairs={{0,3},{1,0},{2,1},{3,2},{4,7},{5,4},{6,5},{7,6},{8,11},{9,8},{10,9... | collective-permute-start | bytes 98312 | tf_op jit(solution)/shard_map/ppermute | solution.py:902
  22.1 1.0 %collective-permute-start.9 = (f32[8,8,128]{2,1,0:T(8,128)S(1)}, f32[8,8,128]{2,1,0:T(8,128)S(1)}, u32[]{:S(2)}, u32[]{:S(2)}) collective-permute-start(f32[8,8,128]{2,1,0:T(8,128)S(1)} %get-tuple-element.72.refs_5_), channel_id=1, source_target_pairs={{0,2},{1,3},{2,0},{3,1},{4,6},{5,7},{6,4},{7,5},{8,10},{9,11},{10,... | collective-permute-start | bytes 98312 | tf_op jit(solution)/shard_map/ppermute | solution.py:902
  23.1 1.6 %collective-permute-start.8 = (f32[8,8,128]{2,1,0:T(8,128)S(1)}, f32[8,8,128]{2,1,0:T(8,128)S(1)}, u32[]{:S(2)}, u32[]{:S(2)}) collective-permute-start(f32[8,8,128]{2,1,0:T(8,128)S(1)} %get-tuple-element.72.refs_5_), channel_id=1, source_target_pairs={{0,1},{1,2},{2,3},{3,0},{4,5},{5,6},{6,7},{7,4},{8,9},{9,10},{10,1... | collective-permute-start | bytes 98312 | tf_op jit(solution)/shard_map/ppermute | solution.py:902
  24.7 0.8 %shard_map.49 = (f32[8,11,8,128]{3,2,1,0:T(8,128)S(1)}, f32[8,6,8,128]{3,2,1,0:T(8,128)S(1)}, f32[2,11,8,128]{3,2,1,0:T(8,128)S(1)}, f32[4,11,8,128]{3,2,1,0:T(8,128)S(1)}) custom-call(f32[5,8,1024]{2,1,0:T(8,128)S(1)} %copy-done.1, f32[5,64,128]{2,1,0:T(8,128)S(1)} %get-tuple-element.60.turn_ref, f32[8,3,8,128]{3,2,1,0:T(8,128)S(1)} %get-tuple-element.61.inverse_ref, ...), custom_call_target="tpu_custom_call" | custom-call | tf_op jit(solution)/shard_map/pallas_call | solution.py:796
  25.5 1.4 %collective-permute-done.9.refs_7_ = f32[8,8,128]{2,1,0:T(8,128)S(1)} collective-permute-done((f32[8,8,128]{2,1,0:T(8,128)S(1)}, f32[8,8,128]{2,1,0:T(8,128)S(1)}, u32[]{:S(2)}, u32[]{:S(2)}) %collective-permute-start.9) | collective-permute-done | bytes 32800 | tf_op jit(solution)/shard_map/ppermute | solution.py:902
  26.9 1.9 %collective-permute-done.8.refs_6_ = f32[8,8,128]{2,1,0:T(8,128)S(1)} collective-permute-done((f32[8,8,128]{2,1,0:T(8,128)S(1)}, f32[8,8,128]{2,1,0:T(8,128)S(1)}, u32[]{:S(2)}, u32[]{:S(2)}) %collective-permute-start.8) | collective-permute-done | bytes 32800 | tf_op jit(solution)/shard_map/ppermute | solution.py:902
  28.9 0.9 %shard_map.50 = f32[5,8,1024]{2,1,0:T(8,128)} custom-call(f32[5,8,1024]{2,1,0:T(8,128)S(1)} %copy-done.1, f32[8,11,8,128]{3,2,1,0:T(8,128)S(1)} %get-tuple-element.68.refs_1_, f32[8,6,8,128]{3,2,1,0:T(8,128)S(1)} %get-tuple-element.69.refs_2_, f32[2,11,8,128]{3,2,1,0:T(8,128)S(1)} %get-tuple-element.70.refs_3_, ...), custom_call_target="tpu_custom_call" | custom-call | tf_op jit(solution)/shard_map/pallas_call | solution.py:796
  (20 shorter events, 1.2 us)
Async XLA Ops:
  0.0 0.9 %copy-start = (f32[5,8,1024]{2,1,0:T(8,128)S(1)}, f32[5,8,1024]{2,1,0:T(8,128)}, u32[]{:S(2)}) copy-start(f32[5,8,1024]{2,1,0:T(8,128)} %refs_0_.1) | copy-start | bytes 491524
  1.0 0.7 %copy-start.2 = (s32[2,32]{1,0:T(2,128)S(1)}, s32[2,32]{1,0:T(2,128)}, u32[]{:S(2)}) copy-start(s32[2,32]{1,0:T(2,128)} %codes_ref.2) | copy-start | bytes 772
  1.9 1.5 %collective-permute-start.3 = (f32[22,8,128]{2,1,0:T(8,128)S(1)}, f32[22,8,128]{2,1,0:T(8,128)S(1)}, u32[]{:S(2)}, u32[]{:S(2)}) collective-permute-start(f32[22,8,128]{2,1,0:T(8,128)S(1)} %get-tuple-element.53.own_factor_ref.own_ref), channel_id=1, source_target_pairs={{0,4},{4,0},{8,12},{12,8},{16,20},{20,16},{24,28},{28,24},{1,5},{5... | collective-permute-start | bytes 270344 | tf_op jit(solution)/shard_map/ppermute | solution.py:855
  3.4 9.8 %collective-permute-start.5 = (f32[22,8,128]{2,1,0:T(8,128)S(1)}, f32[22,8,128]{2,1,0:T(8,128)S(1)}, u32[]{:S(2)}, u32[]{:S(2)}) collective-permute-start(f32[22,8,128]{2,1,0:T(8,128)S(1)} %shard_map.43.own_factor_ref.own_ref), channel_id=1, source_target_pairs={{0,12},{4,8},{8,4},{12,0},{16,28},{20,24},{24,20},{28,16},{1,13},{... | collective-permute-start | bytes 270344 | tf_op jit(solution)/shard_map/ppermute | solution.py:855
  6.1 2.9 %collective-permute-start = (f32[2,8,128]{2,1,0:T(8,128)S(1)}, f32[2,8,128]{2,1,0:T(8,128)S(1)}, u32[]{:S(2)}, u32[]{:S(2)}) collective-permute-start(f32[2,8,128]{2,1,0:T(8,128)S(1)} %get-tuple-element.43), channel_id=1, source_target_pairs={{0,1},{1,2},{2,3},{3,7},{4,0},{5,4},{6,5},{7,6},{8,9},{9,10},{10,1... | collective-permute-start | bytes 24584 | tf_op jit(solution)/shard_map/ppermute | solution.py:845
  7.7 3.7 %collective-permute-start.1 = (f32[2,8,128]{2,1,0:T(8,128)S(1)}, f32[2,8,128]{2,1,0:T(8,128)S(1)}, u32[]{:S(2)}, u32[]{:S(2)}) collective-permute-start(f32[2,8,128]{2,1,0:T(8,128)S(1)} %get-tuple-element.44), channel_id=1, source_target_pairs={{1,0},{2,1},{3,2},{7,3},{0,4},{4,5},{5,6},{6,7},{9,8},{10,9},{11,1... | collective-permute-start | bytes 24584 | tf_op jit(solution)/shard_map/ppermute | solution.py:846
  7.7 3.7 %copy-start.1 = (f32[5,8,1024]{2,1,0:T(8,128)S(1)}, f32[5,8,1024]{2,1,0:T(8,128)}, u32[]{:S(2)}) copy-start(f32[5,8,1024]{2,1,0:T(8,128)} %refs_0_.1) | copy-start | bytes 491524
  11.5 1.3 %collective-permute-start.2 = (f32[10,8,128]{2,1,0:T(8,128)S(1)}, f32[10,8,128]{2,1,0:T(8,128)S(1)}, u32[]{:S(2)}, u32[]{:S(2)}) collective-permute-start(f32[10,8,128]{2,1,0:T(8,128)S(1)} %get-tuple-element.52.own_ref), channel_id=1, source_target_pairs={{0,4},{4,0},{8,12},{12,8},{16,20},{20,16},{24,28},{28,24},{1,5},{5... | collective-permute-start | bytes 122888 | tf_op jit(solution)/shard_map/ppermute | solution.py:871
  12.9 3.6 %collective-permute-start.4 = (f32[10,8,128]{2,1,0:T(8,128)S(1)}, f32[10,8,128]{2,1,0:T(8,128)S(1)}, u32[]{:S(2)}, u32[]{:S(2)}) collective-permute-start(f32[10,8,128]{2,1,0:T(8,128)S(1)} %get-tuple-element.54.own_ref), channel_id=1, source_target_pairs={{0,12},{4,8},{8,4},{12,0},{16,28},{20,24},{24,20},{28,16},{1,13},{... | collective-permute-start | bytes 122888 | tf_op jit(solution)/shard_map/ppermute | solution.py:871
  13.3 6.1 %collective-permute-start.7 = (f32[8,8,128]{2,1,0:T(8,128)S(1)}, f32[8,8,128]{2,1,0:T(8,128)S(1)}, u32[]{:S(2)}, u32[]{:S(2)}) collective-permute-start(f32[8,8,128]{2,1,0:T(8,128)S(1)} %shard_map.45.own_ref), channel_id=1, source_target_pairs={{0,20},{4,16},{8,28},{12,24},{16,4},{20,0},{24,12},{28,8},{1,21},{... | collective-permute-start | bytes 98312 | tf_op jit(solution)/shard_map/ppermute | solution.py:855
  16.5 3.3 %collective-permute-start.6 = (f32[5,8,128]{2,1,0:T(8,128)S(1)}, f32[5,8,128]{2,1,0:T(8,128)S(1)}, u32[]{:S(2)}, u32[]{:S(2)}) collective-permute-start(f32[5,8,128]{2,1,0:T(8,128)S(1)} %get-tuple-element.55.refs_4_), channel_id=1, source_target_pairs={{0,20},{4,16},{8,28},{12,24},{16,4},{20,0},{24,12},{28,8},{1,21},{... | collective-permute-start | bytes 61448 | tf_op jit(solution)/shard_map/ppermute | solution.py:878
  18.1 0.7 %copy-start.3 = (s32[2,8]{1,0:T(2,128)S(1)}, s32[2,8]{1,0:T(2,128)}, u32[]{:S(2)}) copy-start(s32[2,8]{1,0:T(2,128)} %codes_ref.3) | copy-start | bytes 196
  20.1 5.5 %collective-permute-start.10 = (f32[8,8,128]{2,1,0:T(8,128)S(1)}, f32[8,8,128]{2,1,0:T(8,128)S(1)}, u32[]{:S(2)}, u32[]{:S(2)}) collective-permute-start(f32[8,8,128]{2,1,0:T(8,128)S(1)} %get-tuple-element.72.refs_5_), channel_id=1, source_target_pairs={{0,3},{1,0},{2,1},{3,2},{4,7},{5,4},{6,5},{7,6},{8,11},{9,8},{10,9... | collective-permute-start | bytes 98312 | tf_op jit(solution)/shard_map/ppermute | solution.py:902
  22.1 4.8 %collective-permute-start.9 = (f32[8,8,128]{2,1,0:T(8,128)S(1)}, f32[8,8,128]{2,1,0:T(8,128)S(1)}, u32[]{:S(2)}, u32[]{:S(2)}) collective-permute-start(f32[8,8,128]{2,1,0:T(8,128)S(1)} %get-tuple-element.72.refs_5_), channel_id=1, source_target_pairs={{0,2},{1,3},{2,0},{3,1},{4,6},{5,7},{6,4},{7,5},{8,10},{9,11},{10,... | collective-permute-start | bytes 98312 | tf_op jit(solution)/shard_map/ppermute | solution.py:902
  23.1 5.7 %collective-permute-start.8 = (f32[8,8,128]{2,1,0:T(8,128)S(1)}, f32[8,8,128]{2,1,0:T(8,128)S(1)}, u32[]{:S(2)}, u32[]{:S(2)}) collective-permute-start(f32[8,8,128]{2,1,0:T(8,128)S(1)} %get-tuple-element.72.refs_5_), channel_id=1, source_target_pairs={{0,1},{1,2},{2,3},{3,0},{4,5},{5,6},{6,7},{7,4},{8,9},{9,10},{10,1... | collective-permute-start | bytes 98312 | tf_op jit(solution)/shard_map/ppermute | solution.py:902

commit v6 on v5

--- a/solution.py
+++ b/solution.py
@@ -462,8 +462,9 @@
 
 
 def y_merge_kernel(level, own_ref, other_ref, out_ref, side_ref):
-    joined, side = merge(bit_low("gy", level), load(own_ref), load(other_ref), PACKED_SPEED)
-    store(out_ref, joined)
+    own, other = expand(load(own_ref)), expand(load(other_ref))
+    joined, side = merge(bit_low("gy", level), own, other, PACKED_SPEED)
+    store(out_ref, compress(joined))
     store(side_ref, side)
 
 
@@ -662,10 +663,19 @@
             ends.append(terms[0])
     ends = [v + pltpu.roll(v, LANES // 2, 1) for v in ends]
     ends = [v + pltpu.roll(v, NZ, 1) for v in ends]
-    rows = []
-    for a in (ends[:5], ends[5:]):
-        rows += [four(group, a[0], a[1], a[4], a[2]), a[3]]
+    rows = [four(group, a[0], a[1], a[4], a[2]) for a in (ends[:5], ends[5:])]
+    rows.append(jnp.where(group == GROUPS - 1, ends[8], ends[3]))
     store(out_ref, rows + load(packed_ref))
+
+
+def expand(rows):
+    return [rows[0], rows[2], rows[1], pltpu.roll(rows[2], LANES // 2, 1)] + rows[3:]
+
+
+def compress(rows):
+    group = lax.broadcasted_iota(jnp.int32, rows[0].shape, 1) // NZ
+    mixed = jnp.where(group == GROUPS - 1, pltpu.roll(rows[3], LANES // 2, 1), rows[1])
+    return [rows[0], rows[2], mixed] + rows[4:]
 
 
 def y_sweep(turn_ref, cells, group, factor_refs, join_ref):
@@ -752,7 +762,7 @@
     chunks = flow_ref.shape[2] // LANES
     group = lax.broadcasted_iota(jnp.int32, (cells, LANES), 1) // NZ
     place = (lax.axis_index("gy") >> levels) % 4
-    outer = outer_of_four(place, load(mine_ref), [load(ref) for ref in arrived], PACKED_SPEED)
+    outer = outer_of_four(place, expand(load(mine_ref)), [expand(load(ref)) for ref in arrived], PACKED_SPEED)
     for level in range(levels - 1, -1, -1):
         outer = step_down(bit_low("gy", level), load(sides[level]), outer, PACKED_SPEED)
     outer = tuple(
@@ -883,7 +893,7 @@
     packed, turn = call(
         functools.partial(y_kernel, levels_x),
         [xpoints, own, left, right, rows, other, last, y_factors, yweight] + sides,
-        [(8,) + tile_y, (5, cells * chunks, LANES)],
+        [(7,) + tile_y, (5, cells * chunks, LANES)],
     )
     prepared = call(
         prepare_kernel, [flow, turn, yinverse, ylower, yup, yjoin, yleft, yright, yside],
@@ -894,7 +904,7 @@
         other = lax.ppermute(packed, "gy", pairs_at(count_y, level))
         packed, side_rows = call(
             functools.partial(y_merge_kernel, level),
-            [packed, other], [(8,) + tile_y, (4,) + tile_y],
+            [packed, other], [(7,) + tile_y, (4,) + tile_y],
         )
         sides.append(side_rows)
     arrived = []

time: 30 us -> 29.9 us (level)
  no operation moved by 1% of the time
where the time goes in v6:
time: 29.9 us; the launch traced here: 29.8 us
  starting transfers between devices  13 us (43%)
  waiting for transfers between devices  10.6 us (35%)
  Pallas kernels  3.85 us (13%)
  local copies, waits for them, and re-layouts  2.21 us (7%)
    ppermute x3, starting transfers between devices, local(): other = lax.ppermute(factors, 'gx', pairs_across(count_x, level))  4.75 us
    ppermute x3, starting transfers between devices, local(): arrived.append(lax.ppermute(packed, 'gy', ring_of_four(count_y, step)))  4.66 us
    pallas_call x14, Pallas kernels, call(): pl.pallas_call(kernel, out_shape=[jax.ShapeDtypeStruct(shape, jnp.float32...  3.85 us
    ppermute x3, waiting for transfers between devices, local(): arrived.append(lax.ppermute(packed, 'gy', ring_of_four(count_y, step)))  3.27 us
    ppermute x2, waiting for transfers between devices, local(): other = lax.ppermute(rows, 'gx', pairs_across(count_x, level))  2.83 us
    ppermute x1, waiting for transfers between devices, local(): two = lax.ppermute(two, ('gx', 'gy'), [(b, a) for a, b in round_trip])  2.28 us
    unnamed x8, local copies, waits for them, and re-layouts  2.21 us
    ppermute x1, starting transfers between devices, local(): one = lax.ppermute(one, ('gx', 'gy'), round_trip)  1.58 us
  transfers between devices with their start and end apart: 11, of which 8 were waited for; matrix products, arithmetic and copies ran while one was open for 0% of the time, Pallas kernels for 8%

profile of v6, /device:TPU:0, one launch (start us, length us, event | category | flops | bytes accessed | tf_op | source)
XLA Modules:
  0.0 29.8 jit_solution(13587038444117217012)
XLA Ops:
  0.0 0.9 %copy-done = f32[5,8,1024]{2,1,0:T(8,128)S(1)} copy-done((f32[5,8,1024]{2,1,0:T(8,128)S(1)}, f32[5,8,1024]{2,1,0:T(8,128)}, u32[]{:S(2)}) %copy-start) | copy-done | bytes 163864
  1.0 0.7 %copy-done.2 = s32[2,32]{1,0:T(2,128)S(1)} copy-done((s32[2,32]{1,0:T(2,128)S(1)}, s32[2,32]{1,0:T(2,128)}, u32[]{:S(2)}) %copy-start.2) | copy-done | bytes 280
  1.9 0.6 %collective-permute-start.3 = (f32[22,8,128]{2,1,0:T(8,128)S(1)}, f32[22,8,128]{2,1,0:T(8,128)S(1)}, u32[]{:S(2)}, u32[]{:S(2)}) collective-permute-start(f32[22,8,128]{2,1,0:T(8,128)S(1)} %get-tuple-element.53.own_factor_ref.own_ref), channel_id=1, source_target_pairs={{0,4},{4,0},{8,12},{12,8},{16,20},{20,16},{24,28},{28,24},{1,5},{5... | collective-permute-start | bytes 270344 | tf_op jit(solution)/shard_map/ppermute | solution.py:865
  2.4 0.9 %collective-permute-done.3.other_factor_ref.other_ref = f32[22,8,128]{2,1,0:T(8,128)S(1)} collective-permute-done((f32[22,8,128]{2,1,0:T(8,128)S(1)}, f32[22,8,128]{2,1,0:T(8,128)S(1)}, u32[]{:S(2)}, u32[]{:S(2)}) %collective-permute-start.3) | collective-permute-done | bytes 90144 | tf_op jit(solution)/shard_map/ppermute | solution.py:865
  3.4 2.7 %collective-permute-start.5 = (f32[22,8,128]{2,1,0:T(8,128)S(1)}, f32[22,8,128]{2,1,0:T(8,128)S(1)}, u32[]{:S(2)}, u32[]{:S(2)}) collective-permute-start(f32[22,8,128]{2,1,0:T(8,128)S(1)} %shard_map.43.own_factor_ref.own_ref), channel_id=1, source_target_pairs={{0,12},{4,8},{8,4},{12,0},{16,28},{20,24},{24,20},{28,16},{1,13},{... | collective-permute-start | bytes 270344 | tf_op jit(solution)/shard_map/ppermute | solution.py:865
  6.1 1.6 %collective-permute-start = (f32[2,8,128]{2,1,0:T(8,128)S(1)}, f32[2,8,128]{2,1,0:T(8,128)S(1)}, u32[]{:S(2)}, u32[]{:S(2)}) collective-permute-start(f32[2,8,128]{2,1,0:T(8,128)S(1)} %get-tuple-element.43), channel_id=1, source_target_pairs={{0,1},{1,2},{2,3},{3,7},{4,0},{5,4},{6,5},{7,6},{8,9},{9,10},{10,1... | collective-permute-start | bytes 24584 | tf_op jit(solution)/shard_map/ppermute | solution.py:855
  7.7 0.4 %shard_map.39 = (f32[8,5,8,128]{3,2,1,0:T(8,128)S(1)}, f32[10,8,128]{2,1,0:T(8,128)S(1)}) custom-call(f32[5,64,128]{2,1,0:T(8,128)S(1)} %get-tuple-element.39.qx_ref, f32[8,6,8,128]{3,2,1,0:T(8,128)S(1)} %get-tuple-element.41.weight_ref), custom_call_target="tpu_custom_call" | custom-call | tf_op jit(solution)/shard_map/pallas_call | solution.py:806
  8.0 1.0 %collective-permute-done.one_ref = f32[2,8,128]{2,1,0:T(8,128)S(1)} collective-permute-done((f32[2,8,128]{2,1,0:T(8,128)S(1)}, f32[2,8,128]{2,1,0:T(8,128)S(1)}, u32[]{:S(2)}, u32[]{:S(2)}) %collective-permute-start) | collective-permute-done | bytes 8224 | tf_op jit(solution)/shard_map/ppermute | solution.py:855
  9.0 2.3 %collective-permute-done.1.two_ref = f32[2,8,128]{2,1,0:T(8,128)S(1)} collective-permute-done((f32[2,8,128]{2,1,0:T(8,128)S(1)}, f32[2,8,128]{2,1,0:T(8,128)S(1)}, u32[]{:S(2)}, u32[]{:S(2)}) %collective-permute-start.1) | collective-permute-done | bytes 8224 | tf_op jit(solution)/shard_map/ppermute | solution.py:856
  11.6 1.2 %collective-permute-done.2.other_ref = f32[10,8,128]{2,1,0:T(8,128)S(1)} collective-permute-done((f32[10,8,128]{2,1,0:T(8,128)S(1)}, f32[10,8,128]{2,1,0:T(8,128)S(1)}, u32[]{:S(2)}, u32[]{:S(2)}) %collective-permute-start.2) | collective-permute-done | bytes 40992 | tf_op jit(solution)/shard_map/ppermute | solution.py:881
  12.9 0.4 %collective-permute-start.4 = (f32[10,8,128]{2,1,0:T(8,128)S(1)}, f32[10,8,128]{2,1,0:T(8,128)S(1)}, u32[]{:S(2)}, u32[]{:S(2)}) collective-permute-start(f32[10,8,128]{2,1,0:T(8,128)S(1)} %get-tuple-element.54.own_ref), channel_id=1, source_target_pairs={{0,12},{4,8},{8,4},{12,0},{16,28},{20,24},{24,20},{28,16},{1,13},{... | collective-permute-start | bytes 122888 | tf_op jit(solution)/shard_map/ppermute | solution.py:881
  13.3 1.5 %collective-permute-start.7 = (f32[8,8,128]{2,1,0:T(8,128)S(1)}, f32[8,8,128]{2,1,0:T(8,128)S(1)}, u32[]{:S(2)}, u32[]{:S(2)}) collective-permute-start(f32[8,8,128]{2,1,0:T(8,128)S(1)} %shard_map.45.own_ref), channel_id=1, source_target_pairs={{0,20},{4,16},{8,28},{12,24},{16,4},{20,0},{24,12},{28,8},{1,21},{... | collective-permute-start | bytes 98312 | tf_op jit(solution)/shard_map/ppermute | solution.py:865
  14.9 1.6 %collective-permute-done.4.other_ref = f32[10,8,128]{2,1,0:T(8,128)S(1)} collective-permute-done((f32[10,8,128]{2,1,0:T(8,128)S(1)}, f32[10,8,128]{2,1,0:T(8,128)S(1)}, u32[]{:S(2)}, u32[]{:S(2)}) %collective-permute-start.4) | collective-permute-done | bytes 40992 | tf_op jit(solution)/shard_map/ppermute | solution.py:881
  16.5 1.6 %collective-permute-start.6 = (f32[5,8,128]{2,1,0:T(8,128)S(1)}, f32[5,8,128]{2,1,0:T(8,128)S(1)}, u32[]{:S(2)}, u32[]{:S(2)}) collective-permute-start(f32[5,8,128]{2,1,0:T(8,128)S(1)} %get-tuple-element.55.refs_4_), channel_id=1, source_target_pairs={{0,20},{4,16},{8,28},{12,24},{16,4},{20,0},{24,12},{28,8},{1,21},{... | collective-permute-start | bytes 61448 | tf_op jit(solution)/shard_map/ppermute | solution.py:888
  18.2 0.6 %copy-done.3 = s32[2,8]{1,0:T(2,128)S(1)} copy-done((s32[2,8]{1,0:T(2,128)S(1)}, s32[2,8]{1,0:T(2,128)}, u32[]{:S(2)}) %copy-start.3) | copy-done | bytes 88
  18.8 0.6 %shard_map.47 = (f32[4,8,128]{2,1,0:T(8,128)S(1)}, f32[8,3,8,128]{3,2,1,0:T(8,128)S(1)}, f32[8,3,8,128]{3,2,1,0:T(8,128)S(1)}, f32[8,3,8,128]{3,2,1,0:T(8,128)S(...) custom-call(f32[5,8,1024]{2,1,0:T(8,128)S(1)} %copy-done.1, ...), custom_call_target="tpu_custom_call" | custom-call | tf_op jit(solution)/shard_map/pallas_call | solution.py:806
  19.5 0.3 %collective-permute-done.6.refs_5_ = f32[5,8,128]{2,1,0:T(8,128)S(1)} collective-permute-done((f32[5,8,128]{2,1,0:T(8,128)S(1)}, f32[5,8,128]{2,1,0:T(8,128)S(1)}, u32[]{:S(2)}, u32[]{:S(2)}) %collective-permute-start.6) | collective-permute-done | bytes 20512 | tf_op jit(solution)/shard_map/ppermute | solution.py:888
  20.1 2.1 %collective-permute-start.10 = (f32[7,8,128]{2,1,0:T(8,128)S(1)}, f32[7,8,128]{2,1,0:T(8,128)S(1)}, u32[]{:S(2)}, u32[]{:S(2)}) collective-permute-start(f32[7,8,128]{2,1,0:T(8,128)S(1)} %get-tuple-element.72.refs_5_), channel_id=1, source_target_pairs={{0,3},{1,0},{2,1},{3,2},{4,7},{5,4},{6,5},{7,6},{8,11},{9,8},{10,9... | collective-permute-start | bytes 86024 | tf_op jit(solution)/shard_map/ppermute | solution.py:912
  22.1 1.0 %collective-permute-start.9 = (f32[7,8,128]{2,1,0:T(8,128)S(1)}, f32[7,8,128]{2,1,0:T(8,128)S(1)}, u32[]{:S(2)}, u32[]{:S(2)}) collective-permute-start(f32[7,8,128]{2,1,0:T(8,128)S(1)} %get-tuple-element.72.refs_5_), channel_id=1, source_target_pairs={{0,2},{1,3},{2,0},{3,1},{4,6},{5,7},{6,4},{7,5},{8,10},{9,11},{10,... | collective-permute-start | bytes 86024 | tf_op jit(solution)/shard_map/ppermute | solution.py:912
  23.1 1.6 %collective-permute-start.8 = (f32[7,8,128]{2,1,0:T(8,128)S(1)}, f32[7,8,128]{2,1,0:T(8,128)S(1)}, u32[]{:S(2)}, u32[]{:S(2)}) collective-permute-start(f32[7,8,128]{2,1,0:T(8,128)S(1)} %get-tuple-element.72.refs_5_), channel_id=1, source_target_pairs={{0,1},{1,2},{2,3},{3,0},{4,5},{5,6},{6,7},{7,4},{8,9},{9,10},{10,1... | collective-permute-start | bytes 86024 | tf_op jit(solution)/shard_map/ppermute | solution.py:912
  24.7 0.8 %shard_map.49 = (f32[8,11,8,128]{3,2,1,0:T(8,128)S(1)}, f32[8,6,8,128]{3,2,1,0:T(8,128)S(1)}, f32[2,11,8,128]{3,2,1,0:T(8,128)S(1)}, f32[4,11,8,128]{3,2,1,0:T(8,128)S(1)}) custom-call(f32[5,8,1024]{2,1,0:T(8,128)S(1)} %copy-done.1, f32[5,64,128]{2,1,0:T(8,128)S(1)} %get-tuple-element.60.turn_ref, f32[8,3,8,128]{3,2,1,0:T(8,128)S(1)} %get-tuple-element.61.inverse_ref, ...), custom_call_target="tpu_custom_call" | custom-call | tf_op jit(solution)/shard_map/pallas_call | solution.py:806
  25.5 1.4 %collective-permute-done.9.refs_7_ = f32[7,8,128]{2,1,0:T(8,128)S(1)} collective-permute-done((f32[7,8,128]{2,1,0:T(8,128)S(1)}, f32[7,8,128]{2,1,0:T(8,128)S(1)}, u32[]{:S(2)}, u32[]{:S(2)}) %collective-permute-start.9) | collective-permute-done | bytes 28704 | tf_op jit(solution)/shard_map/ppermute | solution.py:912
  26.9 1.9 %collective-permute-done.8.refs_6_ = f32[7,8,128]{2,1,0:T(8,128)S(1)} collective-permute-done((f32[7,8,128]{2,1,0:T(8,128)S(1)}, f32[7,8,128]{2,1,0:T(8,128)S(1)}, u32[]{:S(2)}, u32[]{:S(2)}) %collective-permute-start.8) | collective-permute-done | bytes 28704 | tf_op jit(solution)/shard_map/ppermute | solution.py:912
  28.8 0.9 %shard_map.50 = f32[5,8,1024]{2,1,0:T(8,128)} custom-call(f32[5,8,1024]{2,1,0:T(8,128)S(1)} %copy-done.1, f32[8,11,8,128]{3,2,1,0:T(8,128)S(1)} %get-tuple-element.68.refs_1_, f32[8,6,8,128]{3,2,1,0:T(8,128)S(1)} %get-tuple-element.69.refs_2_, f32[2,11,8,128]{3,2,1,0:T(8,128)S(1)} %get-tuple-element.70.refs_3_, ...), custom_call_target="tpu_custom_call" | custom-call | tf_op jit(solution)/shard_map/pallas_call | solution.py:806
  (20 shorter events, 1.2 us)
Async XLA Ops:
  0.0 0.9 %copy-start = (f32[5,8,1024]{2,1,0:T(8,128)S(1)}, f32[5,8,1024]{2,1,0:T(8,128)}, u32[]{:S(2)}) copy-start(f32[5,8,1024]{2,1,0:T(8,128)} %refs_0_.1) | copy-start | bytes 491524
  1.0 0.7 %copy-start.2 = (s32[2,32]{1,0:T(2,128)S(1)}, s32[2,32]{1,0:T(2,128)}, u32[]{:S(2)}) copy-start(s32[2,32]{1,0:T(2,128)} %codes_ref.2) | copy-start | bytes 772
  1.9 1.5 %collective-permute-start.3 = (f32[22,8,128]{2,1,0:T(8,128)S(1)}, f32[22,8,128]{2,1,0:T(8,128)S(1)}, u32[]{:S(2)}, u32[]{:S(2)}) collective-permute-start(f32[22,8,128]{2,1,0:T(8,128)S(1)} %get-tuple-element.53.own_factor_ref.own_ref), channel_id=1, source_target_pairs={{0,4},{4,0},{8,12},{12,8},{16,20},{20,16},{24,28},{28,24},{1,5},{5... | collective-permute-start | bytes 270344 | tf_op jit(solution)/shard_map/ppermute | solution.py:865
  3.4 9.8 %collective-permute-start.5 = (f32[22,8,128]{2,1,0:T(8,128)S(1)}, f32[22,8,128]{2,1,0:T(8,128)S(1)}, u32[]{:S(2)}, u32[]{:S(2)}) collective-permute-start(f32[22,8,128]{2,1,0:T(8,128)S(1)} %shard_map.43.own_factor_ref.own_ref), channel_id=1, source_target_pairs={{0,12},{4,8},{8,4},{12,0},{16,28},{20,24},{24,20},{28,16},{1,13},{... | collective-permute-start | bytes 270344 | tf_op jit(solution)/shard_map/ppermute | solution.py:865
  6.1 2.9 %collective-permute-start = (f32[2,8,128]{2,1,0:T(8,128)S(1)}, f32[2,8,128]{2,1,0:T(8,128)S(1)}, u32[]{:S(2)}, u32[]{:S(2)}) collective-permute-start(f32[2,8,128]{2,1,0:T(8,128)S(1)} %get-tuple-element.43), channel_id=1, source_target_pairs={{0,1},{1,2},{2,3},{3,7},{4,0},{5,4},{6,5},{7,6},{8,9},{9,10},{10,1... | collective-permute-start | bytes 24584 | tf_op jit(solution)/shard_map/ppermute | solution.py:855
  7.7 3.7 %collective-permute-start.1 = (f32[2,8,128]{2,1,0:T(8,128)S(1)}, f32[2,8,128]{2,1,0:T(8,128)S(1)}, u32[]{:S(2)}, u32[]{:S(2)}) collective-permute-start(f32[2,8,128]{2,1,0:T(8,128)S(1)} %get-tuple-element.44), channel_id=1, source_target_pairs={{1,0},{2,1},{3,2},{7,3},{0,4},{4,5},{5,6},{6,7},{9,8},{10,9},{11,1... | collective-permute-start | bytes 24584 | tf_op jit(solution)/shard_map/ppermute | solution.py:856
  7.7 3.7 %copy-start.1 = (f32[5,8,1024]{2,1,0:T(8,128)S(1)}, f32[5,8,1024]{2,1,0:T(8,128)}, u32[]{:S(2)}) copy-start(f32[5,8,1024]{2,1,0:T(8,128)} %refs_0_.1) | copy-start | bytes 491524
  11.5 1.3 %collective-permute-start.2 = (f32[10,8,128]{2,1,0:T(8,128)S(1)}, f32[10,8,128]{2,1,0:T(8,128)S(1)}, u32[]{:S(2)}, u32[]{:S(2)}) collective-permute-start(f32[10,8,128]{2,1,0:T(8,128)S(1)} %get-tuple-element.52.own_ref), channel_id=1, source_target_pairs={{0,4},{4,0},{8,12},{12,8},{16,20},{20,16},{24,28},{28,24},{1,5},{5... | collective-permute-start | bytes 122888 | tf_op jit(solution)/shard_map/ppermute | solution.py:881
  12.9 3.6 %collective-permute-start.4 = (f32[10,8,128]{2,1,0:T(8,128)S(1)}, f32[10,8,128]{2,1,0:T(8,128)S(1)}, u32[]{:S(2)}, u32[]{:S(2)}) collective-permute-start(f32[10,8,128]{2,1,0:T(8,128)S(1)} %get-tuple-element.54.own_ref), channel_id=1, source_target_pairs={{0,12},{4,8},{8,4},{12,0},{16,28},{20,24},{24,20},{28,16},{1,13},{... | collective-permute-start | bytes 122888 | tf_op jit(solution)/shard_map/ppermute | solution.py:881
  13.3 6.1 %collective-permute-start.7 = (f32[8,8,128]{2,1,0:T(8,128)S(1)}, f32[8,8,128]{2,1,0:T(8,128)S(1)}, u32[]{:S(2)}, u32[]{:S(2)}) collective-permute-start(f32[8,8,128]{2,1,0:T(8,128)S(1)} %shard_map.45.own_ref), channel_id=1, source_target_pairs={{0,20},{4,16},{8,28},{12,24},{16,4},{20,0},{24,12},{28,8},{1,21},{... | collective-permute-start | bytes 98312 | tf_op jit(solution)/shard_map/ppermute | solution.py:865
  16.5 3.3 %collective-permute-start.6 = (f32[5,8,128]{2,1,0:T(8,128)S(1)}, f32[5,8,128]{2,1,0:T(8,128)S(1)}, u32[]{:S(2)}, u32[]{:S(2)}) collective-permute-start(f32[5,8,128]{2,1,0:T(8,128)S(1)} %get-tuple-element.55.refs_4_), channel_id=1, source_target_pairs={{0,20},{4,16},{8,28},{12,24},{16,4},{20,0},{24,12},{28,8},{1,21},{... | collective-permute-start | bytes 61448 | tf_op jit(solution)/shard_map/ppermute | solution.py:888
  18.1 0.7 %copy-start.3 = (s32[2,8]{1,0:T(2,128)S(1)}, s32[2,8]{1,0:T(2,128)}, u32[]{:S(2)}) copy-start(s32[2,8]{1,0:T(2,128)} %codes_ref.3) | copy-start | bytes 196
  20.1 5.5 %collective-permute-start.10 = (f32[7,8,128]{2,1,0:T(8,128)S(1)}, f32[7,8,128]{2,1,0:T(8,128)S(1)}, u32[]{:S(2)}, u32[]{:S(2)}) collective-permute-start(f32[7,8,128]{2,1,0:T(8,128)S(1)} %get-tuple-element.72.refs_5_), channel_id=1, source_target_pairs={{0,3},{1,0},{2,1},{3,2},{4,7},{5,4},{6,5},{7,6},{8,11},{9,8},{10,9... | collective-permute-start | bytes 86024 | tf_op jit(solution)/shard_map/ppermute | solution.py:912
  22.1 4.8 %collective-permute-start.9 = (f32[7,8,128]{2,1,0:T(8,128)S(1)}, f32[7,8,128]{2,1,0:T(8,128)S(1)}, u32[]{:S(2)}, u32[]{:S(2)}) collective-permute-start(f32[7,8,128]{2,1,0:T(8,128)S(1)} %get-tuple-element.72.refs_5_), channel_id=1, source_target_pairs={{0,2},{1,3},{2,0},{3,1},{4,6},{5,7},{6,4},{7,5},{8,10},{9,11},{10,... | collective-permute-start | bytes 86024 | tf_op jit(solution)/shard_map/ppermute | solution.py:912
  23.1 5.7 %collective-permute-start.8 = (f32[7,8,128]{2,1,0:T(8,128)S(1)}, f32[7,8,128]{2,1,0:T(8,128)S(1)}, u32[]{:S(2)}, u32[]{:S(2)}) collective-permute-start(f32[7,8,128]{2,1,0:T(8,128)S(1)} %get-tuple-element.72.refs_5_), channel_id=1, source_target_pairs={{0,1},{1,2},{2,3},{3,0},{4,5},{5,6},{6,7},{7,4},{8,9},{9,10},{10,1... | collective-permute-start | bytes 86024 | tf_op jit(solution)/shard_map/ppermute | solution.py:912
